TPU v7x, 32 devices: a whole 2x2x4 slice. The times are simulated.
32 devices in a mesh: tiles: 2 (over y), depth: 4 (over z), rows: 4 (over x, core).
Axes of the slice: x: 2, y: 2, z: 4, core: 2. Of those that a mesh axis runs over, the one named last changes fastest.
Arguments:
- volume: bfloat16 [32, 32, 32, 128], P(('tiles', 'depth'), 'rows'), parts along dimension 0, may hold values from -6 to 6
- prior: float32 [32, 32, 128], P(('tiles', 'depth'), 'rows'), parts along dimension 0, as said below
- first_kernel: bfloat16 [3, 3, 3, 32, 32], replicated, may hold values from -0.21875 to 0.21875
- second_kernel: bfloat16 [3, 3, 3, 32, 32], replicated, may hold values from -0.21875 to 0.21875
- projection: float32 [32], replicated, may hold values from -2 to 2
Outputs:
- joined: float32 [64, 32, 128], P(('tiles', 'rows')), parts along dimension 0
- depth_estimate: float32 [64, 128], P(('tiles', 'rows')), parts along dimension 0
There are 2 independent parts, one for each index of `tiles`. A program takes and returns all parts, laid end to end along the dimension named above; an argument that names none is the same for every part. Nothing has to cross between parts.
Inputs may be any that keep to these rules, and one draw needn't show every extreme that they name: `prior`: finite real values.
All inputs are finite; a program needn't handle non-finite values.
Results may differ from a plain program's by a relative error of at most 0.0045.
Values may be sent and summed in bfloat16 or wider, within the bound.
No kernel may reach another device: no remote copies, remote signals or barrier semaphores. Data moves between devices by JAX's collectives and lax.ppermute only.
A program may use at most 64 MiB of HBM per device.

v0:
```python
import jax
import jax.numpy as jnp
from jax import lax
from jax.sharding import PartitionSpec as P


def padded_2(cells, sides, width):
    for axis, dim in sides:
        count = lax.axis_size(axis)
        ends = count - 1
        head = lax.slice_in_dim(cells, 0, width, axis=dim)
        tail = lax.slice_in_dim(cells, cells.shape[dim] - width, cells.shape[dim], axis=dim)
        cells = jnp.concatenate(
            [
                lax.ppermute(tail, axis, [(i, (i + 1) % count) for i in range(ends)]),
                cells,
                lax.ppermute(head, axis, [((i + 1) % count, i) for i in range(ends)]),
            ],
            axis=dim,
        )
    return cells


def convolve(padded, kernel):
    return lax.conv_general_dilated(
        padded[None],
        kernel,
        (1, 1, 1),
        ((0, 0), (0, 0), (1, 1)),
        dimension_numbers=("NDHCW", "DHWIO", "NDHCW"),
        preferred_element_type=jnp.float32,
    )[0]


def borders(field):
    return padded_2(field, (("depth", 0), ("rows", 1)), 1)


def per_device(volume, prior, first_kernel, second_kernel, projection):
    planes_dev = volume.shape[0]
    all_planes = planes_dev * lax.axis_size("depth")
    first = jnp.maximum(convolve(borders(volume), first_kernel), 0.0).astype(jnp.bfloat16)
    first = borders(first)
    second = jnp.maximum(convolve(first, second_kernel), 0.0).astype(jnp.bfloat16)
    features = second.astype(jnp.float32)
    score = jnp.sum(features * projection[None, None, :, None], axis=2) + prior
    plane_frac = (
        (lax.axis_index("depth") * planes_dev + jnp.arange(planes_dev)).astype(jnp.float32) + 0.5
    ) / all_planes
    local_peak = jnp.max(score, axis=0)
    peak = lax.pmax(local_peak, "depth")
    expd = jnp.exp(score - peak[None])
    local_sum = jnp.sum(expd, axis=0)
    local_feat = jnp.einsum("dhw,dhcw->hcw", expd, features)
    local_depth = jnp.sum(expd * plane_frac[:, None, None], axis=0)
    total, feat_total, depth_total = lax.psum((local_sum, local_feat, local_depth), "depth")
    joined = feat_total / total[:, None, :]
    depth_estimate = depth_total / total
    return (joined, depth_estimate)


def solution(mesh):
    placed = (
        P(("tiles", "depth"), "rows", None, None),
        P(("tiles", "depth"), "rows", None),
        P(),
        P(),
        P(),
    )
    return jax.shard_map(
        per_device,
        mesh=mesh,
        in_specs=placed,
        out_specs=(P(("tiles", "rows"), None, None), P(("tiles", "rows"), None)),
        check_vma=False,
    )
```

profile of v0, /device:TPU:0, one launch (start us, length us, event | category | flops | bytes accessed | tf_op | source)
XLA Modules:
  0.0 137.2 jit_solution(4873633169051905231)
XLA Ops:
  7.2 0.0 copy-start
  7.2 0.0 all-reduce.3.cloned.1.call-start
  7.2 0.9 fusion.33
  8.2 5.0 %collective-permute-start = (bf16[1,8,32,128]{3,2,1,0:T(8,128)(2,1)S(1)}, bf16[1,8,32,128]{3,2,1,0:T(8,128)(2,1)S(1)}, u32[]{:S(2)}, u32[]{:S(2)}) collective-permute-start(bf16[1,8,32,128]{3,2,1,0:T(8,128)(2,1)S(1)} %get-tuple-element.18), channel_id=1, source_target_pairs={{0,4},{4,8},{8,12},{1,5},{5,9},{9,13},{2,6},{6,10},{10,14},{3,7},{... | collective-permute-start | bytes 196616 | tf_op jit(solution)/shard_map/ppermute | solution.py:15
  13.1 1.3 collective-permute-start.1
  14.4 0.6 collective-permute-done
  15.0 1.0 constant_dynamic-update-slice_fusion.1
  16.0 3.3 %collective-permute-done.1 = bf16[1,8,32,128]{3,2,1,0:T(8,128)(2,1)S(1)} collective-permute-done((bf16[1,8,32,128]{3,2,1,0:T(8,128)(2,1)S(1)}, bf16[1,8,32,128]{3,2,1,0:T(8,128)(2,1)S(1)}, u32[]{:S(2)}, u32[]{:S(2)}) %collective-permute-start.1) | collective-permute-done | bytes 65568 | tf_op jit(solution)/shard_map/ppermute | solution.py:17
  19.3 1.3 collective-permute-start.2
  20.6 1.3 collective-permute-start.3
  21.9 3.5 %collective-permute-done.3 = bf16[6,1,32,128]{3,2,1,0:T(8,128)(2,1)S(1)} collective-permute-done((bf16[6,1,32,128]{3,2,1,0:T(8,128)(2,1)S(1)}, bf16[6,1,32,128]{3,2,1,0:T(8,128)(2,1)S(1)}, u32[]{:S(2)}, u32[]{:S(2)}) %collective-permute-start.3) | collective-permute-done | bytes 49184 | tf_op jit(solution)/shard_map/ppermute | solution.py:17
  25.5 0.1 maximum_bitcast_fusion
  25.5 0.4 pad
  25.9 4.1 %reshape.24 = bf16[6,10,32,1,8,17]{5,4,2,1,0,3:T(8,128)(2,1)} reshape(bf16[6,10,32,1,136]{4,2,1,0,3:T(8,128)(2,1)S(1)} %pad) | data formatting | bytes 1044480 | tf_op jit(solution)/shard_map/conv_general_dilated | solution.py:25
  30.0 5.1 %copy.30 = bf16[6,10,32,1,8,17]{2,4,5,1,0,3:T(8,128)(2,1)S(1)} copy(bf16[6,10,32,1,8,17]{5,4,2,1,0,3:T(8,128)(2,1)} %reshape.24) | data formatting | bytes 1044480 | tf_op jit(solution)/shard_map/conv_general_dilated | solution.py:25
  35.1 0.1 slice.50
  35.2 4.2 %maximum_convert_fusion.1 = bf16[4,8,8,17,32]{4,2,3,1,0:T(8,128)(2,1)S(1)} fusion(bf16[3,3,3,32,32]{4,3,2,1,0:T(8,128)(2,1)S(1)} %copy-done, bf16[6,10,32,1,7,2]{2,4,5,1,0,3:T(8,128)(2,1)S(1)} %slice.50, bf16[6,10,32,1,8,17]{2,4,5,1,0,3:T(8,128)(2,1)S(1)} %copy.30, pred[8,17]{0,1:T(8,128)(4,1)S(1)} %copy-done.4), kind=kOutput, calls=%fused_computation.16 | convolution fusion | flops 242817024 | bytes 909960 | tf_op jit(solution)/shard_map/conv_general_dilated | solution.py:25
  39.5 0.1 copy.32
  39.7 3.5 %collective-permute-start.4 = (bf16[1,8,32,128]{2,1,3,0:T(8,128)(2,1)S(1)}, bf16[1,8,32,128]{2,1,3,0:T(8,128)(2,1)S(1)}, u32[]{:S(2)}, u32[]{:S(2)}) collective-permute-start(bf16[1,8,32,128]{2,1,3,0:T(8,128)(2,1)S(1)} %slice_bitcast_fusion.2), channel_id=1, source_target_pairs={{0,4},{4,8},{8,12},{1,5},{5,9},{9,13},{2,6},{6,10},{10,14},{3,7},{... | collective-permute-start | bytes 196616 | tf_op jit(solution)/shard_map/ppermute | solution.py:15
  43.3 1.3 collective-permute-start.5
  44.6 0.1 slice_bitcast_fusion
  44.7 0.6 copy.35
  45.3 2.8 %collective-permute-done.4 = bf16[1,8,32,128]{2,1,3,0:T(8,128)(2,1)S(1)} collective-permute-done((bf16[1,8,32,128]{2,1,3,0:T(8,128)(2,1)S(1)}, bf16[1,8,32,128]{2,1,3,0:T(8,128)(2,1)S(1)}, u32[]{:S(2)}, u32[]{:S(2)}) %collective-permute-start.4) | collective-permute-done | bytes 65568 | tf_op jit(solution)/shard_map/ppermute | solution.py:15
  48.1 0.2 copy.34
  48.3 4.6 %collective-permute-done.5 = bf16[1,8,32,128]{2,1,3,0:T(8,128)(2,1)S(1)} collective-permute-done((bf16[1,8,32,128]{2,1,3,0:T(8,128)(2,1)S(1)}, bf16[1,8,32,128]{2,1,3,0:T(8,128)(2,1)S(1)}, u32[]{:S(2)}, u32[]{:S(2)}) %collective-permute-start.5) | collective-permute-done | bytes 65568 | tf_op jit(solution)/shard_map/ppermute | solution.py:17
  52.9 0.2 copy.36
  53.1 3.3 %collective-permute-start.6 = (bf16[6,1,32,128]{3,2,1,0:T(8,128)(2,1)S(1)}, bf16[6,1,32,128]{3,2,1,0:T(8,128)(2,1)S(1)}, u32[]{:S(2)}, u32[]{:S(2)}) collective-permute-start(bf16[6,1,32,128]{3,2,1,0:T(8,128)(2,1)S(1)} %get-tuple-element.12), channel_id=1, source_target_pairs={{0,1},{1,2},{2,3},{4,5},{5,6},{6,7},{8,9},{9,10},{10,11},{12,13},{... | collective-permute-start | bytes 147464 | tf_op jit(solution)/shard_map/ppermute | solution.py:15
  56.3 1.5 %collective-permute-start.7 = (bf16[6,1,32,128]{3,2,1,0:T(8,128)(2,1)S(1)}, bf16[6,1,32,128]{3,2,1,0:T(8,128)(2,1)S(1)}, u32[]{:S(2)}, u32[]{:S(2)}) collective-permute-start(bf16[6,1,32,128]{3,2,1,0:T(8,128)(2,1)S(1)} %get-tuple-element.13), channel_id=1, source_target_pairs={{1,0},{2,1},{3,2},{5,4},{6,5},{7,6},{9,8},{10,9},{11,10},{13,12},{... | collective-permute-start | bytes 147464 | tf_op jit(solution)/shard_map/ppermute | solution.py:17
  57.8 0.1 copy.40
  58.0 1.5 %collective-permute-done.7 = bf16[6,1,32,128]{3,2,1,0:T(8,128)(2,1)S(1)} collective-permute-done((bf16[6,1,32,128]{3,2,1,0:T(8,128)(2,1)S(1)}, bf16[6,1,32,128]{3,2,1,0:T(8,128)(2,1)S(1)}, u32[]{:S(2)}, u32[]{:S(2)}) %collective-permute-start.7) | collective-permute-done | bytes 49184 | tf_op jit(solution)/shard_map/ppermute | solution.py:17
  59.5 0.1 maximum_bitcast_fusion.1
  59.5 0.4 pad.2
  59.9 4.1 %reshape.35 = bf16[6,10,32,1,8,17]{5,4,2,1,0,3:T(8,128)(2,1)} reshape(bf16[6,10,32,1,136]{4,2,1,0,3:T(8,128)(2,1)S(1)} %pad.2) | data formatting | bytes 1044480 | tf_op jit(solution)/shard_map/conv_general_dilated | solution.py:25
  64.1 5.1 %copy.38 = bf16[6,10,32,1,8,17]{2,4,5,1,0,3:T(8,128)(2,1)S(1)} copy(bf16[6,10,32,1,8,17]{5,4,2,1,0,3:T(8,128)(2,1)} %reshape.35) | data formatting | bytes 1044480 | tf_op jit(solution)/shard_map/conv_general_dilated | solution.py:25
  69.2 0.1 slice.56
  69.2 4.2 %maximum_convert_fusion = bf16[4,8,8,17,32]{4,2,3,1,0:T(8,128)(2,1)S(1)} fusion(bf16[3,3,3,32,32]{4,3,2,1,0:T(8,128)(2,1)S(1)} %copy-done.3, bf16[6,10,32,1,7,2]{2,4,5,1,0,3:T(8,128)(2,1)S(1)} %slice.56, bf16[6,10,32,1,8,17]{2,4,5,1,0,3:T(8,128)(2,1)S(1)} %copy.38, pred[8,17]{0,1:T(8,128)(4,1)S(1)} %copy-done.4), kind=kOutput, calls=%fused_computation.15 | convolution fusion | flops 242817024 | bytes 909960 | tf_op jit(solution)/shard_map/conv_general_dilated | solution.py:25
  73.5 0.1 copy.39
  73.7 0.5 copy-done.2
  74.1 0.6 multiply_reduce_fusion.1
  74.8 17.9 %pmax.7 = f32[8,128]{0,1:T(8,128)S(1)} all-reduce(f32[8,128]{0,1:T(8,128)S(1)} %get-tuple-element.8), channel_id=1, replica_groups=mesh['tiles'=2,'depth'=4,'rows'=4] {'depth'}, use_global_device_ids=true, to_apply=%region_2.0 | all-reduce | flops 1024 | bytes 8192 | tf_op jit(solution)/shard_map/pmax | solution.py:51
  92.7 0.1 multiply_reduce_fusion.2
  92.8 0.7 multiply_reduce_fusion
  93.6 0.9 copy.49
  94.4 0.0 all-reduce.3.cloned.1.call-update
  94.5 18.5 %all-reduce = (f32[8,128]{0,1:T(8,128)S(1)}, f32[8,128]{0,1:T(8,128)S(1)}) all-reduce(f32[8,128]{0,1:T(8,128)S(1)} %get-tuple-element.5, f32[8,128]{0,1:T(8,128)S(1)} %get-tuple-element.4), channel_id=1, replica_groups=mesh['tiles'=2,'depth'=4,'rows'=4] {'depth'}, use_global_device_ids=true, to_apply=%region_5.0 | all-reduce | flops 2048 | bytes 16384 | tf_op jit(solution)/shard_map/psum | solution.py:56
  113.0 0.7 copy.42
  113.7 15.1 %all-reduce.3.cloned.1.call-done = f32[8,32,128]{2,1,0:T(8,128)} async-done(((f32[8,32,128]{2,1,0:T(8,128)}), f32[8,32,128]{2,1,0:T(8,128)}) %all-reduce.3.cloned.1.call-update) | async-done | bytes 131088 | tf_op jit(solution)/shard_map/psum | solution.py:56
  128.8 1.6 %broadcast_divide_fusion = f32[8,32,128]{2,1,0:T(8,128)} fusion(f32[8,32,128]{2,1,0:T(8,128)} %all-reduce.3.cloned.1.call-done, f32[8,128]{1,0:T(8,128)S(1)} %copy.41), kind=kLoop, calls=%fused_computation.30 | loop fusion | flops 32768 | bytes 266240 | tf_op jit(solution)/shard_map/div | solution.py:57
  (23 shorter events, 0.4 us)
Async XLA Ops:
  7.2 28.0 %copy-start = (bf16[3,3,3,32,32]{4,3,2,1,0:T(8,128)(2,1)S(1)}, bf16[3,3,3,32,32]{4,3,2,1,0:T(8,128)(2,1)}, u32[]{:S(2)}) copy-start(bf16[3,3,3,32,32]{4,3,2,1,0:T(8,128)(2,1)} %param.7) | copy-start | bytes 165892
  7.2 121.6 %all-reduce.3.cloned.1.call-start = ((), (), s32[]{:S(2)}) async-start(), calls=%async_computation | async-start | bytes 262144 | tf_op jit(solution)/shard_map/psum | solution.py:56
  8.2 6.9 %collective-permute-start = (bf16[1,8,32,128]{3,2,1,0:T(8,128)(2,1)S(1)}, bf16[1,8,32,128]{3,2,1,0:T(8,128)(2,1)S(1)}, u32[]{:S(2)}, u32[]{:S(2)}) collective-permute-start(bf16[1,8,32,128]{3,2,1,0:T(8,128)(2,1)S(1)} %get-tuple-element.18), channel_id=1, source_target_pairs={{0,4},{4,8},{8,12},{1,5},{5,9},{9,13},{2,6},{6,10},{10,14},{3,7},{... | collective-permute-start | bytes 196616 | tf_op jit(solution)/shard_map/ppermute | solution.py:15
  13.1 6.2 %collective-permute-start.1 = (bf16[1,8,32,128]{3,2,1,0:T(8,128)(2,1)S(1)}, bf16[1,8,32,128]{3,2,1,0:T(8,128)(2,1)S(1)}, u32[]{:S(2)}, u32[]{:S(2)}) collective-permute-start(bf16[1,8,32,128]{3,2,1,0:T(8,128)(2,1)S(1)} %get-tuple-element.17), channel_id=1, source_target_pairs={{4,0},{8,4},{12,8},{5,1},{9,5},{13,9},{6,2},{10,6},{14,10},{7,3},{... | collective-permute-start | bytes 196616 | tf_op jit(solution)/shard_map/ppermute | solution.py:17
  19.3 2.6 %collective-permute-start.2 = (bf16[6,1,32,128]{3,2,1,0:T(8,128)(2,1)S(1)}, bf16[6,1,32,128]{3,2,1,0:T(8,128)(2,1)S(1)}, u32[]{:S(2)}, u32[]{:S(2)}) collective-permute-start(bf16[6,1,32,128]{3,2,1,0:T(8,128)(2,1)S(1)} %get-tuple-element.14), channel_id=1, source_target_pairs={{0,1},{1,2},{2,3},{4,5},{5,6},{6,7},{8,9},{9,10},{10,11},{12,13},{... | collective-permute-start | bytes 147464 | tf_op jit(solution)/shard_map/ppermute | solution.py:15
  20.6 4.8 %collective-permute-start.3 = (bf16[6,1,32,128]{3,2,1,0:T(8,128)(2,1)S(1)}, bf16[6,1,32,128]{3,2,1,0:T(8,128)(2,1)S(1)}, u32[]{:S(2)}, u32[]{:S(2)}) collective-permute-start(bf16[6,1,32,128]{3,2,1,0:T(8,128)(2,1)S(1)} %get-tuple-element.15), channel_id=1, source_target_pairs={{1,0},{2,1},{3,2},{5,4},{6,5},{7,6},{9,8},{10,9},{11,10},{13,12},{... | collective-permute-start | bytes 147464 | tf_op jit(solution)/shard_map/ppermute | solution.py:17
  30.0 5.2 %copy-start.4 = (pred[8,17]{0,1:T(8,128)(4,1)S(1)}, pred[8,17]{0,1:T(8,128)(4,1)}, u32[]{:S(2)}) copy-start(pred[8,17]{0,1:T(8,128)(4,1)} %constant.27) | copy-start | bytes 412
  39.7 8.4 %collective-permute-start.4 = (bf16[1,8,32,128]{2,1,3,0:T(8,128)(2,1)S(1)}, bf16[1,8,32,128]{2,1,3,0:T(8,128)(2,1)S(1)}, u32[]{:S(2)}, u32[]{:S(2)}) collective-permute-start(bf16[1,8,32,128]{2,1,3,0:T(8,128)(2,1)S(1)} %slice_bitcast_fusion.2), channel_id=1, source_target_pairs={{0,4},{4,8},{8,12},{1,5},{5,9},{9,13},{2,6},{6,10},{10,14},{3,7},{... | collective-permute-start | bytes 196616 | tf_op jit(solution)/shard_map/ppermute | solution.py:15
  43.3 9.5 %collective-permute-start.5 = (bf16[1,8,32,128]{2,1,3,0:T(8,128)(2,1)S(1)}, bf16[1,8,32,128]{2,1,3,0:T(8,128)(2,1)S(1)}, u32[]{:S(2)}, u32[]{:S(2)}) collective-permute-start(bf16[1,8,32,128]{2,1,3,0:T(8,128)(2,1)S(1)} %slice_bitcast_fusion.1), channel_id=1, source_target_pairs={{4,0},{8,4},{12,8},{5,1},{9,5},{13,9},{6,2},{10,6},{14,10},{7,3},{... | collective-permute-start | bytes 196616 | tf_op jit(solution)/shard_map/ppermute | solution.py:17
  44.6 13.2 %copy-start.1 = (f32[4,8,128]{2,1,0:T(8,128)S(1)}, f32[4,8,128]{2,1,0:T(8,128)}, u32[]{:S(2)}) copy-start(f32[4,8,128]{2,1,0:T(8,128)} %param.6) | copy-start | bytes 49156
  53.1 4.9 %collective-permute-start.6 = (bf16[6,1,32,128]{3,2,1,0:T(8,128)(2,1)S(1)}, bf16[6,1,32,128]{3,2,1,0:T(8,128)(2,1)S(1)}, u32[]{:S(2)}, u32[]{:S(2)}) collective-permute-start(bf16[6,1,32,128]{3,2,1,0:T(8,128)(2,1)S(1)} %get-tuple-element.12), channel_id=1, source_target_pairs={{0,1},{1,2},{2,3},{4,5},{5,6},{6,7},{8,9},{9,10},{10,11},{12,13},{... | collective-permute-start | bytes 147464 | tf_op jit(solution)/shard_map/ppermute | solution.py:15
  56.3 3.1 %collective-permute-start.7 = (bf16[6,1,32,128]{3,2,1,0:T(8,128)(2,1)S(1)}, bf16[6,1,32,128]{3,2,1,0:T(8,128)(2,1)S(1)}, u32[]{:S(2)}, u32[]{:S(2)}) collective-permute-start(bf16[6,1,32,128]{3,2,1,0:T(8,128)(2,1)S(1)} %get-tuple-element.13), channel_id=1, source_target_pairs={{1,0},{2,1},{3,2},{5,4},{6,5},{7,6},{9,8},{10,9},{11,10},{13,12},{... | collective-permute-start | bytes 147464 | tf_op jit(solution)/shard_map/ppermute | solution.py:17
  64.0 5.2 %copy-start.3 = (bf16[3,3,3,32,32]{4,3,2,1,0:T(8,128)(2,1)S(1)}, bf16[3,3,3,32,32]{4,3,2,1,0:T(8,128)(2,1)}, u32[]{:S(2)}) copy-start(bf16[3,3,3,32,32]{4,3,2,1,0:T(8,128)(2,1)} %param.8) | copy-start | bytes 165892
  73.5 0.7 copy-start.2
Sparse Core Ops, SparseCore 0:
  94.6 34.1 all-reduce.2
where the time goes:
time: 138 us; the launch traced here: 137 us
  blocking collectives  36.4 us (26%)
  waiting for transfers between devices  31.3 us (23%)
  local copies, waits for them, and re-layouts  24.9 us (18%)
  starting transfers between devices  18.4 us (13%)
  between operations  14.4 us (10%)
  matrix products  8.49 us (6%)
  other arithmetic  3.27 us (2%)
    conv_general_dilated x6, local copies, waits for them, and re-layouts, convolve(): lax.conv_general_dilated(padded[None], kernel, (1, 1, 1), ((0, 0), (0, 0)...  18.5 us
    psum x1, blocking collectives, per_device(): lax.psum((local_sum, local_feat, local_depth), 'depth')  18.5 us
    pmax x1, blocking collectives, per_device(): peak = lax.pmax(local_peak, 'depth')  17.9 us
    psum x1, waiting for transfers between devices, per_device(): lax.psum((local_sum, local_feat, local_depth), 'depth')  15.1 us
    ppermute x4, starting transfers between devices, padded_2(): lax.ppermute(tail, axis, [(i, (i + 1) % count) for i in range(ends)])  13 us
    ppermute x4, waiting for transfers between devices, padded_2(): lax.ppermute(head, axis, [((i + 1) % count, i) for i in range(ends)])  12.9 us
    conv_general_dilated x2, matrix products, convolve(): lax.conv_general_dilated(padded[None], kernel, (1, 1, 1), ((0, 0), (0, 0)...  8.49 us
    ppermute x4, starting transfers between devices, padded_2(): lax.ppermute(head, axis, [((i + 1) % count, i) for i in range(ends)])  5.35 us
  transfers between devices with their start and end apart: 9, of which 7 were waited for; matrix products, arithmetic and copies ran while one was open for 2% of the time, Pallas kernels for 0%

commit v1 on v0

v1 whole, which is shorter than its diff:
```python
import functools

import jax
import jax.numpy as jnp
from jax import lax
from jax.experimental import pallas as pl
from jax.experimental.pallas import tpu as pltpu
from jax.sharding import PartitionSpec as P

F32 = jnp.float32
BF16 = jnp.bfloat16
AXES = ("depth", "rows")
VMEM = pl.BlockSpec(memory_space=pltpu.VMEM)


def exchange(value, shape, target):
    depth, rows = shape
    pairs = []
    for d in range(depth):
        for r in range(rows):
            to_d, to_r = target(d, r)
            if 0 <= to_d < depth and 0 <= to_r < rows:
                pairs.append((d * rows + r, to_d * rows + to_r))
    return lax.ppermute(value, AXES, pairs)


def prepare_kernel(k1_ref, k2_ref, proj_ref, w1_ref, w2_ref, pb_ref):
    taps = k1_ref.shape[0]
    chans = k1_ref.shape[3]
    span = taps * chans
    for k_ref, w_ref in ((k1_ref, w1_ref), (k2_ref, w2_ref)):
        made = w_ref.shape[0] // (taps * chans)
        for e in range(taps):
            flat = jnp.concatenate(
                [k_ref[a, b, e].astype(F32) for a in range(taps) for b in range(taps)]
                + [jnp.zeros(((made - 1) * span, chans), F32)],
                axis=0,
            )
            turned = flat.T
            for p in range(made):
                moved = turned if p == 0 else pltpu.roll(turned, p * span, 1)
                at = (e * made + p) * chans
                w_ref[at : at + chans, :] = moved.astype(BF16)
    lanes = pb_ref.shape[1]
    pb_ref[...] = jnp.broadcast_to(proj_ref[...], (lanes, chans)).T


def shifted_sum(y, group):
    width = y.shape[1] // 2
    lane = lax.broadcasted_iota(jnp.int32, (1, width), 1)
    parts = []
    for s in range(2):
        cols = slice(s * width, (s + 1) * width)
        before = pltpu.roll(y[:group, cols], 1, 1)
        here = y[group : 2 * group, cols]
        after = pltpu.roll(y[2 * group :, cols], width - 1, 1)
        parts.append(
            here + jnp.where(lane == 0, 0.0, before) + jnp.where(lane == width - 1, 0.0, after)
        )
    return parts


def pieces(value, count):
    out = []
    for _ in range(count - 1):
        top = value.astype(BF16).astype(F32)
        out.append(top)
        value = value - top
    return out + [value]


def store_parcel(ref, rows, feats, peak, total, depth):
    for i in range(rows):
        ref[i] = feats[i].astype(BF16)
    chans = ref.shape[1]
    flat = pieces(peak * 0.5, 3) + pieces(total, 2) + pieces(depth, 2)
    flat = flat + [jnp.zeros_like(peak)] * (-len(flat) % (chans // rows))
    per = chans // rows
    for j in range(0, len(flat), per):
        ref[rows + j // per] = jnp.concatenate(flat[j : j + per], axis=0).astype(BF16)


def load_stats(ref, rows):
    per = ref.shape[1] // rows
    flat = []
    for j in range(ref.shape[0] - rows):
        block = ref[rows + j].astype(F32)
        flat += [block[k * rows : (k + 1) * rows] for k in range(per)]
    peak = ((flat[0] + flat[1]) + flat[2]) * 2.0
    return peak, flat[3] + flat[4], flat[5] + flat[6]


def stat_blocks(rows, chans):
    per = chans // rows
    return -(-7 // per)


def volume_kernel(
    shape, own_ref, sib_ref, zh_ref, xt_ref, xb_ref, dt_ref, db_ref, op_ref, sp_ref, w1_ref,
    w2_ref, pb_ref, keep_ref, stat_ref, send_ref, xs_ref, fs_ref, ps_ref, ss_ref,
):
    depth, rows_axis = shape
    planes, rows, chans, width = own_ref.shape
    half = planes // 2
    halo = 2
    wide = 2 * width
    d = lax.axis_index("depth")
    r = lax.axis_index("rows")
    core = r % 2
    col = r // 2
    at_top = col == 0
    at_bottom = col == rows_axis // 2 - 1
    left = slice(0, width)
    right = slice(width, wide)
    zero_rows = jnp.zeros((planes, halo, chans, width), BF16)

    def fill(c):
        blocks = (own_ref, sib_ref) if c == 0 else (sib_ref, own_ref)
        base = halo * (1 - c)
        mine = slice(base, base + planes)
        zs = slice(0, halo) if c == 0 else slice(planes, planes + halo)
        n = rows + halo
        xs_ref[mine, halo:n, :, left] = blocks[0][...]
        xs_ref[mine, n:, :, left] = blocks[1][:, :halo]
        xs_ref[mine, :halo, :, right] = blocks[0][:, rows - halo :]
        xs_ref[mine, halo:n, :, right] = blocks[1][...]
        xs_ref[mine, :halo, :, left] = jnp.where(at_top, zero_rows, xt_ref[...])
        xs_ref[mine, n:, :, right] = jnp.where(at_bottom, zero_rows, xb_ref[...])
        xs_ref[zs, halo:, :, left] = zh_ref[:, :n]
        xs_ref[zs, :n, :, right] = zh_ref[:, rows - halo :]
        xs_ref[zs, :halo, :, left] = jnp.where(at_top, zero_rows[:halo], dt_ref[...])
        xs_ref[zs, n:, :, right] = jnp.where(at_bottom, zero_rows[:halo], db_ref[...])
        mine_p = slice(half * c, half * c + half)
        ps_ref[:, :, left] = (op_ref if c == 0 else sp_ref)[mine_p]
        ps_ref[:, :, right] = (sp_ref if c == 0 else op_ref)[mine_p]

    for c in range(2):
        pl.when(core == c)(functools.partial(fill, c))

    group = half * chans
    first_plane = d * planes + core * half - 1
    all_planes = depth * planes
    w1 = w1_ref[...]
    for g in range(0, half + 2, half):
        for i in range(rows + 2):
            x = xs_ref[g : g + half + 2, i : i + 3].reshape((half + 2) * 3 * chans, wide)
            y = jnp.dot(w1, x, preferred_element_type=F32)
            lo, hi = shifted_sum(y, group)
            lo = jnp.maximum(lo, 0.0)
            hi = jnp.maximum(hi, 0.0)
            if i == 0:
                lo = jnp.where(at_top, 0.0, lo)
            if i == rows + 1:
                hi = jnp.where(at_bottom, 0.0, hi)
            for p in range(half):
                part = slice(p * chans, (p + 1) * chans)
                a, b = lo[part], hi[part]
                if g + p == 0 or g + p == half + 1:
                    plane = first_plane + g + p
                    outside = jnp.logical_or(plane < 0, plane >= all_planes)
                    a = jnp.where(outside, 0.0, a)
                    b = jnp.where(outside, 0.0, b)
                fs_ref[g + p, i, :, left] = a.astype(BF16)
                fs_ref[g + p, i, :, right] = b.astype(BF16)

    w2 = w2_ref[...]
    pb = pb_ref[...]
    kept = core == 0
    fracs = [
        ((first_plane + 1 + p).astype(F32) + 0.5) / all_planes for p in range(half)
    ]
    for i in range(rows):
        x = fs_ref[:, i : i + 3].reshape((half + 2) * 3 * chans, wide)
        y = jnp.dot(w2, x, preferred_element_type=F32)
        sides = []
        for s, side in enumerate(shifted_sum(y, group)):
            cols = left if s == 0 else right
            side = jnp.maximum(side, 0.0).astype(BF16).astype(F32)
            feats = [side[p * chans : (p + 1) * chans] for p in range(half)]
            scores = [
                jnp.sum(feats[p] * pb, axis=0, keepdims=True) + ps_ref[p, i : i + 1, cols]
                for p in range(half)
            ]
            peak = functools.reduce(jnp.maximum, scores)
            weights = [jnp.exp(s_ - peak) for s_ in scores]
            total = functools.reduce(jnp.add, weights)
            depth_sum = functools.reduce(jnp.add, [w * f for w, f in zip(weights, fracs)])
            feat = functools.reduce(jnp.add, [w * f for w, f in zip(weights, feats)])
            sides.append((feat, peak, total, depth_sum))
        lo, hi = sides
        keep_ref[i] = jnp.where(kept, lo[0], hi[0])
        send_ref[i] = jnp.where(kept, hi[0], lo[0]).astype(BF16)
        for k in range(3):
            stat_ref[k, i : i + 1, :] = jnp.where(kept, lo[k + 1], hi[k + 1])
            ss_ref[k, i : i + 1, :] = jnp.where(kept, hi[k + 1], lo[k + 1])
    per = chans // rows
    flat = pieces(ss_ref[0] * 0.5, 3) + pieces(ss_ref[1], 2) + pieces(ss_ref[2], 2)
    flat = flat + [jnp.zeros_like(flat[0])] * (-len(flat) % per)
    for j in range(0, len(flat), per):
        send_ref[rows + j // per] = jnp.concatenate(flat[j : j + per], axis=0).astype(BF16)


def merge(one, two, rows):
    (feat_a, stats_a), (feat_b, stats_b) = one, two
    peak = jnp.maximum(stats_a[0], stats_b[0])
    wa = jnp.exp(stats_a[0] - peak)
    wb = jnp.exp(stats_b[0] - peak)
    total = wa * stats_a[1] + wb * stats_b[1]
    depth = wa * stats_a[2] + wb * stats_b[2]
    feats = [
        wa[i : i + 1] * feat_a(i) + wb[i : i + 1] * feat_b(i) for i in range(rows)
    ]
    return feats, peak, total, depth


def parcel(ref, rows):
    return (lambda i: ref[i].astype(F32)), load_stats(ref, rows)


def first_merge_kernel(keep_ref, stat_ref, got_ref, out_ref):
    rows = keep_ref.shape[0]
    mine = (lambda i: keep_ref[i]), tuple(stat_ref[k] for k in range(3))
    store_parcel(out_ref, rows, *merge(mine, parcel(got_ref, rows), rows))


def merge_kernel(step, own_ref, got_ref, out_ref):
    chans = own_ref.shape[1]
    rows = stat_ref_rows(own_ref.shape)
    low = (lax.axis_index("depth") // step) % 2 == 0

    def go(a_ref, b_ref):
        store_parcel(out_ref, rows, *merge(parcel(a_ref, rows), parcel(b_ref, rows), rows))

    pl.when(low)(lambda: go(own_ref, got_ref))
    pl.when(jnp.logical_not(low))(lambda: go(got_ref, own_ref))


def stat_ref_rows(shape):
    for rows in range(1, shape[0]):
        if rows + stat_blocks(rows, shape[1]) == shape[0]:
            return rows


def last_merge_kernel(step, own_ref, got_ref, joined_ref, depth_ref):
    rows = joined_ref.shape[0]
    low = (lax.axis_index("depth") // step) % 2 == 0

    def go(a_ref, b_ref):
        feats, _, total, depth = merge(parcel(a_ref, rows), parcel(b_ref, rows), rows)
        inverse = 1.0 / total
        for i in range(rows):
            joined_ref[i] = feats[i] * inverse[i : i + 1]
        depth_ref[...] = depth * inverse

    pl.when(low)(lambda: go(own_ref, got_ref))
    pl.when(jnp.logical_not(low))(lambda: go(got_ref, own_ref))


def call(kernel, outs, *args, scratch=(), flops=0, nbytes=0):
    return pl.pallas_call(
        kernel,
        out_shape=[jax.ShapeDtypeStruct(s, t) for s, t in outs],
        in_specs=[VMEM] * len(args),
        out_specs=[VMEM] * len(outs),
        scratch_shapes=list(scratch),
        cost_estimate=pl.CostEstimate(flops=flops, bytes_accessed=nbytes, transcendentals=0),
    )(*args)


def per_device(volume, prior, first_kernel, second_kernel, projection):
    planes, rows, chans, width = volume.shape
    depth, rows_axis = lax.axis_size("depth"), lax.axis_size("rows")
    shape = (depth, rows_axis)
    half = planes // 2
    halo = 2
    taps = first_kernel.shape[0]
    columns = rows_axis // 2
    assert half == halo and rows_axis % 2 == 0 and depth & (depth - 1) == 0 and chans % rows == 0

    def move(value, target):
        return exchange(value, shape, target)

    weight_shape = (taps * half * chans, (half + 2) * taps * chans)
    w1, w2, pb = call(
        prepare_kernel,
        [(weight_shape, BF16), (weight_shape, BF16), ((chans, width), F32)],
        first_kernel, second_kernel, projection[None, :],
        flops=10**8, nbytes=10**6,
    )

    core = lax.axis_index("rows") % 2
    col = lax.axis_index("rows") // 2
    lower = core == 0
    beside = move(volume, lambda d, r: (d, r ^ 1))
    prior_beside = move(prior, lambda d, r: (d, r ^ 1))

    top = jnp.where(lower, volume, beside)
    bottom = jnp.where(lower, beside, volume)
    edge = jnp.concatenate([top, bottom], axis=1)
    edge = jnp.where(lower, edge[:half], edge[half:])
    up = lambda d, r: (d + 1, r ^ 1) if r % 2 else (d - 1, r ^ 1)
    zh = move(edge, up)
    high = slice(0, halo)
    low = slice(rows - halo, rows)
    if columns == 2:
        first_col = col == 0
        pay = jnp.where(first_col, bottom[:, low], top[:, high])
        corner = jnp.where(lower, pay[:half], pay[half:])
        xt = xb = move(pay, lambda d, r: (d, r ^ 2))
        dt = db = move(corner, lambda d, r: (up(d, r)[0], r ^ 3))
    else:
        pays = bottom[:, low], top[:, high]
        corners = [jnp.where(lower, pay[:half], pay[half:]) for pay in pays]
        xt = move(pays[0], lambda d, r: (d, r + 2))
        xb = move(pays[1], lambda d, r: (d, r - 2))
        dt = move(corners[0], lambda d, r: (up(d, r)[0], (r ^ 1) + 2))
        db = move(corners[1], lambda d, r: (up(d, r)[0], (r ^ 1) - 2))

    parcel_shape = (rows + stat_blocks(rows, chans), chans, width)
    keep, stat, send = call(
        functools.partial(volume_kernel, shape),
        [((rows, chans, width), F32), ((3, rows, width), F32), (parcel_shape, BF16)],
        volume, beside, zh, xt, xb, dt, db, prior, prior_beside, w1, w2, pb,
        scratch=[
            pltpu.VMEM((planes + halo, rows + 2 * halo, chans, 2 * width), BF16),
            pltpu.VMEM((half + 2, rows + 2, chans, 2 * width), BF16),
            pltpu.VMEM((half, rows, 2 * width), F32),
            pltpu.VMEM((3, rows, width), F32),
        ],
        flops=10**9, nbytes=2 * 10**6,
    )
    got = move(send, lambda d, r: (d, r ^ 1))
    (sums,) = call(first_merge_kernel, [(parcel_shape, BF16)], keep, stat, got)
    step = 1
    while step < depth:
        got = move(sums, lambda d, r: (d ^ step, r))
        if 2 * step < depth:
            (sums,) = call(functools.partial(merge_kernel, step), [(parcel_shape, BF16)], sums, got)
        else:
            joined, depth_estimate = call(
                functools.partial(last_merge_kernel, step),
                [((rows, chans, width), F32), ((rows, width), F32)],
                sums, got,
            )
        step *= 2
    return joined, depth_estimate


def solution(mesh):
    placed = (
        P(("tiles", "depth"), "rows", None, None),
        P(("tiles", "depth"), "rows", None),
        P(),
        P(),
        P(),
    )
    return jax.shard_map(
        per_device,
        mesh=mesh,
        in_specs=placed,
        out_specs=(P(("tiles", "rows"), None, None), P(("tiles", "rows"), None)),
        check_vma=False,
    )
```

time: 138 us -> 40.7 us (0.29)
  blocking collectives: 36.4 us -> 0 us
  local copies, waits for them, and re-layouts: 24.9 us -> 2.59 us
  waiting for transfers between devices: 31.3 us -> 10.1 us
  between operations: 14.4 us -> 0.74 us
  Pallas kernels: 0 us -> 10.8 us
  matrix products: 8.49 us -> 0 us
  starting transfers between devices: 18.4 us -> 15 us
  other arithmetic: 3.27 us -> 1.14 us
    conv_general_dilated x6 -> x0, local copies, waits for them, and re-layouts: 18.5 us -> none  [convolve(): lax.conv_general_dilated(padded[None], kernel, (1, 1, 1), ((0, 0), (0, 0)...]
    psum x1 -> x0, blocking collectives: 18.5 us -> none  [per_device(): lax.psum((local_sum, local_feat, local_depth), 'depth')]
    pmax x1 -> x0, blocking collectives: 17.9 us -> none  [per_device(): peak = lax.pmax(local_peak, 'depth')]
    psum x1 -> x0, waiting for transfers between devices: 15.1 us -> none  [per_device(): lax.psum((local_sum, local_feat, local_depth), 'depth')]
    pallas_call x0 -> x5, Pallas kernels: none -> 10.8 us  [call(): pl.pallas_call(kernel, out_shape=[jax.ShapeDtypeStruct(s, t) for s, t in...]
    conv_general_dilated x2 -> x0, matrix products: 8.49 us -> none  [convolve(): lax.conv_general_dilated(padded[None], kernel, (1, 1, 1), ((0, 0), (0, 0)...]
    ppermute x8, waiting for transfers between devices: 16.2 us -> 10.1 us  [exchange(): return lax.ppermute(value, AXES, pairs)]
    ppermute x8, starting transfers between devices: 18.4 us -> 15 us  [exchange(): return lax.ppermute(value, AXES, pairs)]
  transfers between devices with their start and end apart: 9 -> 8, of which waited for: 7 -> 4; matrix products, arithmetic and copies ran while one was open for 2% -> 0% of each run, Pallas kernels for 0% -> 5%
where the time goes in v1:
time: 40.7 us; the launch traced here: 40.4 us
  starting transfers between devices  15 us (37%)
  Pallas kernels  10.8 us (27%)
  waiting for transfers between devices  10.1 us (25%)
  local copies, waits for them, and re-layouts  2.59 us (6%)
  other arithmetic  1.14 us (3%)
  between operations  0.74 us (2%)
    ppermute x8, starting transfers between devices, exchange(): return lax.ppermute(value, AXES, pairs)  15 us
    pallas_call x5, Pallas kernels, call(): pl.pallas_call(kernel, out_shape=[jax.ShapeDtypeStruct(s, t) for s, t in...  10.8 us
    ppermute x8, waiting for transfers between devices, exchange(): return lax.ppermute(value, AXES, pairs)  10.1 us
    unnamed x18, local copies, waits for them, and re-layouts  2.59 us
    select_n x1, other arithmetic, per_device(): bottom = jnp.where(lower, beside, volume)  1.08 us
  transfers between devices with their start and end apart: 8, of which 4 were waited for; matrix products, arithmetic and copies ran while one was open for 0% of the time, Pallas kernels for 5%

profile of v1, /device:TPU:0, one launch (start us, length us, event | category | flops | bytes accessed | tf_op | source)
XLA Modules:
  0.0 40.4 jit_solution(7790934558089480208)
XLA Ops:
  0.6 0.6 %collective-permute-start = (bf16[4,8,32,128]{3,2,1,0:T(8,128)(2,1)}, bf16[4,8,32,128]{3,2,1,0:T(8,128)(2,1)S(1)}, u32[]{:S(2)}, u32[]{:S(2)}) collective-permute-start(bf16[4,8,32,128]{3,2,1,0:T(8,128)(2,1)} %own_ref.1), channel_id=1, source_target_pairs={{0,1},{1,0},{2,3},{3,2},{4,5},{5,4},{6,7},{7,6},{8,9},{9,8},{10,11... | collective-permute-start | bytes 786440 | tf_op jit(solution)/shard_map/ppermute | solution.py:24
  1.2 1.4 %collective-permute-done.sib_ref = bf16[4,8,32,128]{3,2,1,0:T(8,128)(2,1)S(1)} collective-permute-done((bf16[4,8,32,128]{3,2,1,0:T(8,128)(2,1)}, bf16[4,8,32,128]{3,2,1,0:T(8,128)(2,1)S(1)}, u32[]{:S(2)}, u32[]{:S(2)}) %collective-permute-start) | collective-permute-done | bytes 262176 | tf_op jit(solution)/shard_map/ppermute | solution.py:24
  2.6 0.0 copy-start
  2.6 1.1 %broadcast_select_fusion = (bf16[4,8,32,128]{3,2,1,0:T(8,128)(2,1)S(1)}, bf16[4,8,32,128]{3,2,1,0:T(8,128)(2,1)S(1)}) fusion(bf16[4,8,32,128]{3,2,1,0:T(8,128)(2,1)S(1)} %collective-permute-done.sib_ref, bf16[4,8,32,128]{3,2,1,0:T(8,128)(2,1)} %own_ref.1, pred[]{:T(512)S(6)} %eq.8), kind=kLoop, calls=%fused_computation.5 | loop fusion | flops 262144 | bytes 1048577 | tf_op jit(solution)/shard_map/jit(_where)/select_n | solution.py:298
  3.6 0.0 copy-done
  3.7 0.7 %collective-permute-start.1 = (bf16[2,16,32,128]{3,2,1,0:T(8,128)(2,1)S(1)}, bf16[2,16,32,128]{3,2,1,0:T(8,128)(2,1)S(1)}, u32[]{:S(2)}, u32[]{:S(2)}) collective-permute-start(bf16[2,16,32,128]{3,2,1,0:T(8,128)(2,1)S(1)} %fusion.1), channel_id=1, source_target_pairs={{1,4},{3,6},{4,1},{5,8},{6,3},{7,10},{8,5},{9,12},{10,7},{11,14},{... | collective-permute-start | bytes 786440 | tf_op jit(solution)/shard_map/ppermute | solution.py:24
  4.4 0.0 copy-start.7
  4.4 2.9 %collective-permute-start.2 = (bf16[4,2,32,128]{3,2,1,0:T(8,128)(2,1)S(1)}, bf16[4,2,32,128]{3,2,1,0:T(8,128)(2,1)S(1)}, u32[]{:S(2)}, u32[]{:S(2)}) collective-permute-start(bf16[4,2,32,128]{3,2,1,0:T(8,128)(2,1)S(1)} %slice_select_fusion), channel_id=1, source_target_pairs={{0,2},{1,3},{2,0},{3,1},{4,6},{5,7},{6,4},{7,5},{8,10},{9,11},{10,... | collective-permute-start | bytes 196616 | tf_op jit(solution)/shard_map/ppermute | solution.py:24
  7.3 0.7 %collective-permute-start.3 = (bf16[2,2,32,128]{3,2,1,0:T(8,128)(2,1)S(1)}, bf16[2,2,32,128]{3,2,1,0:T(8,128)(2,1)S(1)}, u32[]{:S(2)}, u32[]{:S(2)}) collective-permute-start(bf16[2,2,32,128]{3,2,1,0:T(8,128)(2,1)S(1)} %slice_select_fusion.1), channel_id=1, source_target_pairs={{1,6},{3,4},{4,3},{5,10},{6,1},{7,8},{8,7},{9,14},{10,5},{11,12},{... | collective-permute-start | bytes 98312 | tf_op jit(solution)/shard_map/ppermute | solution.py:24
  8.0 0.0 copy-done.7
  8.0 4.2 %collective-permute-start.4 = (f32[4,8,128]{2,1,0:T(8,128)S(1)}, f32[4,8,128]{2,1,0:T(8,128)S(1)}, u32[]{:S(2)}, u32[]{:S(2)}) collective-permute-start(f32[4,8,128]{2,1,0:T(8,128)S(1)} %copy-done.7), channel_id=1, source_target_pairs={{0,1},{1,0},{2,3},{3,2},{4,5},{5,4},{6,7},{7,6},{8,9},{9,8},{10,11... | collective-permute-start | bytes 49160 | tf_op jit(solution)/shard_map/ppermute | solution.py:24
  12.2 2.1 %shard_map.68 = (bf16[192,384]{1,0:T(8,128)(2,1)}, bf16[192,384]{1,0:T(8,128)(2,1)}, f32[32,128]{1,0:T(8,128)}) custom-call(bf16[3,3,3,32,32]{4,3,2,1,0:T(8,128)(2,1)} %k1_ref.1, bf16[3,3,3,32,32]{4,3,2,1,0:T(8,128)(2,1)} %k2_ref.1, f32[1,32]{1,0:T(1,128)} %bitcast.1), custom_call_target="tpu_custom_call" | custom-call | flops 100000000 | bytes 1000000 | tf_op jit(solution)/shard_map/pallas_call | solution.py:260
  14.3 0.0 collective-permute-done.4.sp_ref
  14.3 0.0 copy-start.8
  14.3 0.0 collective-permute-done.3.dt_ref.db_ref
  14.3 0.0 copy-start.6
  14.3 0.0 collective-permute-done.2.xt_ref.xb_ref
  14.3 0.0 copy-start.5
  14.3 0.0 collective-permute-done.1.zh_ref
  14.3 0.0 copy-start.4
  14.4 0.5 %copy-done.8 = f32[4,8,128]{2,1,0:T(8,128)} copy-done((f32[4,8,128]{2,1,0:T(8,128)}, f32[4,8,128]{2,1,0:T(8,128)S(1)}, u32[]{:S(2)}) %copy-start.8) | copy-done | bytes 16408
  14.9 0.0 copy-done.6
  14.9 0.0 copy-done.5
  15.0 0.1 copy-done.4
  15.1 3.9 %shard_map.69 = (f32[8,32,128]{2,1,0:T(8,128)}, f32[3,8,128]{2,1,0:T(8,128)}, bf16[10,32,128]{2,1,0:T(8,128)(2,1)}) custom-call(bf16[4,8,32,128]{3,2,1,0:T(8,128)(2,1)} %own_ref.1, bf16[4,8,32,128]{3,2,1,0:T(8,128)(2,1)} %copy-done, bf16[2,16,32,128]{3,2,1,0:T(8,128)(2,1)} %copy-done.4, bf16[4,2,32,128]{3,2,1,0:T(8,128)(2,1)} %copy-done.5, ...), custom_call_target="tpu_custom_call" | custom-call | flops 1000000000 | bytes 2000000 | tf_op jit(solution)/shard_map/pallas_call | solution.py:260
  19.0 1.8 %collective-permute-start.5 = (bf16[10,32,128]{2,1,0:T(8,128)(2,1)}, bf16[10,32,128]{2,1,0:T(8,128)(2,1)S(1)}, u32[]{:S(2)}, u32[]{:S(2)}) collective-permute-start(bf16[10,32,128]{2,1,0:T(8,128)(2,1)} %get-tuple-element.13), channel_id=1, source_target_pairs={{0,1},{1,0},{2,3},{3,2},{4,5},{5,4},{6,7},{7,6},{8,9},{9,8},{10,11... | collective-permute-start | bytes 245768 | tf_op jit(solution)/shard_map/ppermute | solution.py:24
  20.8 1.1 %collective-permute-done.5.got_ref = bf16[10,32,128]{2,1,0:T(8,128)(2,1)S(1)} collective-permute-done((bf16[10,32,128]{2,1,0:T(8,128)(2,1)}, bf16[10,32,128]{2,1,0:T(8,128)(2,1)S(1)}, u32[]{:S(2)}, u32[]{:S(2)}) %collective-permute-start.5) | collective-permute-done | bytes 81952 | tf_op jit(solution)/shard_map/ppermute | solution.py:24
  21.9 0.0 copy-start.2
  21.9 0.6 %copy-done.2 = bf16[10,32,128]{2,1,0:T(8,128)(2,1)} copy-done((bf16[10,32,128]{2,1,0:T(8,128)(2,1)}, bf16[10,32,128]{2,1,0:T(8,128)(2,1)S(1)}, u32[]{:S(2)}) %copy-start.2) | copy-done | bytes 81944
  22.5 1.6 %shard_map.70.own_ref = bf16[10,32,128]{2,1,0:T(8,128)(2,1)} custom-call(f32[8,32,128]{2,1,0:T(8,128)} %get-tuple-element.11.keep_ref, f32[3,8,128]{2,1,0:T(8,128)} %get-tuple-element.12.stat_ref, bf16[10,32,128]{2,1,0:T(8,128)(2,1)} %copy-done.2), custom_call_target="tpu_custom_call" | custom-call | tf_op jit(solution)/shard_map/pallas_call | solution.py:260
  24.2 1.6 %collective-permute-start.6 = (bf16[10,32,128]{2,1,0:T(8,128)(2,1)}, bf16[10,32,128]{2,1,0:T(8,128)(2,1)S(1)}, u32[]{:S(2)}, u32[]{:S(2)}) collective-permute-start(bf16[10,32,128]{2,1,0:T(8,128)(2,1)} %shard_map.70.own_ref), channel_id=1, source_target_pairs={{0,4},{1,5},{2,6},{3,7},{4,0},{5,1},{6,2},{7,3},{8,12},{9,13},{10,... | collective-permute-start | bytes 245768 | tf_op jit(solution)/shard_map/ppermute | solution.py:24
  25.7 3.3 %collective-permute-done.6.got_ref = bf16[10,32,128]{2,1,0:T(8,128)(2,1)S(1)} collective-permute-done((bf16[10,32,128]{2,1,0:T(8,128)(2,1)}, bf16[10,32,128]{2,1,0:T(8,128)(2,1)S(1)}, u32[]{:S(2)}, u32[]{:S(2)}) %collective-permute-start.6) | collective-permute-done | bytes 81952 | tf_op jit(solution)/shard_map/ppermute | solution.py:24
  29.1 0.0 copy-start.3
  29.1 0.6 %copy-done.3 = bf16[10,32,128]{2,1,0:T(8,128)(2,1)} copy-done((bf16[10,32,128]{2,1,0:T(8,128)(2,1)}, bf16[10,32,128]{2,1,0:T(8,128)(2,1)S(1)}, u32[]{:S(2)}) %copy-start.3) | copy-done | bytes 81944
  29.7 1.6 %shard_map.71.own_ref = bf16[10,32,128]{2,1,0:T(8,128)(2,1)} custom-call(bf16[10,32,128]{2,1,0:T(8,128)(2,1)} %shard_map.70.own_ref, bf16[10,32,128]{2,1,0:T(8,128)(2,1)} %copy-done.3), custom_call_target="tpu_custom_call" | custom-call | tf_op jit(solution)/shard_map/pallas_call | solution.py:260
  31.3 2.6 %collective-permute-start.7 = (bf16[10,32,128]{2,1,0:T(8,128)(2,1)}, bf16[10,32,128]{2,1,0:T(8,128)(2,1)S(1)}, u32[]{:S(2)}, u32[]{:S(2)}) collective-permute-start(bf16[10,32,128]{2,1,0:T(8,128)(2,1)} %shard_map.71.own_ref), channel_id=1, source_target_pairs={{0,8},{1,9},{2,10},{3,11},{4,12},{5,13},{6,14},{7,15},{8,0},{9,1},... | collective-permute-start | bytes 245768 | tf_op jit(solution)/shard_map/ppermute | solution.py:24
  33.9 4.3 %collective-permute-done.7.got_ref = bf16[10,32,128]{2,1,0:T(8,128)(2,1)S(1)} collective-permute-done((bf16[10,32,128]{2,1,0:T(8,128)(2,1)}, bf16[10,32,128]{2,1,0:T(8,128)(2,1)S(1)}, u32[]{:S(2)}, u32[]{:S(2)}) %collective-permute-start.7) | collective-permute-done | bytes 81952 | tf_op jit(solution)/shard_map/ppermute | solution.py:24
  38.2 0.0 copy-start.1
  38.2 0.6 %copy-done.1 = bf16[10,32,128]{2,1,0:T(8,128)(2,1)} copy-done((bf16[10,32,128]{2,1,0:T(8,128)(2,1)}, bf16[10,32,128]{2,1,0:T(8,128)(2,1)S(1)}, u32[]{:S(2)}) %copy-start.1) | copy-done | bytes 81944
  38.8 1.6 %shard_map.72 = (f32[8,32,128]{2,1,0:T(8,128)}, f32[8,128]{1,0:T(8,128)}) custom-call(bf16[10,32,128]{2,1,0:T(8,128)(2,1)} %shard_map.71.own_ref, bf16[10,32,128]{2,1,0:T(8,128)(2,1)} %copy-done.1), custom_call_target="tpu_custom_call" | custom-call | tf_op jit(solution)/shard_map/pallas_call | solution.py:260
  (3 shorter events, 0.1 us)
Async XLA Ops:
  0.6 1.9 %collective-permute-start = (bf16[4,8,32,128]{3,2,1,0:T(8,128)(2,1)}, bf16[4,8,32,128]{3,2,1,0:T(8,128)(2,1)S(1)}, u32[]{:S(2)}, u32[]{:S(2)}) collective-permute-start(bf16[4,8,32,128]{3,2,1,0:T(8,128)(2,1)} %own_ref.1), channel_id=1, source_target_pairs={{0,1},{1,0},{2,3},{3,2},{4,5},{5,4},{6,7},{7,6},{8,9},{9,8},{10,11... | collective-permute-start | bytes 786440 | tf_op jit(solution)/shard_map/ppermute | solution.py:24
  2.6 1.1 %copy-start = (bf16[4,8,32,128]{3,2,1,0:T(8,128)(2,1)}, bf16[4,8,32,128]{3,2,1,0:T(8,128)(2,1)S(1)}, u32[]{:S(2)}) copy-start(bf16[4,8,32,128]{3,2,1,0:T(8,128)(2,1)S(1)} %collective-permute-done.sib_ref) | copy-start | bytes 786436
  3.7 10.6 %collective-permute-start.1 = (bf16[2,16,32,128]{3,2,1,0:T(8,128)(2,1)S(1)}, bf16[2,16,32,128]{3,2,1,0:T(8,128)(2,1)S(1)}, u32[]{:S(2)}, u32[]{:S(2)}) collective-permute-start(bf16[2,16,32,128]{3,2,1,0:T(8,128)(2,1)S(1)} %fusion.1), channel_id=1, source_target_pairs={{1,4},{3,6},{4,1},{5,8},{6,3},{7,10},{8,5},{9,12},{10,7},{11,14},{... | collective-permute-start | bytes 786440 | tf_op jit(solution)/shard_map/ppermute | solution.py:24
  4.4 3.6 %copy-start.7 = (f32[4,8,128]{2,1,0:T(8,128)S(1)}, f32[4,8,128]{2,1,0:T(8,128)}, u32[]{:S(2)}) copy-start(f32[4,8,128]{2,1,0:T(8,128)} %op_ref.1) | copy-start | bytes 49156
  4.4 9.9 %collective-permute-start.2 = (bf16[4,2,32,128]{3,2,1,0:T(8,128)(2,1)S(1)}, bf16[4,2,32,128]{3,2,1,0:T(8,128)(2,1)S(1)}, u32[]{:S(2)}, u32[]{:S(2)}) collective-permute-start(bf16[4,2,32,128]{3,2,1,0:T(8,128)(2,1)S(1)} %slice_select_fusion), channel_id=1, source_target_pairs={{0,2},{1,3},{2,0},{3,1},{4,6},{5,7},{6,4},{7,5},{8,10},{9,11},{10,... | collective-permute-start | bytes 196616 | tf_op jit(solution)/shard_map/ppermute | solution.py:24
  7.3 7.0 %collective-permute-start.3 = (bf16[2,2,32,128]{3,2,1,0:T(8,128)(2,1)S(1)}, bf16[2,2,32,128]{3,2,1,0:T(8,128)(2,1)S(1)}, u32[]{:S(2)}, u32[]{:S(2)}) collective-permute-start(bf16[2,2,32,128]{3,2,1,0:T(8,128)(2,1)S(1)} %slice_select_fusion.1), channel_id=1, source_target_pairs={{1,6},{3,4},{4,3},{5,10},{6,1},{7,8},{8,7},{9,14},{10,5},{11,12},{... | collective-permute-start | bytes 98312 | tf_op jit(solution)/shard_map/ppermute | solution.py:24
  8.0 6.3 %collective-permute-start.4 = (f32[4,8,128]{2,1,0:T(8,128)S(1)}, f32[4,8,128]{2,1,0:T(8,128)S(1)}, u32[]{:S(2)}, u32[]{:S(2)}) collective-permute-start(f32[4,8,128]{2,1,0:T(8,128)S(1)} %copy-done.7), channel_id=1, source_target_pairs={{0,1},{1,0},{2,3},{3,2},{4,5},{5,4},{6,7},{7,6},{8,9},{9,8},{10,11... | collective-permute-start | bytes 49160 | tf_op jit(solution)/shard_map/ppermute | solution.py:24
  14.3 0.6 %copy-start.8 = (f32[4,8,128]{2,1,0:T(8,128)}, f32[4,8,128]{2,1,0:T(8,128)S(1)}, u32[]{:S(2)}) copy-start(f32[4,8,128]{2,1,0:T(8,128)S(1)} %collective-permute-done.4.sp_ref) | copy-start | bytes 49156
  14.3 0.6 %copy-start.6 = (bf16[2,2,32,128]{3,2,1,0:T(8,128)(2,1)}, bf16[2,2,32,128]{3,2,1,0:T(8,128)(2,1)S(1)}, u32[]{:S(2)}) copy-start(bf16[2,2,32,128]{3,2,1,0:T(8,128)(2,1)S(1)} %collective-permute-done.3.dt_ref.db_ref) | copy-start | bytes 98308
  14.3 0.6 %copy-start.5 = (bf16[4,2,32,128]{3,2,1,0:T(8,128)(2,1)}, bf16[4,2,32,128]{3,2,1,0:T(8,128)(2,1)S(1)}, u32[]{:S(2)}) copy-start(bf16[4,2,32,128]{3,2,1,0:T(8,128)(2,1)S(1)} %collective-permute-done.2.xt_ref.xb_ref) | copy-start | bytes 196612
  14.3 0.7 %copy-start.4 = (bf16[2,16,32,128]{3,2,1,0:T(8,128)(2,1)}, bf16[2,16,32,128]{3,2,1,0:T(8,128)(2,1)S(1)}, u32[]{:S(2)}) copy-start(bf16[2,16,32,128]{3,2,1,0:T(8,128)(2,1)S(1)} %collective-permute-done.1.zh_ref) | copy-start | bytes 786436
  19.0 2.9 %collective-permute-start.5 = (bf16[10,32,128]{2,1,0:T(8,128)(2,1)}, bf16[10,32,128]{2,1,0:T(8,128)(2,1)S(1)}, u32[]{:S(2)}, u32[]{:S(2)}) collective-permute-start(bf16[10,32,128]{2,1,0:T(8,128)(2,1)} %get-tuple-element.13), channel_id=1, source_target_pairs={{0,1},{1,0},{2,3},{3,2},{4,5},{5,4},{6,7},{7,6},{8,9},{9,8},{10,11... | collective-permute-start | bytes 245768 | tf_op jit(solution)/shard_map/ppermute | solution.py:24
  21.9 0.6 %copy-start.2 = (bf16[10,32,128]{2,1,0:T(8,128)(2,1)}, bf16[10,32,128]{2,1,0:T(8,128)(2,1)S(1)}, u32[]{:S(2)}) copy-start(bf16[10,32,128]{2,1,0:T(8,128)(2,1)S(1)} %collective-permute-done.5.got_ref) | copy-start | bytes 245764
  24.2 4.9 %collective-permute-start.6 = (bf16[10,32,128]{2,1,0:T(8,128)(2,1)}, bf16[10,32,128]{2,1,0:T(8,128)(2,1)S(1)}, u32[]{:S(2)}, u32[]{:S(2)}) collective-permute-start(bf16[10,32,128]{2,1,0:T(8,128)(2,1)} %shard_map.70.own_ref), channel_id=1, source_target_pairs={{0,4},{1,5},{2,6},{3,7},{4,0},{5,1},{6,2},{7,3},{8,12},{9,13},{10,... | collective-permute-start | bytes 245768 | tf_op jit(solution)/shard_map/ppermute | solution.py:24
  29.1 0.6 %copy-start.3 = (bf16[10,32,128]{2,1,0:T(8,128)(2,1)}, bf16[10,32,128]{2,1,0:T(8,128)(2,1)S(1)}, u32[]{:S(2)}) copy-start(bf16[10,32,128]{2,1,0:T(8,128)(2,1)S(1)} %collective-permute-done.6.got_ref) | copy-start | bytes 245764
  31.3 6.8 %collective-permute-start.7 = (bf16[10,32,128]{2,1,0:T(8,128)(2,1)}, bf16[10,32,128]{2,1,0:T(8,128)(2,1)S(1)}, u32[]{:S(2)}, u32[]{:S(2)}) collective-permute-start(bf16[10,32,128]{2,1,0:T(8,128)(2,1)} %shard_map.71.own_ref), channel_id=1, source_target_pairs={{0,8},{1,9},{2,10},{3,11},{4,12},{5,13},{6,14},{7,15},{8,0},{9,1},... | collective-permute-start | bytes 245768 | tf_op jit(solution)/shard_map/ppermute | solution.py:24
  38.2 0.6 %copy-start.1 = (bf16[10,32,128]{2,1,0:T(8,128)(2,1)}, bf16[10,32,128]{2,1,0:T(8,128)(2,1)S(1)}, u32[]{:S(2)}) copy-start(bf16[10,32,128]{2,1,0:T(8,128)(2,1)S(1)} %collective-permute-done.7.got_ref) | copy-start | bytes 245764

commit v2 on v1

--- a/solution.py
+++ b/solution.py
@@ -256,7 +256,7 @@
     pl.when(jnp.logical_not(low))(lambda: go(got_ref, own_ref))
 
 
-def call(kernel, outs, *args, scratch=(), flops=0, nbytes=0):
+def call(kernel, outs, *args, scratch=(), flops=0, nbytes=0, room=4):
     return pl.pallas_call(
         kernel,
         out_shape=[jax.ShapeDtypeStruct(s, t) for s, t in outs],
@@ -264,6 +264,7 @@
         out_specs=[VMEM] * len(outs),
         scratch_shapes=list(scratch),
         cost_estimate=pl.CostEstimate(flops=flops, bytes_accessed=nbytes, transcendentals=0),
+        compiler_params=pltpu.CompilerParams(vmem_limit_bytes=room * 2**20),
     )(*args)
 
 
@@ -293,23 +294,34 @@
     lower = core == 0
     beside = move(volume, lambda d, r: (d, r ^ 1))
     prior_beside = move(prior, lambda d, r: (d, r ^ 1))
-
-    top = jnp.where(lower, volume, beside)
-    bottom = jnp.where(lower, beside, volume)
-    edge = jnp.concatenate([top, bottom], axis=1)
-    edge = jnp.where(lower, edge[:half], edge[half:])
+    beside, prior_beside = lax.optimization_barrier((beside, prior_beside))
+
+    high = slice(0, halo)
+    low = slice(rows - halo, rows)
+
+    def parts(block):
+        picked = jnp.where(lower, block[:half], block[half:])
+        return picked, block[:, high], block[:, low]
+
+    own_pick, own_high, own_low = lax.optimization_barrier(parts(volume))
+    sib_pick, sib_high, sib_low = parts(beside)
+    edge = jnp.where(
+        lower,
+        jnp.concatenate([own_pick, sib_pick], axis=1),
+        jnp.concatenate([sib_pick, own_pick], axis=1),
+    )
+    top_high = jnp.where(lower, own_high, sib_high)
+    bottom_low = jnp.where(lower, sib_low, own_low)
     up = lambda d, r: (d + 1, r ^ 1) if r % 2 else (d - 1, r ^ 1)
     zh = move(edge, up)
-    high = slice(0, halo)
-    low = slice(rows - halo, rows)
     if columns == 2:
         first_col = col == 0
-        pay = jnp.where(first_col, bottom[:, low], top[:, high])
+        pay = jnp.where(first_col, bottom_low, top_high)
         corner = jnp.where(lower, pay[:half], pay[half:])
         xt = xb = move(pay, lambda d, r: (d, r ^ 2))
         dt = db = move(corner, lambda d, r: (up(d, r)[0], r ^ 3))
     else:
-        pays = bottom[:, low], top[:, high]
+        pays = bottom_low, top_high
         corners = [jnp.where(lower, pay[:half], pay[half:]) for pay in pays]
         xt = move(pays[0], lambda d, r: (d, r + 2))
         xb = move(pays[1], lambda d, r: (d, r - 2))
@@ -327,7 +339,7 @@
             pltpu.VMEM((half, rows, 2 * width), F32),
             pltpu.VMEM((3, rows, width), F32),
         ],
-        flops=10**9, nbytes=2 * 10**6,
+        flops=10**9, nbytes=2 * 10**6, room=12,
     )
     got = move(send, lambda d, r: (d, r ^ 1))
     (sums,) = call(first_merge_kernel, [(parcel_shape, BF16)], keep, stat, got)

time: 40.7 us -> 30.7 us (0.75)
  Pallas kernels: 10.8 us -> 3.12 us
  local copies, waits for them, and re-layouts: 2.59 us -> 0.04 us
  starting transfers between devices: 15 us -> 15.7 us
    pallas_call x5, Pallas kernels: 10.8 us -> 3.12 us  [call(): pl.pallas_call(kernel, out_shape=[jax.ShapeDtypeStruct(s, t) for s, t in...]
    unnamed x18 -> x10, local copies, waits for them, and re-layouts: 2.59 us -> 0.03 us
    ppermute x8, starting transfers between devices: 15 us -> 15.7 us  [exchange(): return lax.ppermute(value, AXES, pairs)]
    select_n x3 -> x4, other arithmetic: 1.14 us -> 1.04 us  [the longest x2 1 us: parts(): picked = jnp.where(lower, block[:half], block[half:])]
  transfers between devices with their start and end apart: 8 -> 8, of which waited for: 4 -> 5; matrix products, arithmetic and copies ran while one was open for 0% -> 3% of each run, Pallas kernels for 5% -> 1%
where the time goes in v2:
time: 30.7 us; the launch traced here: 30.6 us
  starting transfers between devices  15.7 us (51%)
  waiting for transfers between devices  9.85 us (32%)
  Pallas kernels  3.12 us (10%)
  other arithmetic  1.05 us (3%)
  between operations  0.79 us (3%)
    ppermute x8, starting transfers between devices, exchange(): return lax.ppermute(value, AXES, pairs)  15.7 us
    ppermute x8, waiting for transfers between devices, exchange(): return lax.ppermute(value, AXES, pairs)  9.85 us
    pallas_call x5, Pallas kernels, call(): pl.pallas_call(kernel, out_shape=[jax.ShapeDtypeStruct(s, t) for s, t in...  3.12 us
    select_n x2, other arithmetic, parts(): picked = jnp.where(lower, block[:half], block[half:])  1 us
  transfers between devices with their start and end apart: 8, of which 5 were waited for; matrix products, arithmetic and copies ran while one was open for 3% of the time, Pallas kernels for 1%

profile of v2, /device:TPU:0, one launch (start us, length us, event | category | flops | bytes accessed | tf_op | source)
XLA Modules:
  0.0 30.6 jit_solution(10750737770788061257)
XLA Ops:
  0.6 0.0 copy-start
  0.6 0.6 %collective-permute-start.1 = (f32[4,8,128]{2,1,0:T(8,128)}, f32[4,8,128]{2,1,0:T(8,128)S(1)}, u32[]{:S(2)}, u32[]{:S(2)}) collective-permute-start(f32[4,8,128]{2,1,0:T(8,128)} %op_ref.1), channel_id=1, source_target_pairs={{0,1},{1,0},{2,3},{3,2},{4,5},{5,4},{6,7},{7,6},{8,9},{9,8},{10,11... | collective-permute-start | bytes 49160 | tf_op jit(solution)/shard_map/ppermute | solution.py:24
  1.2 0.1 collective-permute-start
  1.3 1.0 %slice_select_fusion.1 = bf16[2,8,32,128]{3,2,1,0:T(8,128)(2,1)S(1)} fusion(bf16[4,8,32,128]{3,2,1,0:T(8,128)(2,1)} %own_ref.1, pred[]{:T(512)S(6)} %eq.8), kind=kLoop, calls=%fused_computation.2 | loop fusion | flops 65536 | bytes 393217 | tf_op jit(solution)/shard_map/jit(_where)/select_n | solution.py:303
  2.3 0.0 copy-done
  2.3 0.0 collective-permute-done.1.sp_ref
  2.3 0.6 %collective-permute-done.sib_ref = bf16[4,8,32,128]{3,2,1,0:T(8,128)(2,1)S(1)} collective-permute-done((bf16[4,8,32,128]{3,2,1,0:T(8,128)(2,1)}, bf16[4,8,32,128]{3,2,1,0:T(8,128)(2,1)S(1)}, u32[]{:S(2)}, u32[]{:S(2)}) %collective-permute-start) | collective-permute-done | bytes 262176 | tf_op jit(solution)/shard_map/ppermute | solution.py:24
  3.0 0.0 copy-start.2
  3.0 0.0 copy-start.1
  3.0 0.8 %collective-permute-start.2 = (bf16[2,16,32,128]{3,2,1,0:T(8,128)(2,1)S(1)}, bf16[2,16,32,128]{3,2,1,0:T(8,128)(2,1)S(1)}, u32[]{:S(2)}, u32[]{:S(2)}) collective-permute-start(bf16[2,16,32,128]{3,2,1,0:T(8,128)(2,1)S(1)} %maximum_select_fusion), channel_id=1, source_target_pairs={{1,4},{3,6},{4,1},{5,8},{6,3},{7,10},{8,5},{9,12},{10,7},{11,14},{... | collective-permute-start | bytes 786440 | tf_op jit(solution)/shard_map/ppermute | solution.py:24
  3.9 2.7 %collective-permute-start.3 = (bf16[4,2,32,128]{3,2,1,0:T(8,128)(2,1)S(1)}, bf16[4,2,32,128]{3,2,1,0:T(8,128)(2,1)S(1)}, u32[]{:S(2)}, u32[]{:S(2)}) collective-permute-start(bf16[4,2,32,128]{3,2,1,0:T(8,128)(2,1)S(1)} %select_select_fusion), channel_id=1, source_target_pairs={{0,2},{1,3},{2,0},{3,1},{4,6},{5,7},{6,4},{7,5},{8,10},{9,11},{10,... | collective-permute-start | bytes 196616 | tf_op jit(solution)/shard_map/ppermute | solution.py:24
  6.5 0.0 copy-start.3
  6.6 0.7 %collective-permute-start.4 = (bf16[2,2,32,128]{3,2,1,0:T(8,128)(2,1)S(1)}, bf16[2,2,32,128]{3,2,1,0:T(8,128)(2,1)S(1)}, u32[]{:S(2)}, u32[]{:S(2)}) collective-permute-start(bf16[2,2,32,128]{3,2,1,0:T(8,128)(2,1)S(1)} %slice_select_fusion.2), channel_id=1, source_target_pairs={{1,6},{3,4},{4,3},{5,10},{6,1},{7,8},{8,7},{9,14},{10,5},{11,12},{... | collective-permute-start | bytes 98312 | tf_op jit(solution)/shard_map/ppermute | solution.py:24
  7.2 0.0 copy-done.2
  7.2 0.0 copy-done.1
  7.2 0.0 copy-done.3
  7.3 0.0 copy-start.4
  7.3 0.4 %shard_map.68 = (bf16[192,384]{1,0:T(8,128)(2,1)S(1)}, bf16[192,384]{1,0:T(8,128)(2,1)S(1)}, f32[32,128]{1,0:T(8,128)S(1)}) custom-call(bf16[3,3,3,32,32]{4,3,2,1,0:T(8,128)(2,1)S(1)} %copy-done.1, bf16[3,3,3,32,32]{4,3,2,1,0:T(8,128)(2,1)S(1)} %copy-done.2, f32[1,32]{1,0:T(1,128)S(1)} %bitcast.1), custom_call_target="tpu_custom_call" | custom-call | flops 100000000 | bytes 1000000 | tf_op jit(solution)/shard_map/pallas_call | solution.py:260
  7.6 0.0 collective-permute-done.4.dt_ref.db_ref
  7.7 1.1 %collective-permute-done.3.xt_ref.xb_ref = bf16[4,2,32,128]{3,2,1,0:T(8,128)(2,1)S(1)} collective-permute-done((bf16[4,2,32,128]{3,2,1,0:T(8,128)(2,1)S(1)}, bf16[4,2,32,128]{3,2,1,0:T(8,128)(2,1)S(1)}, u32[]{:S(2)}, u32[]{:S(2)}) %collective-permute-start.3) | collective-permute-done | bytes 65568 | tf_op jit(solution)/shard_map/ppermute | solution.py:24
  8.8 0.0 collective-permute-done.2.zh_ref
  8.8 0.0 copy-done.4
  8.8 2.0 %shard_map.69 = (f32[8,32,128]{2,1,0:T(8,128)S(1)}, f32[3,8,128]{2,1,0:T(8,128)S(1)}, bf16[10,32,128]{2,1,0:T(8,128)(2,1)S(1)}) custom-call(bf16[4,8,32,128]{3,2,1,0:T(8,128)(2,1)S(1)} %copy-done, bf16[4,8,32,128]{3,2,1,0:T(8,128)(2,1)S(1)} %collective-permute-done.sib_ref, bf16[2,16,32,128]{3,2,1,0:T(8,128)(2,1)S(1)} %collective-permute-done.2.zh_ref, ...), custom_call_target="tpu_custom_call" | custom-call | flops 1000000000 | bytes 2000000 | tf_op jit(solution)/shard_map/pallas_call | solution.py:260
  10.7 6.6 %collective-permute-start.5 = (bf16[10,32,128]{2,1,0:T(8,128)(2,1)S(1)}, bf16[10,32,128]{2,1,0:T(8,128)(2,1)S(1)}, u32[]{:S(2)}, u32[]{:S(2)}) collective-permute-start(bf16[10,32,128]{2,1,0:T(8,128)(2,1)S(1)} %get-tuple-element.23), channel_id=1, source_target_pairs={{0,1},{1,0},{2,3},{3,2},{4,5},{5,4},{6,7},{7,6},{8,9},{9,8},{10,11... | collective-permute-start | bytes 245768 | tf_op jit(solution)/shard_map/ppermute | solution.py:24
  17.4 0.9 %collective-permute-done.5.got_ref = bf16[10,32,128]{2,1,0:T(8,128)(2,1)S(1)} collective-permute-done((bf16[10,32,128]{2,1,0:T(8,128)(2,1)S(1)}, bf16[10,32,128]{2,1,0:T(8,128)(2,1)S(1)}, u32[]{:S(2)}, u32[]{:S(2)}) %collective-permute-start.5) | collective-permute-done | bytes 81952 | tf_op jit(solution)/shard_map/ppermute | solution.py:24
  18.4 1.6 %collective-permute-start.6 = (bf16[10,32,128]{2,1,0:T(8,128)(2,1)S(1)}, bf16[10,32,128]{2,1,0:T(8,128)(2,1)S(1)}, u32[]{:S(2)}, u32[]{:S(2)}) collective-permute-start(bf16[10,32,128]{2,1,0:T(8,128)(2,1)S(1)} %shard_map.70.own_ref), channel_id=1, source_target_pairs={{0,4},{1,5},{2,6},{3,7},{4,0},{5,1},{6,2},{7,3},{8,12},{9,13},{10,... | collective-permute-start | bytes 245768 | tf_op jit(solution)/shard_map/ppermute | solution.py:24
  20.0 3.1 %collective-permute-done.6.got_ref = bf16[10,32,128]{2,1,0:T(8,128)(2,1)S(1)} collective-permute-done((bf16[10,32,128]{2,1,0:T(8,128)(2,1)S(1)}, bf16[10,32,128]{2,1,0:T(8,128)(2,1)S(1)}, u32[]{:S(2)}, u32[]{:S(2)}) %collective-permute-start.6) | collective-permute-done | bytes 81952 | tf_op jit(solution)/shard_map/ppermute | solution.py:24
  23.2 2.7 %collective-permute-start.7 = (bf16[10,32,128]{2,1,0:T(8,128)(2,1)S(1)}, bf16[10,32,128]{2,1,0:T(8,128)(2,1)S(1)}, u32[]{:S(2)}, u32[]{:S(2)}) collective-permute-start(bf16[10,32,128]{2,1,0:T(8,128)(2,1)S(1)} %shard_map.71.own_ref), channel_id=1, source_target_pairs={{0,8},{1,9},{2,10},{3,11},{4,12},{5,13},{6,14},{7,15},{8,0},{9,1},... | collective-permute-start | bytes 245768 | tf_op jit(solution)/shard_map/ppermute | solution.py:24
  25.8 4.0 %collective-permute-done.7.got_ref = bf16[10,32,128]{2,1,0:T(8,128)(2,1)S(1)} collective-permute-done((bf16[10,32,128]{2,1,0:T(8,128)(2,1)S(1)}, bf16[10,32,128]{2,1,0:T(8,128)(2,1)S(1)}, u32[]{:S(2)}, u32[]{:S(2)}) %collective-permute-start.7) | collective-permute-done | bytes 81952 | tf_op jit(solution)/shard_map/ppermute | solution.py:24
  29.9 0.7 %shard_map.72 = (f32[8,32,128]{2,1,0:T(8,128)}, f32[8,128]{1,0:T(8,128)}) custom-call(bf16[10,32,128]{2,1,0:T(8,128)(2,1)S(1)} %shard_map.71.own_ref, bf16[10,32,128]{2,1,0:T(8,128)(2,1)S(1)} %collective-permute-done.7.got_ref), custom_call_target="tpu_custom_call" | custom-call | tf_op jit(solution)/shard_map/pallas_call | solution.py:260
  (7 shorter events, 0.2 us)
Async XLA Ops:
  0.6 1.6 %copy-start = (bf16[4,8,32,128]{3,2,1,0:T(8,128)(2,1)S(1)}, bf16[4,8,32,128]{3,2,1,0:T(8,128)(2,1)}, u32[]{:S(2)}) copy-start(bf16[4,8,32,128]{3,2,1,0:T(8,128)(2,1)} %own_ref.1) | copy-start | bytes 786436
  0.6 1.7 %collective-permute-start.1 = (f32[4,8,128]{2,1,0:T(8,128)}, f32[4,8,128]{2,1,0:T(8,128)S(1)}, u32[]{:S(2)}, u32[]{:S(2)}) collective-permute-start(f32[4,8,128]{2,1,0:T(8,128)} %op_ref.1), channel_id=1, source_target_pairs={{0,1},{1,0},{2,3},{3,2},{4,5},{5,4},{6,7},{7,6},{8,9},{9,8},{10,11... | collective-permute-start | bytes 49160 | tf_op jit(solution)/shard_map/ppermute | solution.py:24
  1.2 1.7 %collective-permute-start = (bf16[4,8,32,128]{3,2,1,0:T(8,128)(2,1)}, bf16[4,8,32,128]{3,2,1,0:T(8,128)(2,1)S(1)}, u32[]{:S(2)}, u32[]{:S(2)}) collective-permute-start(bf16[4,8,32,128]{3,2,1,0:T(8,128)(2,1)} %own_ref.1), channel_id=1, source_target_pairs={{0,1},{1,0},{2,3},{3,2},{4,5},{5,4},{6,7},{7,6},{8,9},{9,8},{10,11... | collective-permute-start | bytes 786440 | tf_op jit(solution)/shard_map/ppermute | solution.py:24
  3.0 4.3 %copy-start.2 = (bf16[3,3,3,32,32]{4,3,2,1,0:T(8,128)(2,1)S(1)}, bf16[3,3,3,32,32]{4,3,2,1,0:T(8,128)(2,1)}, u32[]{:S(2)}) copy-start(bf16[3,3,3,32,32]{4,3,2,1,0:T(8,128)(2,1)} %k2_ref.1) | copy-start | bytes 165892
  3.0 4.2 %copy-start.1 = (bf16[3,3,3,32,32]{4,3,2,1,0:T(8,128)(2,1)S(1)}, bf16[3,3,3,32,32]{4,3,2,1,0:T(8,128)(2,1)}, u32[]{:S(2)}) copy-start(bf16[3,3,3,32,32]{4,3,2,1,0:T(8,128)(2,1)} %k1_ref.1) | copy-start | bytes 165892
  3.0 5.8 %collective-permute-start.2 = (bf16[2,16,32,128]{3,2,1,0:T(8,128)(2,1)S(1)}, bf16[2,16,32,128]{3,2,1,0:T(8,128)(2,1)S(1)}, u32[]{:S(2)}, u32[]{:S(2)}) collective-permute-start(bf16[2,16,32,128]{3,2,1,0:T(8,128)(2,1)S(1)} %maximum_select_fusion), channel_id=1, source_target_pairs={{1,4},{3,6},{4,1},{5,8},{6,3},{7,10},{8,5},{9,12},{10,7},{11,14},{... | collective-permute-start | bytes 786440 | tf_op jit(solution)/shard_map/ppermute | solution.py:24
  3.9 4.9 %collective-permute-start.3 = (bf16[4,2,32,128]{3,2,1,0:T(8,128)(2,1)S(1)}, bf16[4,2,32,128]{3,2,1,0:T(8,128)(2,1)S(1)}, u32[]{:S(2)}, u32[]{:S(2)}) collective-permute-start(bf16[4,2,32,128]{3,2,1,0:T(8,128)(2,1)S(1)} %select_select_fusion), channel_id=1, source_target_pairs={{0,2},{1,3},{2,0},{3,1},{4,6},{5,7},{6,4},{7,5},{8,10},{9,11},{10,... | collective-permute-start | bytes 196616 | tf_op jit(solution)/shard_map/ppermute | solution.py:24
  6.5 0.7 %copy-start.3 = (f32[32]{0:T(128)S(1)}, f32[32]{0:T(128)}, u32[]{:S(2)}) copy-start(f32[32]{0:T(128)} %param.9) | copy-start | bytes 388
  6.6 1.1 %collective-permute-start.4 = (bf16[2,2,32,128]{3,2,1,0:T(8,128)(2,1)S(1)}, bf16[2,2,32,128]{3,2,1,0:T(8,128)(2,1)S(1)}, u32[]{:S(2)}, u32[]{:S(2)}) collective-permute-start(bf16[2,2,32,128]{3,2,1,0:T(8,128)(2,1)S(1)} %slice_select_fusion.2), channel_id=1, source_target_pairs={{1,6},{3,4},{4,3},{5,10},{6,1},{7,8},{8,7},{9,14},{10,5},{11,12},{... | collective-permute-start | bytes 98312 | tf_op jit(solution)/shard_map/ppermute | solution.py:24
  7.3 1.5 %copy-start.4 = (f32[4,8,128]{2,1,0:T(8,128)S(1)}, f32[4,8,128]{2,1,0:T(8,128)}, u32[]{:S(2)}) copy-start(f32[4,8,128]{2,1,0:T(8,128)} %op_ref.1) | copy-start | bytes 49156
  10.7 7.6 %collective-permute-start.5 = (bf16[10,32,128]{2,1,0:T(8,128)(2,1)S(1)}, bf16[10,32,128]{2,1,0:T(8,128)(2,1)S(1)}, u32[]{:S(2)}, u32[]{:S(2)}) collective-permute-start(bf16[10,32,128]{2,1,0:T(8,128)(2,1)S(1)} %get-tuple-element.23), channel_id=1, source_target_pairs={{0,1},{1,0},{2,3},{3,2},{4,5},{5,4},{6,7},{7,6},{8,9},{9,8},{10,11... | collective-permute-start | bytes 245768 | tf_op jit(solution)/shard_map/ppermute | solution.py:24
  18.4 4.8 %collective-permute-start.6 = (bf16[10,32,128]{2,1,0:T(8,128)(2,1)S(1)}, bf16[10,32,128]{2,1,0:T(8,128)(2,1)S(1)}, u32[]{:S(2)}, u32[]{:S(2)}) collective-permute-start(bf16[10,32,128]{2,1,0:T(8,128)(2,1)S(1)} %shard_map.70.own_ref), channel_id=1, source_target_pairs={{0,4},{1,5},{2,6},{3,7},{4,0},{5,1},{6,2},{7,3},{8,12},{9,13},{10,... | collective-permute-start | bytes 245768 | tf_op jit(solution)/shard_map/ppermute | solution.py:24
  23.2 6.7 %collective-permute-start.7 = (bf16[10,32,128]{2,1,0:T(8,128)(2,1)S(1)}, bf16[10,32,128]{2,1,0:T(8,128)(2,1)S(1)}, u32[]{:S(2)}, u32[]{:S(2)}) collective-permute-start(bf16[10,32,128]{2,1,0:T(8,128)(2,1)S(1)} %shard_map.71.own_ref), channel_id=1, source_target_pairs={{0,8},{1,9},{2,10},{3,11},{4,12},{5,13},{6,14},{7,15},{8,0},{9,1},... | collective-permute-start | bytes 245768 | tf_op jit(solution)/shard_map/ppermute | solution.py:24

commit v3 on v2

--- a/solution.py
+++ b/solution.py
@@ -6,6 +6,7 @@
 from jax.experimental import pallas as pl
 from jax.experimental.pallas import tpu as pltpu
 from jax.sharding import PartitionSpec as P
+
 
 F32 = jnp.float32
 BF16 = jnp.bfloat16
@@ -45,6 +46,15 @@
     pb_ref[...] = jnp.broadcast_to(proj_ref[...], (lanes, chans)).T
 
 
+def cut_kernel(block_ref, pick_ref, high_ref, low_ref):
+    half, halo = pick_ref.shape[0], high_ref.shape[1]
+    rows = block_ref.shape[1]
+    core = lax.axis_index("rows") % 2
+    pick_ref[...] = block_ref[pl.ds(core * half, half)]
+    high_ref[...] = block_ref[:, :halo]
+    low_ref[...] = block_ref[:, rows - halo :]
+
+
 def shifted_sum(y, group):
     width = y.shape[1] // 2
     lane = lax.broadcasted_iota(jnp.int32, (1, width), 1)
@@ -95,41 +105,70 @@
     return -(-7 // per)
 
 
-def volume_kernel(
-    shape, own_ref, sib_ref, zh_ref, xt_ref, xb_ref, dt_ref, db_ref, op_ref, sp_ref, w1_ref,
-    w2_ref, pb_ref, keep_ref, stat_ref, send_ref, xs_ref, fs_ref, ps_ref, ss_ref,
+def first_layer(w, x, half, chans, first_plane, g, all_planes, store):
+    lo, hi = shifted_sum(jnp.dot(w, x, preferred_element_type=F32), half * chans)
+    for p in range(half):
+        part = slice(p * chans, (p + 1) * chans)
+        a, b = jnp.maximum(lo[part], 0.0), jnp.maximum(hi[part], 0.0)
+        if g + p == 0 or g + p == half + 1:
+            plane = first_plane + g + p
+            outside = jnp.logical_or(plane < 0, plane >= all_planes)
+            a = jnp.where(outside, 0.0, a)
+            b = jnp.where(outside, 0.0, b)
+        store(g + p, a, b)
+
+
+def second_layer(w, x, pb, prior_row, fracs, half, chans):
+    y = jnp.dot(w, x, preferred_element_type=F32)
+    sides = []
+    for s, side in enumerate(shifted_sum(y, half * chans)):
+        side = jnp.maximum(side, 0.0).astype(BF16).astype(F32)
+        feats = [side[p * chans : (p + 1) * chans] for p in range(half)]
+        scores = [
+            jnp.sum(feats[p] * pb, axis=0, keepdims=True) + prior_row(p, s) for p in range(half)
+        ]
+        peak = functools.reduce(jnp.maximum, scores)
+        weights = [jnp.exp(s_ - peak) for s_ in scores]
+        total = functools.reduce(jnp.add, weights)
+        depth_sum = functools.reduce(jnp.add, [w_ * f for w_, f in zip(weights, fracs)])
+        feat = functools.reduce(jnp.add, [w_ * f for w_, f in zip(weights, feats)])
+        sides.append((feat, peak, total, depth_sum))
+    return sides
+
+
+def place_of(depth, planes):
+    half = planes // 2
+    core = lax.axis_index("rows") % 2
+    first_plane = lax.axis_index("depth") * planes + core * half - 1
+    all_planes = depth * planes
+    fracs = [((first_plane + 1 + p).astype(F32) + 0.5) / all_planes for p in range(half)]
+    return core, first_plane, all_planes, fracs
+
+
+def inner_kernel(
+    depth, own_ref, sib_ref, zh_ref, op_ref, sp_ref, w1_ref, w2_ref, pb_ref,
+    xs_ref, fs_ref, ps_ref, keep_ref, send_ref, stat_ref, ss_ref,
 ):
-    depth, rows_axis = shape
     planes, rows, chans, width = own_ref.shape
     half = planes // 2
     halo = 2
     wide = 2 * width
-    d = lax.axis_index("depth")
-    r = lax.axis_index("rows")
-    core = r % 2
-    col = r // 2
-    at_top = col == 0
-    at_bottom = col == rows_axis // 2 - 1
+    core, first_plane, all_planes, fracs = place_of(depth, planes)
     left = slice(0, width)
     right = slice(width, wide)
-    zero_rows = jnp.zeros((planes, halo, chans, width), BF16)
+    n = rows + halo
 
     def fill(c):
         blocks = (own_ref, sib_ref) if c == 0 else (sib_ref, own_ref)
         base = halo * (1 - c)
         mine = slice(base, base + planes)
         zs = slice(0, halo) if c == 0 else slice(planes, planes + halo)
-        n = rows + halo
         xs_ref[mine, halo:n, :, left] = blocks[0][...]
         xs_ref[mine, n:, :, left] = blocks[1][:, :halo]
         xs_ref[mine, :halo, :, right] = blocks[0][:, rows - halo :]
         xs_ref[mine, halo:n, :, right] = blocks[1][...]
-        xs_ref[mine, :halo, :, left] = jnp.where(at_top, zero_rows, xt_ref[...])
-        xs_ref[mine, n:, :, right] = jnp.where(at_bottom, zero_rows, xb_ref[...])
         xs_ref[zs, halo:, :, left] = zh_ref[:, :n]
         xs_ref[zs, :n, :, right] = zh_ref[:, rows - halo :]
-        xs_ref[zs, :halo, :, left] = jnp.where(at_top, zero_rows[:halo], dt_ref[...])
-        xs_ref[zs, n:, :, right] = jnp.where(at_bottom, zero_rows[:halo], db_ref[...])
         mine_p = slice(half * c, half * c + half)
         ps_ref[:, :, left] = (op_ref if c == 0 else sp_ref)[mine_p]
         ps_ref[:, :, right] = (sp_ref if c == 0 else op_ref)[mine_p]
@@ -137,57 +176,103 @@
     for c in range(2):
         pl.when(core == c)(functools.partial(fill, c))
 
-    group = half * chans
-    first_plane = d * planes + core * half - 1
-    all_planes = depth * planes
+    deep = (half + 2) * 3 * chans
     w1 = w1_ref[...]
     for g in range(0, half + 2, half):
-        for i in range(rows + 2):
-            x = xs_ref[g : g + half + 2, i : i + 3].reshape((half + 2) * 3 * chans, wide)
-            y = jnp.dot(w1, x, preferred_element_type=F32)
-            lo, hi = shifted_sum(y, group)
-            lo = jnp.maximum(lo, 0.0)
-            hi = jnp.maximum(hi, 0.0)
-            if i == 0:
-                lo = jnp.where(at_top, 0.0, lo)
-            if i == rows + 1:
-                hi = jnp.where(at_bottom, 0.0, hi)
-            for p in range(half):
-                part = slice(p * chans, (p + 1) * chans)
-                a, b = lo[part], hi[part]
-                if g + p == 0 or g + p == half + 1:
-                    plane = first_plane + g + p
-                    outside = jnp.logical_or(plane < 0, plane >= all_planes)
-                    a = jnp.where(outside, 0.0, a)
-                    b = jnp.where(outside, 0.0, b)
-                fs_ref[g + p, i, :, left] = a.astype(BF16)
-                fs_ref[g + p, i, :, right] = b.astype(BF16)
+        for i in range(halo, rows):
+            def store(j, a, b, i=i):
+                fs_ref[j, i - halo, :, left] = a.astype(BF16)
+                fs_ref[j, i - halo, :, right] = b.astype(BF16)
+
+            x = xs_ref[g : g + half + 2, i : i + 3].reshape(deep, wide)
+            first_layer(w1, x, half, chans, first_plane, g, all_planes, store)
 
     w2 = w2_ref[...]
     pb = pb_ref[...]
     kept = core == 0
-    fracs = [
-        ((first_plane + 1 + p).astype(F32) + 0.5) / all_planes for p in range(half)
-    ]
-    for i in range(rows):
-        x = fs_ref[:, i : i + 3].reshape((half + 2) * 3 * chans, wide)
-        y = jnp.dot(w2, x, preferred_element_type=F32)
-        sides = []
-        for s, side in enumerate(shifted_sum(y, group)):
-            cols = left if s == 0 else right
-            side = jnp.maximum(side, 0.0).astype(BF16).astype(F32)
-            feats = [side[p * chans : (p + 1) * chans] for p in range(half)]
-            scores = [
-                jnp.sum(feats[p] * pb, axis=0, keepdims=True) + ps_ref[p, i : i + 1, cols]
-                for p in range(half)
-            ]
-            peak = functools.reduce(jnp.maximum, scores)
-            weights = [jnp.exp(s_ - peak) for s_ in scores]
-            total = functools.reduce(jnp.add, weights)
-            depth_sum = functools.reduce(jnp.add, [w * f for w, f in zip(weights, fracs)])
-            feat = functools.reduce(jnp.add, [w * f for w, f in zip(weights, feats)])
-            sides.append((feat, peak, total, depth_sum))
-        lo, hi = sides
+    for i in range(halo, rows - halo):
+        x = fs_ref[:, i - halo : i - halo + 3].reshape(deep, wide)
+        prior_row = lambda p, s: ps_ref[p, i : i + 1, right if s else left]
+        lo, hi = second_layer(w2, x, pb, prior_row, fracs, half, chans)
+        keep_ref[i - halo] = jnp.where(kept, lo[0], hi[0])
+        send_ref[i - halo] = jnp.where(kept, hi[0], lo[0]).astype(BF16)
+        for k in range(3):
+            stat_ref[k, i : i + 1, :] = jnp.where(kept, lo[k + 1], hi[k + 1])
+            ss_ref[k, i : i + 1, :] = jnp.where(kept, hi[k + 1], lo[k + 1])
+
+
+def outer_kernel(
+    shape, xt_ref, xb_ref, dt_ref, db_ref, xs_ref, fi_ref, ps_ref, ki_ref, si_ref, ti_ref, ui_ref,
+    w1_ref, w2_ref, pb_ref, keep_ref, stat_ref, send_ref, top_ref, bottom_ref, fs_ref, ss_ref,
+):
+    depth, rows_axis = shape
+    planes, halo, chans, width = xt_ref.shape
+    half = planes // 2
+    rows = keep_ref.shape[0]
+    core, first_plane, all_planes, fracs = place_of(depth, planes)
+    col = lax.axis_index("rows") // 2
+    at_top = col == 0
+    at_bottom = col == rows_axis // 2 - 1
+    left = slice(0, width)
+    right = slice(width, 2 * width)
+    zero_rows = jnp.zeros((planes, halo, chans, width), BF16)
+
+    def fill(c):
+        base = halo * (1 - c)
+        mine = slice(base, base + planes)
+        zs = slice(0, halo) if c == 0 else slice(planes, planes + halo)
+        top_ref[mine] = jnp.where(at_top, zero_rows, xt_ref[...])
+        bottom_ref[mine] = jnp.where(at_bottom, zero_rows, xb_ref[...])
+        top_ref[zs] = jnp.where(at_top, zero_rows[:halo], dt_ref[...])
+        bottom_ref[zs] = jnp.where(at_bottom, zero_rows[:halo], db_ref[...])
+
+    for c in range(2):
+        pl.when(core == c)(functools.partial(fill, c))
+
+    deep = (half + 2) * 3 * chans
+    last = rows + 2
+    w1 = w1_ref[...]
+    for g in range(0, half + 2, half):
+        span = slice(g, g + half + 2)
+        for i in (0, 1, rows, rows + 1):
+            if i < halo:
+                lhs = jnp.concatenate(
+                    [top_ref[span, i:], xs_ref[span, halo : i + 3, :, left]], axis=1
+                )
+                rhs = xs_ref[span, i : i + 3, :, right]
+            else:
+                lhs = xs_ref[span, i : i + 3, :, left]
+                rhs = jnp.concatenate(
+                    [xs_ref[span, i:last, :, right], bottom_ref[span, : i + 3 - last]], axis=1
+                )
+            x = jnp.concatenate([lhs.reshape(deep, width), rhs.reshape(deep, width)], axis=1)
+
+            def store(j, a, b, i=i):
+                if i == 0:
+                    a = jnp.where(at_top, 0.0, a)
+                if i == rows + 1:
+                    b = jnp.where(at_bottom, 0.0, b)
+                at = i if i < halo else i - rows + halo
+                fs_ref[j, at, :, left] = a.astype(BF16)
+                fs_ref[j, at, :, right] = b.astype(BF16)
+
+            first_layer(w1, x, half, chans, first_plane, g, all_planes, store)
+
+    w2 = w2_ref[...]
+    pb = pb_ref[...]
+    kept = core == 0
+    inner = slice(halo, rows - halo)
+    keep_ref[inner] = ki_ref[...]
+    send_ref[inner] = si_ref[...]
+    stat_ref[:, inner] = ti_ref[:, inner]
+    ss_ref[:, inner] = ui_ref[:, inner]
+    for i in (0, 1, rows - 2, rows - 1):
+        if i < halo:
+            x = jnp.concatenate([fs_ref[:, i:halo], fi_ref[:, : i + 3 - halo]], axis=1)
+        else:
+            x = jnp.concatenate([fi_ref[:, i - halo :], fs_ref[:, halo : i + 3 - rows + halo]], axis=1)
+        prior_row = lambda p, s: ps_ref[p, i : i + 1, right if s else left]
+        lo, hi = second_layer(w2, x.reshape(deep, 2 * width), pb, prior_row, fracs, half, chans)
         keep_ref[i] = jnp.where(kept, lo[0], hi[0])
         send_ref[i] = jnp.where(kept, hi[0], lo[0]).astype(BF16)
         for k in range(3):
@@ -224,7 +309,6 @@
 
 
 def merge_kernel(step, own_ref, got_ref, out_ref):
-    chans = own_ref.shape[1]
     rows = stat_ref_rows(own_ref.shape)
     low = (lax.axis_index("depth") // step) % 2 == 0
 
@@ -268,7 +352,7 @@
     )(*args)
 
 
-def per_device(volume, prior, first_kernel, second_kernel, projection):
+def body(volume, prior, first_kernel, second_kernel, projection):
     planes, rows, chans, width = volume.shape
     depth, rows_axis = lax.axis_size("depth"), lax.axis_size("rows")
     shape = (depth, rows_axis)
@@ -303,7 +387,12 @@
         picked = jnp.where(lower, block[:half], block[half:])
         return picked, block[:, high], block[:, low]
 
-    own_pick, own_high, own_low = lax.optimization_barrier(parts(volume))
+    edge_shape = (planes, halo, chans, width)
+    own_pick, own_high, own_low = call(
+        cut_kernel,
+        [((half, rows, chans, width), BF16), (edge_shape, BF16), (edge_shape, BF16)],
+        volume,
+    )
     sib_pick, sib_high, sib_low = parts(beside)
     edge = jnp.where(
         lower,
@@ -329,17 +418,33 @@
         db = move(corners[1], lambda d, r: (up(d, r)[0], (r ^ 1) - 2))
 
     parcel_shape = (rows + stat_blocks(rows, chans), chans, width)
+    between = rows - 2 * halo
+    stats_shape = (3, rows, width)
+    inside = call(
+        functools.partial(inner_kernel, depth),
+        [
+            ((planes + halo, rows + 2 * halo, chans, 2 * width), BF16),
+            ((half + 2, rows - halo, chans, 2 * width), BF16),
+            ((half, rows, 2 * width), F32),
+            ((between, chans, width), F32),
+            ((between, chans, width), BF16),
+            (stats_shape, F32),
+            (stats_shape, F32),
+        ],
+        volume, beside, zh, prior, prior_beside, w1, w2, pb,
+        flops=5 * 10**8, nbytes=10**6, room=6,
+    )
     keep, stat, send = call(
-        functools.partial(volume_kernel, shape),
-        [((rows, chans, width), F32), ((3, rows, width), F32), (parcel_shape, BF16)],
-        volume, beside, zh, xt, xb, dt, db, prior, prior_beside, w1, w2, pb,
+        functools.partial(outer_kernel, shape),
+        [((rows, chans, width), F32), (stats_shape, F32), (parcel_shape, BF16)],
+        xt, xb, dt, db, *inside, w1, w2, pb,
         scratch=[
-            pltpu.VMEM((planes + halo, rows + 2 * halo, chans, 2 * width), BF16),
-            pltpu.VMEM((half + 2, rows + 2, chans, 2 * width), BF16),
-            pltpu.VMEM((half, rows, 2 * width), F32),
-            pltpu.VMEM((3, rows, width), F32),
+            pltpu.VMEM((planes + halo, halo, chans, width), BF16),
+            pltpu.VMEM((planes + halo, halo, chans, width), BF16),
+            pltpu.VMEM((half + 2, 2 * halo, chans, 2 * width), BF16),
+            pltpu.VMEM(stats_shape, F32),
         ],
-        flops=10**9, nbytes=2 * 10**6, room=12,
+        flops=5 * 10**8, nbytes=10**6, room=6,
     )
     got = move(send, lambda d, r: (d, r ^ 1))
     (sums,) = call(first_merge_kernel, [(parcel_shape, BF16)], keep, stat, got)
@@ -367,7 +472,7 @@
         P(),
     )
     return jax.shard_map(
-        per_device,
+        body,
         mesh=mesh,
         in_specs=placed,
         out_specs=(P(("tiles", "rows"), None, None), P(("tiles", "rows"), None)),

time: 30.7 us -> 32.3 us (1.052)
  local copies, waits for them, and re-layouts: 0.04 us -> 3.51 us
  waiting for transfers between devices: 9.85 us -> 8.2 us
  other arithmetic: 1.05 us -> 0.07 us
  Pallas kernels: 3.12 us -> 3.71 us
    unnamed x10 -> x12, local copies, waits for them, and re-layouts: 0.03 us -> 3.51 us
    ppermute x8, waiting for transfers between devices: 9.85 us -> 8.2 us  [exchange(): return lax.ppermute(value, AXES, pairs)]
    select_n x2 -> x1, other arithmetic: 1 us -> 0.02 us  [parts(): picked = jnp.where(lower, block[:half], block[half:])]
    pallas_call x5 -> x7, Pallas kernels: 3.12 us -> 3.71 us  [call(): pl.pallas_call(kernel, out_shape=[jax.ShapeDtypeStruct(s, t) for s, t in...]
  transfers between devices with their start and end apart: 8 -> 8, of which waited for: 5 -> 4; matrix products, arithmetic and copies ran while one was open for 3% -> 0% of each run, Pallas kernels for 1% -> 6%
where the time goes in v3:
time: 32.3 us; the launch traced here: 32.1 us
  starting transfers between devices  15.8 us (49%)
  waiting for transfers between devices  8.2 us (25%)
  Pallas kernels  3.71 us (11%)
  local copies, waits for them, and re-layouts  3.51 us (11%)
  between operations  0.79 us (2%)
    ppermute x8, starting transfers between devices, exchange(): return lax.ppermute(value, AXES, pairs)  15.8 us
    ppermute x8, waiting for transfers between devices, exchange(): return lax.ppermute(value, AXES, pairs)  8.2 us
    pallas_call x7, Pallas kernels, call(): pl.pallas_call(kernel, out_shape=[jax.ShapeDtypeStruct(s, t) for s, t in...  3.71 us
    unnamed x12, local copies, waits for them, and re-layouts  3.51 us
  transfers between devices with their start and end apart: 8, of which 4 were waited for; matrix products, arithmetic and copies ran while one was open for 0% of the time, Pallas kernels for 6%

profile of v3, /device:TPU:0, one launch (start us, length us, event | category | flops | bytes accessed | tf_op | source)
XLA Modules:
  0.0 32.1 jit_solution(909727563861224419)
XLA Ops:
  0.6 0.0 copy-start.5
  0.6 0.6 %collective-permute-start = (bf16[4,8,32,128]{3,2,1,0:T(8,128)(2,1)}, bf16[4,8,32,128]{3,2,1,0:T(8,128)(2,1)S(1)}, u32[]{:S(2)}, u32[]{:S(2)}) collective-permute-start(bf16[4,8,32,128]{3,2,1,0:T(8,128)(2,1)} %own_ref.1), channel_id=1, source_target_pairs={{0,1},{1,0},{2,3},{3,2},{4,5},{5,4},{6,7},{7,6},{8,9},{9,8},{10,11... | collective-permute-start | bytes 786440 | tf_op jit(solution)/shard_map/ppermute | solution.py:25
  1.2 0.1 collective-permute-start.1
  1.3 0.0 copy-start
  1.3 0.9 %copy-done = bf16[4,8,32,128]{3,2,1,0:T(8,128)(2,1)S(1)} copy-done((bf16[4,8,32,128]{3,2,1,0:T(8,128)(2,1)S(1)}, bf16[4,8,32,128]{3,2,1,0:T(8,128)(2,1)}, u32[]{:S(2)}) %copy-start) | copy-done | bytes 262168
  2.2 0.0 copy-start.1
  2.3 0.0 copy-start.2
  2.3 1.0 %copy-done.2 = bf16[3,3,3,32,32]{4,3,2,1,0:T(8,128)(2,1)S(1)} copy-done((bf16[3,3,3,32,32]{4,3,2,1,0:T(8,128)(2,1)S(1)}, bf16[3,3,3,32,32]{4,3,2,1,0:T(8,128)(2,1)}, u32[]{:S(2)}) %copy-start.2) | copy-done | bytes 55320
  3.3 0.0 copy-start.3
  3.3 0.9 %copy-done.3 = bf16[3,3,3,32,32]{4,3,2,1,0:T(8,128)(2,1)S(1)} copy-done((bf16[3,3,3,32,32]{4,3,2,1,0:T(8,128)(2,1)S(1)}, bf16[3,3,3,32,32]{4,3,2,1,0:T(8,128)(2,1)}, u32[]{:S(2)}) %copy-start.3) | copy-done | bytes 55320
  4.2 0.0 copy-start.4
  4.2 0.7 %copy-done.4 = f32[32]{0:T(128)S(1)} copy-done((f32[32]{0:T(128)S(1)}, f32[32]{0:T(128)}, u32[]{:S(2)}) %copy-start.4) | copy-done | bytes 152
  4.8 0.4 %shard_map.69 = (bf16[192,384]{1,0:T(8,128)(2,1)S(1)}, bf16[192,384]{1,0:T(8,128)(2,1)S(1)}, f32[32,128]{1,0:T(8,128)S(1)}) custom-call(bf16[3,3,3,32,32]{4,3,2,1,0:T(8,128)(2,1)S(1)} %copy-done.2, bf16[3,3,3,32,32]{4,3,2,1,0:T(8,128)(2,1)S(1)} %copy-done.3, f32[1,32]{1,0:T(1,128)S(1)} %bitcast.1), custom_call_target="tpu_custom_call" | custom-call | flops 100000000 | bytes 1000000 | tf_op jit(solution)/shard_map/pallas_call | solution.py:344
  5.2 0.0 collective-permute-done.1.sp_ref
  5.2 0.0 collective-permute-done.sib_ref
  5.3 0.7 %collective-permute-start.4 = (bf16[2,16,32,128]{3,2,1,0:T(8,128)(2,1)S(1)}, bf16[2,16,32,128]{3,2,1,0:T(8,128)(2,1)S(1)}, u32[]{:S(2)}, u32[]{:S(2)}) collective-permute-start(bf16[2,16,32,128]{3,2,1,0:T(8,128)(2,1)S(1)} %maximum_select_fusion), channel_id=1, source_target_pairs={{1,4},{3,6},{4,1},{5,8},{6,3},{7,10},{8,5},{9,12},{10,7},{11,14},{... | collective-permute-start | bytes 786440 | tf_op jit(solution)/shard_map/ppermute | solution.py:25
  6.0 3.0 %collective-permute-start.2 = (bf16[4,2,32,128]{3,2,1,0:T(8,128)(2,1)S(1)}, bf16[4,2,32,128]{3,2,1,0:T(8,128)(2,1)S(1)}, u32[]{:S(2)}, u32[]{:S(2)}) collective-permute-start(bf16[4,2,32,128]{3,2,1,0:T(8,128)(2,1)S(1)} %select_select_fusion), channel_id=1, source_target_pairs={{0,2},{1,3},{2,0},{3,1},{4,6},{5,7},{6,4},{7,5},{8,10},{9,11},{10,... | collective-permute-start | bytes 196616 | tf_op jit(solution)/shard_map/ppermute | solution.py:25
  9.0 0.7 %collective-permute-start.3 = (bf16[2,2,32,128]{3,2,1,0:T(8,128)(2,1)S(1)}, bf16[2,2,32,128]{3,2,1,0:T(8,128)(2,1)S(1)}, u32[]{:S(2)}, u32[]{:S(2)}) collective-permute-start(bf16[2,2,32,128]{3,2,1,0:T(8,128)(2,1)S(1)} %slice_select_fusion.1), channel_id=1, source_target_pairs={{1,6},{3,4},{4,3},{5,10},{6,1},{7,8},{8,7},{9,14},{10,5},{11,12},{... | collective-permute-start | bytes 98312 | tf_op jit(solution)/shard_map/ppermute | solution.py:25
  9.6 0.0 collective-permute-done.4.zh_ref
  9.7 0.0 copy-done.5
  9.7 0.0 copy-done.1
  9.7 1.4 %shard_map.70 = (bf16[6,12,32,256]{3,2,1,0:T(8,128)(2,1)S(1)}, bf16[4,6,32,256]{3,2,1,0:T(8,128)(2,1)S(1)}, f32[2,8,256]{2,1,0:T(8,128)S(1)}, f32[4,32,128]{2,1,...) custom-call(bf16[4,8,32,128]{3,2,1,0:T(8,128)(2,1)S(1)} %copy-done.1, ...), custom_call_target="tpu_custom_call" | custom-call | flops 500000000 | bytes 1000000 | tf_op jit(solution)/shard_map/pallas_call | solution.py:344
  11.1 0.0 collective-permute-done.3.dt_ref.db_ref
  11.1 0.1 collective-permute-done.2.xt_ref.xb_ref
  11.2 1.1 %shard_map.71 = (f32[8,32,128]{2,1,0:T(8,128)S(1)}, f32[3,8,128]{2,1,0:T(8,128)S(1)}, bf16[10,32,128]{2,1,0:T(8,128)(2,1)S(1)}) custom-call(bf16[4,2,32,128]{3,2,1,0:T(8,128)(2,1)S(1)} %collective-permute-done.2.xt_ref.xb_ref, bf16[4,2,32,128]{3,2,1,0:T(8,128)(2,1)S(1)} %collective-permute-done.2.xt_ref.xb_ref, ...), custom_call_target="tpu_custom_call" | custom-call | flops 500000000 | bytes 1000000 | tf_op jit(solution)/shard_map/pallas_call | solution.py:344
  12.3 6.6 %collective-permute-start.5 = (bf16[10,32,128]{2,1,0:T(8,128)(2,1)S(1)}, bf16[10,32,128]{2,1,0:T(8,128)(2,1)S(1)}, u32[]{:S(2)}, u32[]{:S(2)}) collective-permute-start(bf16[10,32,128]{2,1,0:T(8,128)(2,1)S(1)} %get-tuple-element.37), channel_id=1, source_target_pairs={{0,1},{1,0},{2,3},{3,2},{4,5},{5,4},{6,7},{7,6},{8,9},{9,8},{10,11... | collective-permute-start | bytes 245768 | tf_op jit(solution)/shard_map/ppermute | solution.py:25
  18.9 0.9 %collective-permute-done.5.got_ref = bf16[10,32,128]{2,1,0:T(8,128)(2,1)S(1)} collective-permute-done((bf16[10,32,128]{2,1,0:T(8,128)(2,1)S(1)}, bf16[10,32,128]{2,1,0:T(8,128)(2,1)S(1)}, u32[]{:S(2)}, u32[]{:S(2)}) %collective-permute-start.5) | collective-permute-done | bytes 81952 | tf_op jit(solution)/shard_map/ppermute | solution.py:25
  19.9 1.6 %collective-permute-start.6 = (bf16[10,32,128]{2,1,0:T(8,128)(2,1)S(1)}, bf16[10,32,128]{2,1,0:T(8,128)(2,1)S(1)}, u32[]{:S(2)}, u32[]{:S(2)}) collective-permute-start(bf16[10,32,128]{2,1,0:T(8,128)(2,1)S(1)} %shard_map.72.own_ref), channel_id=1, source_target_pairs={{0,4},{1,5},{2,6},{3,7},{4,0},{5,1},{6,2},{7,3},{8,12},{9,13},{10,... | collective-permute-start | bytes 245768 | tf_op jit(solution)/shard_map/ppermute | solution.py:25
  21.5 3.1 %collective-permute-done.6.got_ref = bf16[10,32,128]{2,1,0:T(8,128)(2,1)S(1)} collective-permute-done((bf16[10,32,128]{2,1,0:T(8,128)(2,1)S(1)}, bf16[10,32,128]{2,1,0:T(8,128)(2,1)S(1)}, u32[]{:S(2)}, u32[]{:S(2)}) %collective-permute-start.6) | collective-permute-done | bytes 81952 | tf_op jit(solution)/shard_map/ppermute | solution.py:25
  24.7 2.7 %collective-permute-start.7 = (bf16[10,32,128]{2,1,0:T(8,128)(2,1)S(1)}, bf16[10,32,128]{2,1,0:T(8,128)(2,1)S(1)}, u32[]{:S(2)}, u32[]{:S(2)}) collective-permute-start(bf16[10,32,128]{2,1,0:T(8,128)(2,1)S(1)} %shard_map.73.own_ref), channel_id=1, source_target_pairs={{0,8},{1,9},{2,10},{3,11},{4,12},{5,13},{6,14},{7,15},{8,0},{9,1},... | collective-permute-start | bytes 245768 | tf_op jit(solution)/shard_map/ppermute | solution.py:25
  27.4 4.0 %collective-permute-done.7.got_ref = bf16[10,32,128]{2,1,0:T(8,128)(2,1)S(1)} collective-permute-done((bf16[10,32,128]{2,1,0:T(8,128)(2,1)S(1)}, bf16[10,32,128]{2,1,0:T(8,128)(2,1)S(1)}, u32[]{:S(2)}, u32[]{:S(2)}) %collective-permute-start.7) | collective-permute-done | bytes 81952 | tf_op jit(solution)/shard_map/ppermute | solution.py:25
  31.4 0.7 %shard_map.74 = (f32[8,32,128]{2,1,0:T(8,128)}, f32[8,128]{1,0:T(8,128)}) custom-call(bf16[10,32,128]{2,1,0:T(8,128)(2,1)S(1)} %shard_map.73.own_ref, bf16[10,32,128]{2,1,0:T(8,128)(2,1)S(1)} %collective-permute-done.7.got_ref), custom_call_target="tpu_custom_call" | custom-call | tf_op jit(solution)/shard_map/pallas_call | solution.py:344
  (7 shorter events, 0.2 us)
Async XLA Ops:
  0.6 9.0 %copy-start.5 = (f32[4,8,128]{2,1,0:T(8,128)S(1)}, f32[4,8,128]{2,1,0:T(8,128)}, u32[]{:S(2)}) copy-start(f32[4,8,128]{2,1,0:T(8,128)} %op_ref.1) | copy-start | bytes 49156
  0.6 4.6 %collective-permute-start = (bf16[4,8,32,128]{3,2,1,0:T(8,128)(2,1)}, bf16[4,8,32,128]{3,2,1,0:T(8,128)(2,1)S(1)}, u32[]{:S(2)}, u32[]{:S(2)}) collective-permute-start(bf16[4,8,32,128]{3,2,1,0:T(8,128)(2,1)} %own_ref.1), channel_id=1, source_target_pairs={{0,1},{1,0},{2,3},{3,2},{4,5},{5,4},{6,7},{7,6},{8,9},{9,8},{10,11... | collective-permute-start | bytes 786440 | tf_op jit(solution)/shard_map/ppermute | solution.py:25
  1.2 4.0 %collective-permute-start.1 = (f32[4,8,128]{2,1,0:T(8,128)}, f32[4,8,128]{2,1,0:T(8,128)S(1)}, u32[]{:S(2)}, u32[]{:S(2)}) collective-permute-start(f32[4,8,128]{2,1,0:T(8,128)} %op_ref.1), channel_id=1, source_target_pairs={{0,1},{1,0},{2,3},{3,2},{4,5},{5,4},{6,7},{7,6},{8,9},{9,8},{10,11... | collective-permute-start | bytes 49160 | tf_op jit(solution)/shard_map/ppermute | solution.py:25
  1.3 0.9 %copy-start = (bf16[4,8,32,128]{3,2,1,0:T(8,128)(2,1)S(1)}, bf16[4,8,32,128]{3,2,1,0:T(8,128)(2,1)}, u32[]{:S(2)}) copy-start(bf16[4,8,32,128]{3,2,1,0:T(8,128)(2,1)} %own_ref.1) | copy-start | bytes 786436
  2.2 7.4 %copy-start.1 = (bf16[4,8,32,128]{3,2,1,0:T(8,128)(2,1)S(1)}, bf16[4,8,32,128]{3,2,1,0:T(8,128)(2,1)}, u32[]{:S(2)}) copy-start(bf16[4,8,32,128]{3,2,1,0:T(8,128)(2,1)} %own_ref.1) | copy-start | bytes 786436
  2.3 1.0 %copy-start.2 = (bf16[3,3,3,32,32]{4,3,2,1,0:T(8,128)(2,1)S(1)}, bf16[3,3,3,32,32]{4,3,2,1,0:T(8,128)(2,1)}, u32[]{:S(2)}) copy-start(bf16[3,3,3,32,32]{4,3,2,1,0:T(8,128)(2,1)} %k1_ref.1) | copy-start | bytes 165892
  3.3 0.9 %copy-start.3 = (bf16[3,3,3,32,32]{4,3,2,1,0:T(8,128)(2,1)S(1)}, bf16[3,3,3,32,32]{4,3,2,1,0:T(8,128)(2,1)}, u32[]{:S(2)}) copy-start(bf16[3,3,3,32,32]{4,3,2,1,0:T(8,128)(2,1)} %k2_ref.1) | copy-start | bytes 165892
  4.2 0.7 %copy-start.4 = (f32[32]{0:T(128)S(1)}, f32[32]{0:T(128)}, u32[]{:S(2)}) copy-start(f32[32]{0:T(128)} %param.9) | copy-start | bytes 388
  5.3 4.4 %collective-permute-start.4 = (bf16[2,16,32,128]{3,2,1,0:T(8,128)(2,1)S(1)}, bf16[2,16,32,128]{3,2,1,0:T(8,128)(2,1)S(1)}, u32[]{:S(2)}, u32[]{:S(2)}) collective-permute-start(bf16[2,16,32,128]{3,2,1,0:T(8,128)(2,1)S(1)} %maximum_select_fusion), channel_id=1, source_target_pairs={{1,4},{3,6},{4,1},{5,8},{6,3},{7,10},{8,5},{9,12},{10,7},{11,14},{... | collective-permute-start | bytes 786440 | tf_op jit(solution)/shard_map/ppermute | solution.py:25
  6.0 5.2 %collective-permute-start.2 = (bf16[4,2,32,128]{3,2,1,0:T(8,128)(2,1)S(1)}, bf16[4,2,32,128]{3,2,1,0:T(8,128)(2,1)S(1)}, u32[]{:S(2)}, u32[]{:S(2)}) collective-permute-start(bf16[4,2,32,128]{3,2,1,0:T(8,128)(2,1)S(1)} %select_select_fusion), channel_id=1, source_target_pairs={{0,2},{1,3},{2,0},{3,1},{4,6},{5,7},{6,4},{7,5},{8,10},{9,11},{10,... | collective-permute-start | bytes 196616 | tf_op jit(solution)/shard_map/ppermute | solution.py:25
  9.0 2.1 %collective-permute-start.3 = (bf16[2,2,32,128]{3,2,1,0:T(8,128)(2,1)S(1)}, bf16[2,2,32,128]{3,2,1,0:T(8,128)(2,1)S(1)}, u32[]{:S(2)}, u32[]{:S(2)}) collective-permute-start(bf16[2,2,32,128]{3,2,1,0:T(8,128)(2,1)S(1)} %slice_select_fusion.1), channel_id=1, source_target_pairs={{1,6},{3,4},{4,3},{5,10},{6,1},{7,8},{8,7},{9,14},{10,5},{11,12},{... | collective-permute-start | bytes 98312 | tf_op jit(solution)/shard_map/ppermute | solution.py:25
  12.3 7.5 %collective-permute-start.5 = (bf16[10,32,128]{2,1,0:T(8,128)(2,1)S(1)}, bf16[10,32,128]{2,1,0:T(8,128)(2,1)S(1)}, u32[]{:S(2)}, u32[]{:S(2)}) collective-permute-start(bf16[10,32,128]{2,1,0:T(8,128)(2,1)S(1)} %get-tuple-element.37), channel_id=1, source_target_pairs={{0,1},{1,0},{2,3},{3,2},{4,5},{5,4},{6,7},{7,6},{8,9},{9,8},{10,11... | collective-permute-start | bytes 245768 | tf_op jit(solution)/shard_map/ppermute | solution.py:25
  19.9 4.8 %collective-permute-start.6 = (bf16[10,32,128]{2,1,0:T(8,128)(2,1)S(1)}, bf16[10,32,128]{2,1,0:T(8,128)(2,1)S(1)}, u32[]{:S(2)}, u32[]{:S(2)}) collective-permute-start(bf16[10,32,128]{2,1,0:T(8,128)(2,1)S(1)} %shard_map.72.own_ref), channel_id=1, source_target_pairs={{0,4},{1,5},{2,6},{3,7},{4,0},{5,1},{6,2},{7,3},{8,12},{9,13},{10,... | collective-permute-start | bytes 245768 | tf_op jit(solution)/shard_map/ppermute | solution.py:25
  24.7 6.7 %collective-permute-start.7 = (bf16[10,32,128]{2,1,0:T(8,128)(2,1)S(1)}, bf16[10,32,128]{2,1,0:T(8,128)(2,1)S(1)}, u32[]{:S(2)}, u32[]{:S(2)}) collective-permute-start(bf16[10,32,128]{2,1,0:T(8,128)(2,1)S(1)} %shard_map.73.own_ref), channel_id=1, source_target_pairs={{0,8},{1,9},{2,10},{3,11},{4,12},{5,13},{6,14},{7,15},{8,0},{9,1},... | collective-permute-start | bytes 245768 | tf_op jit(solution)/shard_map/ppermute | solution.py:25

commit v4 on v3

v4 whole, which is shorter than its diff:
```python
import functools

import jax
import jax.numpy as jnp
from jax import lax
from jax.experimental import pallas as pl
from jax.experimental.pallas import tpu as pltpu
from jax.sharding import PartitionSpec as P


F32 = jnp.float32
BF16 = jnp.bfloat16
AXES = ("depth", "rows")
VMEM = pl.BlockSpec(memory_space=pltpu.VMEM)


def exchange(value, shape, target):
    depth, rows = shape
    pairs = []
    for d in range(depth):
        for r in range(rows):
            to_d, to_r = target(d, r)
            if 0 <= to_d < depth and 0 <= to_r < rows:
                pairs.append((d * rows + r, to_d * rows + to_r))
    return lax.ppermute(value, AXES, pairs)


def prepare_kernel(k1_ref, k2_ref, proj_ref, w1_ref, w2_ref, pb_ref):
    taps = k1_ref.shape[0]
    chans = k1_ref.shape[3]
    span = taps * chans
    turned_over = lax.axis_index("rows") // 2 == 1
    row_tap = [jnp.where(turned_over, taps - 1 - b, b) for b in range(taps)]
    for k_ref, w_ref in ((k1_ref, w1_ref), (k2_ref, w2_ref)):
        made = w_ref.shape[0] // (taps * chans)
        for e in range(taps):
            flat = jnp.concatenate(
                [k_ref[a, row_tap[b], e].astype(F32) for a in range(taps) for b in range(taps)]
                + [jnp.zeros(((made - 1) * span, chans), F32)],
                axis=0,
            )
            turned = flat.T
            for p in range(made):
                moved = turned if p == 0 else pltpu.roll(turned, p * span, 1)
                at = (e * made + p) * chans
                w_ref[at : at + chans, :] = moved.astype(BF16)
    lanes = pb_ref.shape[1]
    pb_ref[...] = jnp.broadcast_to(proj_ref[...], (lanes, chans)).T


def cut_kernel(block_ref, pick_ref, high_ref, low_ref):
    half, halo = pick_ref.shape[0], high_ref.shape[1]
    rows = block_ref.shape[1]
    core = lax.axis_index("rows") % 2
    pick_ref[...] = block_ref[pl.ds(core * half, half)]
    high_ref[...] = block_ref[:, :halo]
    low_ref[...] = block_ref[:, rows - halo :]


def shifted_sum(y, group):
    width = y.shape[1] // 2
    lane = lax.broadcasted_iota(jnp.int32, (1, width), 1)
    parts = []
    for s in range(2):
        cols = slice(s * width, (s + 1) * width)
        before = pltpu.roll(y[:group, cols], 1, 1)
        here = y[group : 2 * group, cols]
        after = pltpu.roll(y[2 * group :, cols], width - 1, 1)
        parts.append(
            here + jnp.where(lane == 0, 0.0, before) + jnp.where(lane == width - 1, 0.0, after)
        )
    return parts


def pieces(value, count):
    out = []
    for _ in range(count - 1):
        top = value.astype(BF16).astype(F32)
        out.append(top)
        value = value - top
    return out + [value]


def stat_pieces(peak, total, depth):
    return pieces(peak * 0.5, 3) + pieces(total, 2) + [depth]


def store_parcel(ref, feats, peak, total, depth):
    chans = feats[0].shape[0]
    for i, feat in enumerate(feats):
        ref[i * chans : (i + 1) * chans] = feat.astype(BF16)
    flat = stat_pieces(peak, total, depth)
    ref[len(feats) * chans :] = jnp.concatenate(flat, axis=0).astype(BF16)


def load_stats(ref, rows):
    flat = ref[ref.shape[0] - 6 * rows :].astype(F32)
    flat = [flat[k * rows : (k + 1) * rows] for k in range(6)]
    return ((flat[0] + flat[1]) + flat[2]) * 2.0, flat[3] + flat[4], flat[5]


def first_layer(w, x, half, chans, first_plane, g, all_planes, store):
    lo, hi = shifted_sum(jnp.dot(w, x, preferred_element_type=F32), half * chans)
    for p in range(half):
        part = slice(p * chans, (p + 1) * chans)
        a, b = jnp.maximum(lo[part], 0.0), jnp.maximum(hi[part], 0.0)
        if g + p == 0 or g + p == half + 1:
            plane = first_plane + g + p
            outside = jnp.logical_or(plane < 0, plane >= all_planes)
            a = jnp.where(outside, 0.0, a)
            b = jnp.where(outside, 0.0, b)
        store(g + p, a.astype(BF16), b.astype(BF16))


def second_layer(w, x, pb, ps_ref, fracs, two_rows, over, feat_ref, stat_ref):
    chans = feat_ref.shape[2]
    rows = feat_ref.shape[1]
    half = len(fracs)
    y = jnp.dot(w, x, preferred_element_type=F32)
    for row, side in zip(two_rows, shifted_sum(y, half * chans)):
        far = row // rows
        at = jnp.where(over, rows - 1 - row % rows, row % rows)
        side = jnp.maximum(side, 0.0).astype(BF16).astype(F32)
        feats = [side[p * chans : (p + 1) * chans] for p in range(half)]
        scores = [
            jnp.sum(feats[p] * pb, axis=0, keepdims=True) + ps_ref[far, p, pl.ds(at, 1), :]
            for p in range(half)
        ]
        peak = functools.reduce(jnp.maximum, scores)
        weights = [jnp.exp(s_ - peak) for s_ in scores]
        total = functools.reduce(jnp.add, weights)
        depth_sum = functools.reduce(jnp.add, [w_ * f for w_, f in zip(weights, fracs)])
        feat_ref[far, at] = functools.reduce(jnp.add, [w_ * f for w_, f in zip(weights, feats)])
        for k, value in enumerate((peak, total, depth_sum)):
            stat_ref[far, k, pl.ds(at, 1), :] = value


def place_of(depth, planes):
    half = planes // 2
    core = lax.axis_index("rows") % 2
    over = lax.axis_index("rows") // 2 == 1
    first_plane = lax.axis_index("depth") * planes + core * half - 1
    all_planes = depth * planes
    fracs = [((first_plane + 1 + p).astype(F32) + 0.5) / all_planes for p in range(half)]
    return core, over, first_plane, all_planes, fracs


def inner_kernel(
    depth, own_ref, sib_ref, zh_ref, op_ref, sp_ref, w1_ref, w2_ref, pb_ref,
    xs_ref, fs_ref, ps_ref, feat_ref, stat_ref,
):
    planes, rows, chans, width = own_ref.shape
    half = planes // 2
    halo = 2
    both = 2 * rows
    lead = rows - 1
    core, over, first_plane, all_planes, fracs = place_of(depth, planes)
    left = slice(0, width)
    right = slice(width, 2 * width)

    def fill(c, flip):
        blocks = (own_ref, sib_ref) if c == 0 else (sib_ref, own_ref)
        base = halo * (1 - c)
        mine = slice(base, base + planes)
        zs = slice(0, halo) if c == 0 else slice(planes, planes + halo)
        for cols, start in ((left, -1), (right, lead - 1)):
            for slot in range(rows + 2):
                row = start + slot
                if row < 0:
                    xs_ref[:, slot, :, cols] = jnp.zeros((planes + halo, chans, width), BF16)
                    continue
                row = both - 1 - row if flip else row
                xs_ref[mine, slot, :, cols] = blocks[row // rows][:, row % rows]
                xs_ref[zs, slot, :, cols] = zh_ref[:, row]
        mine_p = slice(half * c, half * c + half)
        priors = (op_ref, sp_ref) if c == 0 else (sp_ref, op_ref)
        for k in range(2):
            ps_ref[k] = priors[1 - k if flip else k][mine_p]

    for c in range(2):
        for flip in (False, True):
            pl.when(jnp.logical_and(core == c, over == flip))(functools.partial(fill, c, flip))

    deep = (half + 2) * 3 * chans
    w1 = w1_ref[...]
    fs_ref[:, 0, :, left] = jnp.zeros((half + 2, chans, width), BF16)
    for g in range(0, half + 2, half):
        for i in range(rows):
            def store(j, a, b, i=i):
                fs_ref[j, i + 1, :, left] = a
                fs_ref[j, i + 1, :, right] = b
                if i == lead - 1:
                    fs_ref[j, 0, :, right] = a

            x = xs_ref[g : g + half + 2, i : i + 3].reshape(deep, 2 * width)
            first_layer(w1, x, half, chans, first_plane, g, all_planes, store)

    w2 = w2_ref[...]
    pb = pb_ref[...]
    for i in range(lead):
        x = fs_ref[:, i : i + 3].reshape(deep, 2 * width)
        second_layer(w2, x, pb, ps_ref, fracs, (i, i + lead), over, feat_ref, stat_ref)


def outer_kernel(
    depth, side_ref, corner_ref, xs_ref, fs_ref, ps_ref, fi_ref, ti_ref, w1_ref, w2_ref, pb_ref,
    keep_ref, stat_ref, send_ref, halo_ref, late_ref, feat_ref, all_ref,
):
    planes, halo, chans, width = side_ref.shape
    half = planes // 2
    rows = keep_ref.shape[0]
    core, over, first_plane, all_planes, fracs = place_of(depth, planes)
    right = slice(width, 2 * width)

    def fill(c):
        base = halo * (1 - c)
        zs = 0 if c == 0 else planes
        for k in range(halo):
            at = jnp.where(over, halo - 1 - k, k)
            for p in range(planes):
                halo_ref[base + p, k] = side_ref[p, at]
            for p in range(halo):
                halo_ref[zs + p, k] = corner_ref[p, at]

    for c in range(2):
        pl.when(core == c)(functools.partial(fill, c))

    def pair(parts):
        return jnp.concatenate(
            [jnp.concatenate(p, axis=1).reshape(-1, width) for p in parts], axis=1
        )

    w1 = w1_ref[...]
    for g in range(0, half + 2, half):
        span = slice(g, g + half + 2)
        x = pair(
            [
                [xs_ref[span, rows:, :, right], halo_ref[span, :1]],
                [xs_ref[span, rows + 1 :, :, right], halo_ref[span]],
            ]
        )

        def store(j, a, b):
            late_ref[j, 0] = a
            late_ref[j, 1] = b

        first_layer(w1, x, half, chans, first_plane, g, all_planes, store)

    feat_ref[...] = fi_ref[...]
    all_ref[...] = ti_ref[...]
    x = pair(
        [
            [fs_ref[:, rows - 1 :, :, right], late_ref[:, :1]],
            [fs_ref[:, rows:, :, right], late_ref[...]],
        ]
    )
    two_rows = (2 * rows - 2, 2 * rows - 1)
    second_layer(w2_ref[...], x, pb_ref[...], ps_ref, fracs, two_rows, over, feat_ref, all_ref)
    kept = jnp.where(over, 1 - core, core)
    keep_ref[...] = feat_ref[kept]
    stat_ref[...] = all_ref[kept]
    given = 1 - kept
    feats = [feat_ref[given, i] for i in range(rows)]
    store_parcel(send_ref, feats, *[all_ref[given, k] for k in range(3)])


def merge(one, two, rows):
    (feat_a, stats_a), (feat_b, stats_b) = one, two
    peak = jnp.maximum(stats_a[0], stats_b[0])
    wa = jnp.exp(stats_a[0] - peak)
    wb = jnp.exp(stats_b[0] - peak)
    total = wa * stats_a[1] + wb * stats_b[1]
    depth = wa * stats_a[2] + wb * stats_b[2]
    feats = [
        wa[i : i + 1] * feat_a(i) + wb[i : i + 1] * feat_b(i) for i in range(rows)
    ]
    return feats, peak, total, depth


def parcel(ref, rows):
    chans = ref.shape[0] // rows - 6
    return (lambda i: ref[i * chans : (i + 1) * chans].astype(F32)), load_stats(ref, rows)


def first_merge_kernel(keep_ref, stat_ref, got_ref, out_ref):
    rows = keep_ref.shape[0]
    mine = (lambda i: keep_ref[i]), tuple(stat_ref[k] for k in range(3))
    store_parcel(out_ref, *merge(mine, parcel(got_ref, rows), rows))


def merge_kernel(step, rows, own_ref, got_ref, out_ref):
    low = (lax.axis_index("depth") // step) % 2 == 0

    def go(a_ref, b_ref):
        store_parcel(out_ref, *merge(parcel(a_ref, rows), parcel(b_ref, rows), rows))

    pl.when(low)(lambda: go(own_ref, got_ref))
    pl.when(jnp.logical_not(low))(lambda: go(got_ref, own_ref))


def last_merge_kernel(step, own_ref, got_ref, joined_ref, depth_ref):
    rows = joined_ref.shape[0]
    low = (lax.axis_index("depth") // step) % 2 == 0

    def go(a_ref, b_ref):
        feats, _, total, depth = merge(parcel(a_ref, rows), parcel(b_ref, rows), rows)
        inverse = 1.0 / total
        for i in range(rows):
            joined_ref[i] = feats[i] * inverse[i : i + 1]
        depth_ref[...] = depth * inverse

    pl.when(low)(lambda: go(own_ref, got_ref))
    pl.when(jnp.logical_not(low))(lambda: go(got_ref, own_ref))


def call(kernel, outs, *args, scratch=(), flops=0, nbytes=0, room=4):
    return pl.pallas_call(
        kernel,
        out_shape=[jax.ShapeDtypeStruct(s, t) for s, t in outs],
        in_specs=[VMEM] * len(args),
        out_specs=[VMEM] * len(outs),
        scratch_shapes=list(scratch),
        cost_estimate=pl.CostEstimate(flops=flops, bytes_accessed=nbytes, transcendentals=0),
        compiler_params=pltpu.CompilerParams(vmem_limit_bytes=room * 2**20),
    )(*args)


def body(volume, prior, first_kernel, second_kernel, projection):
    planes, rows, chans, width = volume.shape
    depth, rows_axis = lax.axis_size("depth"), lax.axis_size("rows")
    shape = (depth, rows_axis)
    half = planes // 2
    halo = 2
    taps = first_kernel.shape[0]
    columns = rows_axis // 2
    assert half == halo and columns == 2 and rows_axis == 4 and depth & (depth - 1) == 0

    def move(value, target):
        return exchange(value, shape, target)

    weight_shape = (taps * half * chans, (half + 2) * taps * chans)
    w1, w2, pb = call(
        prepare_kernel,
        [(weight_shape, BF16), (weight_shape, BF16), ((chans, width), F32)],
        first_kernel, second_kernel, projection[None, :],
        flops=10**8, nbytes=10**6,
    )

    core = lax.axis_index("rows") % 2
    col = lax.axis_index("rows") // 2
    lower = core == 0
    beside = move(volume, lambda d, r: (d, r ^ 1))
    prior_beside = move(prior, lambda d, r: (d, r ^ 1))
    beside, prior_beside = lax.optimization_barrier((beside, prior_beside))

    high = slice(0, halo)
    low = slice(rows - halo, rows)

    def parts(block):
        picked = jnp.where(lower, block[:half], block[half:])
        return picked, block[:, high], block[:, low]

    edge_shape = (planes, halo, chans, width)
    own_pick, own_high, own_low = call(
        cut_kernel,
        [((half, rows, chans, width), BF16), (edge_shape, BF16), (edge_shape, BF16)],
        volume,
    )
    sib_pick, sib_high, sib_low = parts(beside)
    edge = jnp.where(
        lower,
        jnp.concatenate([own_pick, sib_pick], axis=1),
        jnp.concatenate([sib_pick, own_pick], axis=1),
    )
    top_high = jnp.where(lower, own_high, sib_high)
    bottom_low = jnp.where(lower, sib_low, own_low)
    up = lambda d, r: (d + 1, r ^ 1) if r % 2 else (d - 1, r ^ 1)
    zh = move(edge, up)
    pay = jnp.where(col == 0, bottom_low, top_high)
    corner = jnp.where(lower, pay[:half], pay[half:])
    side = move(pay, lambda d, r: (d, r ^ 2))
    corner = move(corner, lambda d, r: (up(d, r)[0], r ^ 3))

    parcel_shape = (rows * (chans + 6), width)
    stats_shape = (3, rows, width)
    inside = call(
        functools.partial(inner_kernel, depth),
        [
            ((planes + halo, rows + 2, chans, 2 * width), BF16),
            ((half + 2, rows + 1, chans, 2 * width), BF16),
            ((2, half, rows, width), F32),
            ((2, rows, chans, width), F32),
            ((2,) + stats_shape, F32),
        ],
        volume, beside, zh, prior, prior_beside, w1, w2, pb,
        flops=5 * 10**8, nbytes=10**6, room=6,
    )
    keep, stat, send = call(
        functools.partial(outer_kernel, depth),
        [((rows, chans, width), F32), (stats_shape, F32), (parcel_shape, BF16)],
        side, corner, *inside, w1, w2, pb,
        scratch=[
            pltpu.VMEM((planes + halo, halo, chans, width), BF16),
            pltpu.VMEM((half + 2, halo, chans, width), BF16),
            pltpu.VMEM((2, rows, chans, width), F32),
            pltpu.VMEM((2,) + stats_shape, F32),
        ],
        flops=10**8, nbytes=10**6, room=6,
    )
    got = move(send, lambda d, r: (d, r ^ 1))
    (sums,) = call(first_merge_kernel, [(parcel_shape, BF16)], keep, stat, got)
    step = 1
    while step < depth:
        got = move(sums, lambda d, r: (d ^ step, r))
        if 2 * step < depth:
            (sums,) = call(functools.partial(merge_kernel, step, rows), [(parcel_shape, BF16)], sums, got)
        else:
            joined, depth_estimate = call(
                functools.partial(last_merge_kernel, step),
                [((rows, chans, width), F32), ((rows, width), F32)],
                sums, got,
            )
        step *= 2
    return joined, depth_estimate


def solution(mesh):
    placed = (
        P(("tiles", "depth"), "rows", None, None),
        P(("tiles", "depth"), "rows", None),
        P(),
        P(),
        P(),
    )
    return jax.shard_map(
        body,
        mesh=mesh,
        in_specs=placed,
        out_specs=(P(("tiles", "rows"), None, None), P(("tiles", "rows"), None)),
        check_vma=False,
    )
```

time: 32.3 us -> 31.2 us (0.966)
  local copies, waits for them, and re-layouts: 3.51 us -> 2.77 us
    unnamed x12, local copies, waits for them, and re-layouts: 3.51 us -> 2.77 us
  transfers between devices with their start and end apart: 8 -> 8, of which waited for: 4 -> 3; matrix products, arithmetic and copies ran while one was open for 0% -> 0% of each run, Pallas kernels for 6% -> 7%
where the time goes in v4:
time: 31.2 us; the launch traced here: 30.9 us
  starting transfers between devices  15.6 us (50%)
  waiting for transfers between devices  7.88 us (25%)
  Pallas kernels  3.84 us (12%)
  local copies, waits for them, and re-layouts  2.77 us (9%)
  between operations  0.8 us (3%)
    ppermute x8, starting transfers between devices, exchange(): return lax.ppermute(value, AXES, pairs)  15.6 us
    ppermute x8, waiting for transfers between devices, exchange(): return lax.ppermute(value, AXES, pairs)  7.88 us
    pallas_call x7, Pallas kernels, call(): pl.pallas_call(kernel, out_shape=[jax.ShapeDtypeStruct(s, t) for s, t in...  3.84 us
    unnamed x12, local copies, waits for them, and re-layouts  2.77 us
  transfers between devices with their start and end apart: 8, of which 3 were waited for; matrix products, arithmetic and copies ran while one was open for 0% of the time, Pallas kernels for 7%

profile of v4, /device:TPU:0, one launch (start us, length us, event | category | flops | bytes accessed | tf_op | source)
XLA Modules:
  0.0 30.9 jit_solution(6710106748353425577)
XLA Ops:
  0.6 0.6 %collective-permute-start = (bf16[4,8,32,128]{3,2,1,0:T(8,128)(2,1)}, bf16[4,8,32,128]{3,2,1,0:T(8,128)(2,1)S(1)}, u32[]{:S(2)}, u32[]{:S(2)}) collective-permute-start(bf16[4,8,32,128]{3,2,1,0:T(8,128)(2,1)} %own_ref.1), channel_id=1, source_target_pairs={{0,1},{1,0},{2,3},{3,2},{4,5},{5,4},{6,7},{7,6},{8,9},{9,8},{10,11... | collective-permute-start | bytes 786440 | tf_op jit(solution)/shard_map/ppermute | solution.py:25
  1.2 0.1 collective-permute-start.1
  1.3 0.0 copy-start
  1.3 0.9 %copy-done = bf16[4,8,32,128]{3,2,1,0:T(8,128)(2,1)S(1)} copy-done((bf16[4,8,32,128]{3,2,1,0:T(8,128)(2,1)S(1)}, bf16[4,8,32,128]{3,2,1,0:T(8,128)(2,1)}, u32[]{:S(2)}) %copy-start) | copy-done | bytes 262168
  2.2 0.0 copy-start.2
  2.3 0.0 copy-start.4
  2.3 0.9 %copy-done.2 = bf16[3,3,3,32,32]{4,3,2,1,0:T(8,128)(2,1)S(1)} copy-done((bf16[3,3,3,32,32]{4,3,2,1,0:T(8,128)(2,1)S(1)}, bf16[3,3,3,32,32]{4,3,2,1,0:T(8,128)(2,1)}, u32[]{:S(2)}) %copy-start.2) | copy-done | bytes 55320
  3.2 0.0 copy-done.4
  3.2 0.0 copy-start.3
  3.2 0.9 %copy-done.3 = bf16[3,3,3,32,32]{4,3,2,1,0:T(8,128)(2,1)S(1)} copy-done((bf16[3,3,3,32,32]{4,3,2,1,0:T(8,128)(2,1)S(1)}, bf16[3,3,3,32,32]{4,3,2,1,0:T(8,128)(2,1)}, u32[]{:S(2)}) %copy-start.3) | copy-done | bytes 55320
  4.1 0.4 %shard_map.69 = (bf16[192,384]{1,0:T(8,128)(2,1)S(1)}, bf16[192,384]{1,0:T(8,128)(2,1)S(1)}, f32[32,128]{1,0:T(8,128)S(1)}) custom-call(bf16[3,3,3,32,32]{4,3,2,1,0:T(8,128)(2,1)S(1)} %copy-done.2, bf16[3,3,3,32,32]{4,3,2,1,0:T(8,128)(2,1)S(1)} %copy-done.3, f32[1,32]{1,0:T(1,128)S(1)} %bitcast.1), custom_call_target="tpu_custom_call" | custom-call | flops 100000000 | bytes 1000000 | tf_op jit(solution)/shard_map/pallas_call | solution.py:317
  4.5 0.0 collective-permute-done.1.sp_ref
  4.5 0.0 collective-permute-done.sib_ref
  4.5 0.0 copy-start.1
  4.6 0.8 %collective-permute-start.4 = (bf16[2,16,32,128]{3,2,1,0:T(8,128)(2,1)S(1)}, bf16[2,16,32,128]{3,2,1,0:T(8,128)(2,1)S(1)}, u32[]{:S(2)}, u32[]{:S(2)}) collective-permute-start(bf16[2,16,32,128]{3,2,1,0:T(8,128)(2,1)S(1)} %maximum_select_fusion), channel_id=1, source_target_pairs={{1,4},{3,6},{4,1},{5,8},{6,3},{7,10},{8,5},{9,12},{10,7},{11,14},{... | collective-permute-start | bytes 786440 | tf_op jit(solution)/shard_map/ppermute | solution.py:25
  5.4 0.0 copy-start.5
  5.4 3.0 %collective-permute-start.2 = (bf16[4,2,32,128]{3,2,1,0:T(8,128)(2,1)S(1)}, bf16[4,2,32,128]{3,2,1,0:T(8,128)(2,1)S(1)}, u32[]{:S(2)}, u32[]{:S(2)}) collective-permute-start(bf16[4,2,32,128]{3,2,1,0:T(8,128)(2,1)S(1)} %select_select_fusion), channel_id=1, source_target_pairs={{0,2},{1,3},{2,0},{3,1},{4,6},{5,7},{6,4},{7,5},{8,10},{9,11},{10,... | collective-permute-start | bytes 196616 | tf_op jit(solution)/shard_map/ppermute | solution.py:25
  8.4 0.7 %collective-permute-start.3 = (bf16[2,2,32,128]{3,2,1,0:T(8,128)(2,1)S(1)}, bf16[2,2,32,128]{3,2,1,0:T(8,128)(2,1)S(1)}, u32[]{:S(2)}, u32[]{:S(2)}) collective-permute-start(bf16[2,2,32,128]{3,2,1,0:T(8,128)(2,1)S(1)} %slice_select_fusion.1), channel_id=1, source_target_pairs={{1,6},{3,4},{4,3},{5,10},{6,1},{7,8},{8,7},{9,14},{10,5},{11,12},{... | collective-permute-start | bytes 98312 | tf_op jit(solution)/shard_map/ppermute | solution.py:25
  9.1 0.0 collective-permute-done.4.zh_ref
  9.1 0.0 copy-done.1
  9.1 0.0 copy-done.5
  9.1 1.9 %shard_map.70 = (bf16[6,10,32,256]{3,2,1,0:T(8,128)(2,1)S(1)}, bf16[4,9,32,256]{3,2,1,0:T(8,128)(2,1)S(1)}, f32[2,2,8,128]{3,2,1,0:T(8,128)S(1)}, f32[2,8,32,128]{3,2,1,0:T(8,128)S(1)}, f32[2,3,8,128]{3,2,1,0:T(8,128)S(1)}) custom-call(bf16[4,8,32,128]{3,2,1,0:T(8,128)(2,1)S(1)} %copy-done.1, bf16[4,8,32,128]{3,2,1,0:T(8,128)(2,1)S(1)} %collective-permute-done.sib_ref, ...), custom_call_target="tpu_custom_call" | custom-call | flops 500000000 | bytes 1000000 | tf_op jit(solution)/shard_map/pallas_call | solution.py:317
  11.0 0.0 collective-permute-done.3.corner_ref
  11.0 0.0 collective-permute-done.2.side_ref
  11.0 0.8 %shard_map.71 = (f32[8,32,128]{2,1,0:T(8,128)S(1)}, f32[3,8,128]{2,1,0:T(8,128)S(1)}, bf16[304,128]{1,0:T(8,128)(2,1)S(1)}) custom-call(bf16[4,2,32,128]{3,2,1,0:T(8,128)(2,1)S(1)} %collective-permute-done.2.side_ref, bf16[2,2,32,128]{3,2,1,0:T(8,128)(2,1)S(1)} %collective-permute-done.3.corner_ref, bf16[6,10,32,256]{3,2,1,0:T(8,128)(2,1)S(1)} %get-tuple-element.26.xs_ref, ...), custom_call_target="tpu_custom_call" | custom-call | flops 100000000 | bytes 1000000 | tf_op jit(solution)/shard_map/pallas_call | solution.py:317
  11.8 6.2 %collective-permute-start.5 = (bf16[304,128]{1,0:T(8,128)(2,1)S(1)}, bf16[304,128]{1,0:T(8,128)(2,1)S(1)}, u32[]{:S(2)}, u32[]{:S(2)}) collective-permute-start(bf16[304,128]{1,0:T(8,128)(2,1)S(1)} %get-tuple-element.33), channel_id=1, source_target_pairs={{0,1},{1,0},{2,3},{3,2},{4,5},{5,4},{6,7},{7,6},{8,9},{9,8},{10,11... | collective-permute-start | bytes 233480 | tf_op jit(solution)/shard_map/ppermute | solution.py:25
  18.0 0.9 %collective-permute-done.5.got_ref = bf16[304,128]{1,0:T(8,128)(2,1)S(1)} collective-permute-done((bf16[304,128]{1,0:T(8,128)(2,1)S(1)}, bf16[304,128]{1,0:T(8,128)(2,1)S(1)}, u32[]{:S(2)}, u32[]{:S(2)}) %collective-permute-start.5) | collective-permute-done | bytes 77856 | tf_op jit(solution)/shard_map/ppermute | solution.py:25
  18.9 1.6 %collective-permute-start.6 = (bf16[304,128]{1,0:T(8,128)(2,1)S(1)}, bf16[304,128]{1,0:T(8,128)(2,1)S(1)}, u32[]{:S(2)}, u32[]{:S(2)}) collective-permute-start(bf16[304,128]{1,0:T(8,128)(2,1)S(1)} %shard_map.72.own_ref), channel_id=1, source_target_pairs={{0,4},{1,5},{2,6},{3,7},{4,0},{5,1},{6,2},{7,3},{8,12},{9,13},{10,... | collective-permute-start | bytes 233480 | tf_op jit(solution)/shard_map/ppermute | solution.py:25
  20.6 3.0 %collective-permute-done.6.got_ref = bf16[304,128]{1,0:T(8,128)(2,1)S(1)} collective-permute-done((bf16[304,128]{1,0:T(8,128)(2,1)S(1)}, bf16[304,128]{1,0:T(8,128)(2,1)S(1)}, u32[]{:S(2)}, u32[]{:S(2)}) %collective-permute-start.6) | collective-permute-done | bytes 77856 | tf_op jit(solution)/shard_map/ppermute | solution.py:25
  23.7 2.7 %collective-permute-start.7 = (bf16[304,128]{1,0:T(8,128)(2,1)S(1)}, bf16[304,128]{1,0:T(8,128)(2,1)S(1)}, u32[]{:S(2)}, u32[]{:S(2)}) collective-permute-start(bf16[304,128]{1,0:T(8,128)(2,1)S(1)} %shard_map.73.own_ref), channel_id=1, source_target_pairs={{0,8},{1,9},{2,10},{3,11},{4,12},{5,13},{6,14},{7,15},{8,0},{9,1},... | collective-permute-start | bytes 233480 | tf_op jit(solution)/shard_map/ppermute | solution.py:25
  26.3 3.9 %collective-permute-done.7.got_ref = bf16[304,128]{1,0:T(8,128)(2,1)S(1)} collective-permute-done((bf16[304,128]{1,0:T(8,128)(2,1)S(1)}, bf16[304,128]{1,0:T(8,128)(2,1)S(1)}, u32[]{:S(2)}, u32[]{:S(2)}) %collective-permute-start.7) | collective-permute-done | bytes 77856 | tf_op jit(solution)/shard_map/ppermute | solution.py:25
  30.2 0.7 %shard_map.74 = (f32[8,32,128]{2,1,0:T(8,128)}, f32[8,128]{1,0:T(8,128)}) custom-call(bf16[304,128]{1,0:T(8,128)(2,1)S(1)} %shard_map.73.own_ref, bf16[304,128]{1,0:T(8,128)(2,1)S(1)} %collective-permute-done.7.got_ref), custom_call_target="tpu_custom_call" | custom-call | tf_op jit(solution)/shard_map/pallas_call | solution.py:317
  (7 shorter events, 0.2 us)
Async XLA Ops:
  0.6 3.9 %collective-permute-start = (bf16[4,8,32,128]{3,2,1,0:T(8,128)(2,1)}, bf16[4,8,32,128]{3,2,1,0:T(8,128)(2,1)S(1)}, u32[]{:S(2)}, u32[]{:S(2)}) collective-permute-start(bf16[4,8,32,128]{3,2,1,0:T(8,128)(2,1)} %own_ref.1), channel_id=1, source_target_pairs={{0,1},{1,0},{2,3},{3,2},{4,5},{5,4},{6,7},{7,6},{8,9},{9,8},{10,11... | collective-permute-start | bytes 786440 | tf_op jit(solution)/shard_map/ppermute | solution.py:25
  1.2 3.3 %collective-permute-start.1 = (f32[4,8,128]{2,1,0:T(8,128)}, f32[4,8,128]{2,1,0:T(8,128)S(1)}, u32[]{:S(2)}, u32[]{:S(2)}) collective-permute-start(f32[4,8,128]{2,1,0:T(8,128)} %op_ref.1), channel_id=1, source_target_pairs={{0,1},{1,0},{2,3},{3,2},{4,5},{5,4},{6,7},{7,6},{8,9},{9,8},{10,11... | collective-permute-start | bytes 49160 | tf_op jit(solution)/shard_map/ppermute | solution.py:25
  1.3 0.9 %copy-start = (bf16[4,8,32,128]{3,2,1,0:T(8,128)(2,1)S(1)}, bf16[4,8,32,128]{3,2,1,0:T(8,128)(2,1)}, u32[]{:S(2)}) copy-start(bf16[4,8,32,128]{3,2,1,0:T(8,128)(2,1)} %own_ref.1) | copy-start | bytes 786436
  2.2 0.9 %copy-start.2 = (bf16[3,3,3,32,32]{4,3,2,1,0:T(8,128)(2,1)S(1)}, bf16[3,3,3,32,32]{4,3,2,1,0:T(8,128)(2,1)}, u32[]{:S(2)}) copy-start(bf16[3,3,3,32,32]{4,3,2,1,0:T(8,128)(2,1)} %k1_ref.1) | copy-start | bytes 165892
  2.3 0.9 %copy-start.4 = (f32[32]{0:T(128)S(1)}, f32[32]{0:T(128)}, u32[]{:S(2)}) copy-start(f32[32]{0:T(128)} %param.9) | copy-start | bytes 388
  3.2 0.9 %copy-start.3 = (bf16[3,3,3,32,32]{4,3,2,1,0:T(8,128)(2,1)S(1)}, bf16[3,3,3,32,32]{4,3,2,1,0:T(8,128)(2,1)}, u32[]{:S(2)}) copy-start(bf16[3,3,3,32,32]{4,3,2,1,0:T(8,128)(2,1)} %k2_ref.1) | copy-start | bytes 165892
  4.5 4.5 %copy-start.1 = (bf16[4,8,32,128]{3,2,1,0:T(8,128)(2,1)S(1)}, bf16[4,8,32,128]{3,2,1,0:T(8,128)(2,1)}, u32[]{:S(2)}) copy-start(bf16[4,8,32,128]{3,2,1,0:T(8,128)(2,1)} %own_ref.1) | copy-start | bytes 786436
  4.6 4.5 %collective-permute-start.4 = (bf16[2,16,32,128]{3,2,1,0:T(8,128)(2,1)S(1)}, bf16[2,16,32,128]{3,2,1,0:T(8,128)(2,1)S(1)}, u32[]{:S(2)}, u32[]{:S(2)}) collective-permute-start(bf16[2,16,32,128]{3,2,1,0:T(8,128)(2,1)S(1)} %maximum_select_fusion), channel_id=1, source_target_pairs={{1,4},{3,6},{4,1},{5,8},{6,3},{7,10},{8,5},{9,12},{10,7},{11,14},{... | collective-permute-start | bytes 786440 | tf_op jit(solution)/shard_map/ppermute | solution.py:25
  5.4 3.7 %copy-start.5 = (f32[4,8,128]{2,1,0:T(8,128)S(1)}, f32[4,8,128]{2,1,0:T(8,128)}, u32[]{:S(2)}) copy-start(f32[4,8,128]{2,1,0:T(8,128)} %op_ref.1) | copy-start | bytes 49156
  5.4 5.6 %collective-permute-start.2 = (bf16[4,2,32,128]{3,2,1,0:T(8,128)(2,1)S(1)}, bf16[4,2,32,128]{3,2,1,0:T(8,128)(2,1)S(1)}, u32[]{:S(2)}, u32[]{:S(2)}) collective-permute-start(bf16[4,2,32,128]{3,2,1,0:T(8,128)(2,1)S(1)} %select_select_fusion), channel_id=1, source_target_pairs={{0,2},{1,3},{2,0},{3,1},{4,6},{5,7},{6,4},{7,5},{8,10},{9,11},{10,... | collective-permute-start | bytes 196616 | tf_op jit(solution)/shard_map/ppermute | solution.py:25
  8.4 2.6 %collective-permute-start.3 = (bf16[2,2,32,128]{3,2,1,0:T(8,128)(2,1)S(1)}, bf16[2,2,32,128]{3,2,1,0:T(8,128)(2,1)S(1)}, u32[]{:S(2)}, u32[]{:S(2)}) collective-permute-start(bf16[2,2,32,128]{3,2,1,0:T(8,128)(2,1)S(1)} %slice_select_fusion.1), channel_id=1, source_target_pairs={{1,6},{3,4},{4,3},{5,10},{6,1},{7,8},{8,7},{9,14},{10,5},{11,12},{... | collective-permute-start | bytes 98312 | tf_op jit(solution)/shard_map/ppermute | solution.py:25
  11.8 7.1 %collective-permute-start.5 = (bf16[304,128]{1,0:T(8,128)(2,1)S(1)}, bf16[304,128]{1,0:T(8,128)(2,1)S(1)}, u32[]{:S(2)}, u32[]{:S(2)}) collective-permute-start(bf16[304,128]{1,0:T(8,128)(2,1)S(1)} %get-tuple-element.33), channel_id=1, source_target_pairs={{0,1},{1,0},{2,3},{3,2},{4,5},{5,4},{6,7},{7,6},{8,9},{9,8},{10,11... | collective-permute-start | bytes 233480 | tf_op jit(solution)/shard_map/ppermute | solution.py:25
  18.9 4.7 %collective-permute-start.6 = (bf16[304,128]{1,0:T(8,128)(2,1)S(1)}, bf16[304,128]{1,0:T(8,128)(2,1)S(1)}, u32[]{:S(2)}, u32[]{:S(2)}) collective-permute-start(bf16[304,128]{1,0:T(8,128)(2,1)S(1)} %shard_map.72.own_ref), channel_id=1, source_target_pairs={{0,4},{1,5},{2,6},{3,7},{4,0},{5,1},{6,2},{7,3},{8,12},{9,13},{10,... | collective-permute-start | bytes 233480 | tf_op jit(solution)/shard_map/ppermute | solution.py:25
  23.7 6.6 %collective-permute-start.7 = (bf16[304,128]{1,0:T(8,128)(2,1)S(1)}, bf16[304,128]{1,0:T(8,128)(2,1)S(1)}, u32[]{:S(2)}, u32[]{:S(2)}) collective-permute-start(bf16[304,128]{1,0:T(8,128)(2,1)S(1)} %shard_map.73.own_ref), channel_id=1, source_target_pairs={{0,8},{1,9},{2,10},{3,11},{4,12},{5,13},{6,14},{7,15},{8,0},{9,1},... | collective-permute-start | bytes 233480 | tf_op jit(solution)/shard_map/ppermute | solution.py:25

commit v5 on v4

--- a/solution.py
+++ b/solution.py
@@ -29,7 +29,7 @@
     taps = k1_ref.shape[0]
     chans = k1_ref.shape[3]
     span = taps * chans
-    turned_over = lax.axis_index("rows") // 2 == 1
+    turned_over = (lax.axis_index("rows") >> 1) == 1
     row_tap = [jnp.where(turned_over, taps - 1 - b, b) for b in range(taps)]
     for k_ref, w_ref in ((k1_ref, w1_ref), (k2_ref, w2_ref)):
         made = w_ref.shape[0] // (taps * chans)
@@ -51,7 +51,7 @@
 def cut_kernel(block_ref, pick_ref, high_ref, low_ref):
     half, halo = pick_ref.shape[0], high_ref.shape[1]
     rows = block_ref.shape[1]
-    core = lax.axis_index("rows") % 2
+    core = (lax.axis_index("rows") & 1)
     pick_ref[...] = block_ref[pl.ds(core * half, half)]
     high_ref[...] = block_ref[:, :halo]
     low_ref[...] = block_ref[:, rows - halo :]
@@ -137,8 +137,8 @@
 
 def place_of(depth, planes):
     half = planes // 2
-    core = lax.axis_index("rows") % 2
-    over = lax.axis_index("rows") // 2 == 1
+    core = (lax.axis_index("rows") & 1)
+    over = (lax.axis_index("rows") >> 1) == 1
     first_plane = lax.axis_index("depth") * planes + core * half - 1
     all_planes = depth * planes
     fracs = [((first_plane + 1 + p).astype(F32) + 0.5) / all_planes for p in range(half)]
@@ -163,6 +163,8 @@
         base = halo * (1 - c)
         mine = slice(base, base + planes)
         zs = slice(0, halo) if c == 0 else slice(planes, planes + halo)
+        outside = lax.axis_index("depth") == (0 if c == 0 else depth - 1)
+        zero_planes = jnp.zeros((halo, chans, width), BF16)
         for cols, start in ((left, -1), (right, lead - 1)):
             for slot in range(rows + 2):
                 row = start + slot
@@ -171,7 +173,7 @@
                     continue
                 row = both - 1 - row if flip else row
                 xs_ref[mine, slot, :, cols] = blocks[row // rows][:, row % rows]
-                xs_ref[zs, slot, :, cols] = zh_ref[:, row]
+                xs_ref[zs, slot, :, cols] = jnp.where(outside, zero_planes, zh_ref[:, row])
         mine_p = slice(half * c, half * c + half)
         priors = (op_ref, sp_ref) if c == 0 else (sp_ref, op_ref)
         for k in range(2):
@@ -215,12 +217,14 @@
     def fill(c):
         base = halo * (1 - c)
         zs = 0 if c == 0 else planes
+        outside = lax.axis_index("depth") == (0 if c == 0 else depth - 1)
         for k in range(halo):
             at = jnp.where(over, halo - 1 - k, k)
             for p in range(planes):
                 halo_ref[base + p, k] = side_ref[p, at]
             for p in range(halo):
-                halo_ref[zs + p, k] = corner_ref[p, at]
+                got = corner_ref[p, at]
+                halo_ref[zs + p, k] = jnp.where(outside, jnp.zeros_like(got), got)
 
     for c in range(2):
         pl.when(core == c)(functools.partial(fill, c))
@@ -288,8 +292,13 @@
     store_parcel(out_ref, *merge(mine, parcel(got_ref, rows), rows))
 
 
-def merge_kernel(step, rows, own_ref, got_ref, out_ref):
-    low = (lax.axis_index("depth") // step) % 2 == 0
+def is_low(steps):
+    step = jnp.where((lax.axis_index("rows") & 1) == 0, steps[0], steps[1])
+    return (lax.axis_index("depth") & step) == 0
+
+
+def merge_kernel(steps, rows, own_ref, got_ref, out_ref):
+    low = is_low(steps)
 
     def go(a_ref, b_ref):
         store_parcel(out_ref, *merge(parcel(a_ref, rows), parcel(b_ref, rows), rows))
@@ -298,9 +307,9 @@
     pl.when(jnp.logical_not(low))(lambda: go(got_ref, own_ref))
 
 
-def last_merge_kernel(step, own_ref, got_ref, joined_ref, depth_ref):
+def last_merge_kernel(steps, own_ref, got_ref, joined_ref, depth_ref):
     rows = joined_ref.shape[0]
-    low = (lax.axis_index("depth") // step) % 2 == 0
+    low = is_low(steps)
 
     def go(a_ref, b_ref):
         feats, _, total, depth = merge(parcel(a_ref, rows), parcel(b_ref, rows), rows)
@@ -346,8 +355,8 @@
         flops=10**8, nbytes=10**6,
     )
 
-    core = lax.axis_index("rows") % 2
-    col = lax.axis_index("rows") // 2
+    core = (lax.axis_index("rows") & 1)
+    col = (lax.axis_index("rows") >> 1)
     lower = core == 0
     beside = move(volume, lambda d, r: (d, r ^ 1))
     prior_beside = move(prior, lambda d, r: (d, r ^ 1))
@@ -374,12 +383,20 @@
     )
     top_high = jnp.where(lower, own_high, sib_high)
     bottom_low = jnp.where(lower, sib_low, own_low)
-    up = lambda d, r: (d + 1, r ^ 1) if r % 2 else (d - 1, r ^ 1)
+
+    def up(d, r):
+        to = d + 1 if r % 2 else d - 1
+        return (to, r ^ 1) if 0 <= to < depth else (d, r ^ 2)
+
+    def up_across(d, r):
+        to = d + 1 if r % 2 else d - 1
+        return (to, r ^ 3) if 0 <= to < depth else (d, r ^ 2)
+
     zh = move(edge, up)
     pay = jnp.where(col == 0, bottom_low, top_high)
     corner = jnp.where(lower, pay[:half], pay[half:])
     side = move(pay, lambda d, r: (d, r ^ 2))
-    corner = move(corner, lambda d, r: (up(d, r)[0], r ^ 3))
+    corner = move(corner, up_across)
 
     parcel_shape = (rows * (chans + 6), width)
     stats_shape = (3, rows, width)
@@ -409,18 +426,19 @@
     )
     got = move(send, lambda d, r: (d, r ^ 1))
     (sums,) = call(first_merge_kernel, [(parcel_shape, BF16)], keep, stat, got)
-    step = 1
-    while step < depth:
-        got = move(sums, lambda d, r: (d ^ step, r))
-        if 2 * step < depth:
-            (sums,) = call(functools.partial(merge_kernel, step, rows), [(parcel_shape, BF16)], sums, got)
+    order = [1 << k for k in range(depth.bit_length() - 1)]
+    for k, steps in enumerate(zip(order[::-1], order)):
+        got = move(sums, lambda d, r: (d ^ steps[r & 1], r))
+        if k + 1 < len(order):
+            (sums,) = call(
+                functools.partial(merge_kernel, steps, rows), [(parcel_shape, BF16)], sums, got
+            )
         else:
             joined, depth_estimate = call(
-                functools.partial(last_merge_kernel, step),
+                functools.partial(last_merge_kernel, steps),
                 [((rows, chans, width), F32), ((rows, width), F32)],
                 sums, got,
             )
-        step *= 2
     return joined, depth_estimate
 
 

time: 31.2 us -> 28.3 us (0.907)
  starting transfers between devices: 15.6 us -> 7.97 us
  waiting for transfers between devices: 7.88 us -> 12.6 us
    ppermute x8, starting transfers between devices: 15.6 us -> 7.97 us  [exchange(): return lax.ppermute(value, AXES, pairs)]
    ppermute x8, waiting for transfers between devices: 7.88 us -> 12.6 us  [exchange(): return lax.ppermute(value, AXES, pairs)]
  transfers between devices with their start and end apart: 8 -> 8, of which waited for: 3 -> 4; matrix products, arithmetic and copies ran while one was open for 0% -> 0% of each run, Pallas kernels for 7% -> 8%
where the time goes in v5:
time: 28.3 us; the launch traced here: 28.1 us
  waiting for transfers between devices  12.6 us (45%)
  starting transfers between devices  7.97 us (28%)
  Pallas kernels  3.83 us (14%)
  local copies, waits for them, and re-layouts  2.8 us (10%)
  between operations  0.75 us (3%)
    ppermute x8, waiting for transfers between devices, exchange(): return lax.ppermute(value, AXES, pairs)  12.6 us
    ppermute x8, starting transfers between devices, exchange(): return lax.ppermute(value, AXES, pairs)  7.97 us
    pallas_call x7, Pallas kernels, call(): pl.pallas_call(kernel, out_shape=[jax.ShapeDtypeStruct(s, t) for s, t in...  3.83 us
    unnamed x12, local copies, waits for them, and re-layouts  2.8 us
  transfers between devices with their start and end apart: 8, of which 4 were waited for; matrix products, arithmetic and copies ran while one was open for 0% of the time, Pallas kernels for 8%

profile of v5, /device:TPU:0, one launch (start us, length us, event | category | flops | bytes accessed | tf_op | source)
XLA Modules:
  0.0 28.1 jit_solution(15251081870762172611)
XLA Ops:
  0.6 0.6 %collective-permute-start = (bf16[4,8,32,128]{3,2,1,0:T(8,128)(2,1)}, bf16[4,8,32,128]{3,2,1,0:T(8,128)(2,1)S(1)}, u32[]{:S(2)}, u32[]{:S(2)}) collective-permute-start(bf16[4,8,32,128]{3,2,1,0:T(8,128)(2,1)} %own_ref.1), channel_id=1, source_target_pairs={{0,1},{1,0},{2,3},{3,2},{4,5},{5,4},{6,7},{7,6},{8,9},{9,8},{10,11... | collective-permute-start | bytes 786440 | tf_op jit(solution)/shard_map/ppermute | solution.py:25
  1.2 0.1 collective-permute-start.1
  1.3 0.0 copy-start
  1.3 0.9 %copy-done = bf16[4,8,32,128]{3,2,1,0:T(8,128)(2,1)S(1)} copy-done((bf16[4,8,32,128]{3,2,1,0:T(8,128)(2,1)S(1)}, bf16[4,8,32,128]{3,2,1,0:T(8,128)(2,1)}, u32[]{:S(2)}) %copy-start) | copy-done | bytes 262168
  2.2 0.0 copy-start.2
  2.3 0.0 copy-start.4
  2.3 0.9 %copy-done.2 = bf16[3,3,3,32,32]{4,3,2,1,0:T(8,128)(2,1)S(1)} copy-done((bf16[3,3,3,32,32]{4,3,2,1,0:T(8,128)(2,1)S(1)}, bf16[3,3,3,32,32]{4,3,2,1,0:T(8,128)(2,1)}, u32[]{:S(2)}) %copy-start.2) | copy-done | bytes 55320
  3.2 0.0 copy-done.4
  3.2 0.0 copy-start.3
  3.2 0.9 %copy-done.3 = bf16[3,3,3,32,32]{4,3,2,1,0:T(8,128)(2,1)S(1)} copy-done((bf16[3,3,3,32,32]{4,3,2,1,0:T(8,128)(2,1)S(1)}, bf16[3,3,3,32,32]{4,3,2,1,0:T(8,128)(2,1)}, u32[]{:S(2)}) %copy-start.3) | copy-done | bytes 55320
  4.1 0.4 %shard_map.69 = (bf16[192,384]{1,0:T(8,128)(2,1)S(1)}, bf16[192,384]{1,0:T(8,128)(2,1)S(1)}, f32[32,128]{1,0:T(8,128)S(1)}) custom-call(bf16[3,3,3,32,32]{4,3,2,1,0:T(8,128)(2,1)S(1)} %copy-done.2, bf16[3,3,3,32,32]{4,3,2,1,0:T(8,128)(2,1)S(1)} %copy-done.3, f32[1,32]{1,0:T(1,128)S(1)} %bitcast.1), custom_call_target="tpu_custom_call" | custom-call | flops 100000000 | bytes 1000000 | tf_op jit(solution)/shard_map/pallas_call | solution.py:326
  4.5 0.0 collective-permute-done.1.sp_ref
  4.5 0.0 collective-permute-done.sib_ref
  4.5 0.0 copy-start.1
  4.6 3.0 %collective-permute-start.4 = (bf16[2,16,32,128]{3,2,1,0:T(8,128)(2,1)S(1)}, bf16[2,16,32,128]{3,2,1,0:T(8,128)(2,1)S(1)}, u32[]{:S(2)}, u32[]{:S(2)}) collective-permute-start(bf16[2,16,32,128]{3,2,1,0:T(8,128)(2,1)S(1)} %maximum_select_fusion), channel_id=1, source_target_pairs={{0,2},{1,4},{2,0},{3,6},{4,1},{5,8},{6,3},{7,10},{8,5},{9,12},{10,... | collective-permute-start | bytes 786440 | tf_op jit(solution)/shard_map/ppermute | solution.py:25
  7.6 0.0 copy-start.5
  7.6 0.1 collective-permute-start.2
  7.7 2.0 %collective-permute-start.3 = (bf16[2,2,32,128]{3,2,1,0:T(8,128)(2,1)S(1)}, bf16[2,2,32,128]{3,2,1,0:T(8,128)(2,1)S(1)}, u32[]{:S(2)}, u32[]{:S(2)}) collective-permute-start(bf16[2,2,32,128]{3,2,1,0:T(8,128)(2,1)S(1)} %slice_select_fusion.1), channel_id=1, source_target_pairs={{0,2},{1,6},{2,0},{3,4},{4,3},{5,10},{6,1},{7,8},{8,7},{9,14},{10,... | collective-permute-start | bytes 98312 | tf_op jit(solution)/shard_map/ppermute | solution.py:25
  9.7 2.9 %collective-permute-done.4.zh_ref = bf16[2,16,32,128]{3,2,1,0:T(8,128)(2,1)S(1)} collective-permute-done((bf16[2,16,32,128]{3,2,1,0:T(8,128)(2,1)S(1)}, bf16[2,16,32,128]{3,2,1,0:T(8,128)(2,1)S(1)}, u32[]{:S(2)}, u32[]{:S(2)}) %collective-permute-start.4) | collective-permute-done | bytes 262176 | tf_op jit(solution)/shard_map/ppermute | solution.py:25
  12.6 0.0 copy-done.1
  12.6 0.0 copy-done.5
  12.6 1.9 %shard_map.70 = (bf16[6,10,32,256]{3,2,1,0:T(8,128)(2,1)S(1)}, bf16[4,9,32,256]{3,2,1,0:T(8,128)(2,1)S(1)}, f32[2,2,8,128]{3,2,1,0:T(8,128)S(1)}, f32[2,8,32,128]{3,2,1,0:T(8,128)S(1)}, f32[2,3,8,128]{3,2,1,0:T(8,128)S(1)}) custom-call(bf16[4,8,32,128]{3,2,1,0:T(8,128)(2,1)S(1)} %copy-done.1, bf16[4,8,32,128]{3,2,1,0:T(8,128)(2,1)S(1)} %collective-permute-done.sib_ref, ...), custom_call_target="tpu_custom_call" | custom-call | flops 500000000 | bytes 1000000 | tf_op jit(solution)/shard_map/pallas_call | solution.py:326
  14.5 0.0 collective-permute-done.3.corner_ref
  14.5 0.0 collective-permute-done.2.side_ref
  14.5 0.8 %shard_map.71 = (f32[8,32,128]{2,1,0:T(8,128)S(1)}, f32[3,8,128]{2,1,0:T(8,128)S(1)}, bf16[304,128]{1,0:T(8,128)(2,1)S(1)}) custom-call(bf16[4,2,32,128]{3,2,1,0:T(8,128)(2,1)S(1)} %collective-permute-done.2.side_ref, bf16[2,2,32,128]{3,2,1,0:T(8,128)(2,1)S(1)} %collective-permute-done.3.corner_ref, bf16[6,10,32,256]{3,2,1,0:T(8,128)(2,1)S(1)} %get-tuple-element.26.xs_ref, ...), custom_call_target="tpu_custom_call" | custom-call | flops 100000000 | bytes 1000000 | tf_op jit(solution)/shard_map/pallas_call | solution.py:326
  15.3 0.1 collective-permute-start.5
  15.4 1.3 %collective-permute-done.5.got_ref = bf16[304,128]{1,0:T(8,128)(2,1)S(1)} collective-permute-done((bf16[304,128]{1,0:T(8,128)(2,1)S(1)}, bf16[304,128]{1,0:T(8,128)(2,1)S(1)}, u32[]{:S(2)}, u32[]{:S(2)}) %collective-permute-start.5) | collective-permute-done | bytes 77856 | tf_op jit(solution)/shard_map/ppermute | solution.py:25
  16.7 1.9 %collective-permute-start.6 = (bf16[304,128]{1,0:T(8,128)(2,1)S(1)}, bf16[304,128]{1,0:T(8,128)(2,1)S(1)}, u32[]{:S(2)}, u32[]{:S(2)}) collective-permute-start(bf16[304,128]{1,0:T(8,128)(2,1)S(1)} %shard_map.72.own_ref), channel_id=1, source_target_pairs={{0,8},{1,5},{2,10},{3,7},{4,12},{5,1},{6,14},{7,3},{8,0},{9,13},{1... | collective-permute-start | bytes 233480 | tf_op jit(solution)/shard_map/ppermute | solution.py:25
  18.6 4.3 %collective-permute-done.6.got_ref = bf16[304,128]{1,0:T(8,128)(2,1)S(1)} collective-permute-done((bf16[304,128]{1,0:T(8,128)(2,1)S(1)}, bf16[304,128]{1,0:T(8,128)(2,1)S(1)}, u32[]{:S(2)}, u32[]{:S(2)}) %collective-permute-start.6) | collective-permute-done | bytes 77856 | tf_op jit(solution)/shard_map/ppermute | solution.py:25
  22.9 0.3 %collective-permute-start.7 = (bf16[304,128]{1,0:T(8,128)(2,1)S(1)}, bf16[304,128]{1,0:T(8,128)(2,1)S(1)}, u32[]{:S(2)}, u32[]{:S(2)}) collective-permute-start(bf16[304,128]{1,0:T(8,128)(2,1)S(1)} %shard_map.73.own_ref), channel_id=1, source_target_pairs={{0,4},{1,9},{2,6},{3,11},{4,0},{5,13},{6,2},{7,15},{8,12},{9,1},{1... | collective-permute-start | bytes 233480 | tf_op jit(solution)/shard_map/ppermute | solution.py:25
  23.2 4.2 %collective-permute-done.7.got_ref = bf16[304,128]{1,0:T(8,128)(2,1)S(1)} collective-permute-done((bf16[304,128]{1,0:T(8,128)(2,1)S(1)}, bf16[304,128]{1,0:T(8,128)(2,1)S(1)}, u32[]{:S(2)}, u32[]{:S(2)}) %collective-permute-start.7) | collective-permute-done | bytes 77856 | tf_op jit(solution)/shard_map/ppermute | solution.py:25
  27.4 0.7 %shard_map.74 = (f32[8,32,128]{2,1,0:T(8,128)}, f32[8,128]{1,0:T(8,128)}) custom-call(bf16[304,128]{1,0:T(8,128)(2,1)S(1)} %shard_map.73.own_ref, bf16[304,128]{1,0:T(8,128)(2,1)S(1)} %collective-permute-done.7.got_ref), custom_call_target="tpu_custom_call" | custom-call | tf_op jit(solution)/shard_map/pallas_call | solution.py:326
  (7 shorter events, 0.2 us)
Async XLA Ops:
  0.6 3.9 %collective-permute-start = (bf16[4,8,32,128]{3,2,1,0:T(8,128)(2,1)}, bf16[4,8,32,128]{3,2,1,0:T(8,128)(2,1)S(1)}, u32[]{:S(2)}, u32[]{:S(2)}) collective-permute-start(bf16[4,8,32,128]{3,2,1,0:T(8,128)(2,1)} %own_ref.1), channel_id=1, source_target_pairs={{0,1},{1,0},{2,3},{3,2},{4,5},{5,4},{6,7},{7,6},{8,9},{9,8},{10,11... | collective-permute-start | bytes 786440 | tf_op jit(solution)/shard_map/ppermute | solution.py:25
  1.2 3.3 %collective-permute-start.1 = (f32[4,8,128]{2,1,0:T(8,128)}, f32[4,8,128]{2,1,0:T(8,128)S(1)}, u32[]{:S(2)}, u32[]{:S(2)}) collective-permute-start(f32[4,8,128]{2,1,0:T(8,128)} %op_ref.1), channel_id=1, source_target_pairs={{0,1},{1,0},{2,3},{3,2},{4,5},{5,4},{6,7},{7,6},{8,9},{9,8},{10,11... | collective-permute-start | bytes 49160 | tf_op jit(solution)/shard_map/ppermute | solution.py:25
  1.3 0.9 %copy-start = (bf16[4,8,32,128]{3,2,1,0:T(8,128)(2,1)S(1)}, bf16[4,8,32,128]{3,2,1,0:T(8,128)(2,1)}, u32[]{:S(2)}) copy-start(bf16[4,8,32,128]{3,2,1,0:T(8,128)(2,1)} %own_ref.1) | copy-start | bytes 786436
  2.2 0.9 %copy-start.2 = (bf16[3,3,3,32,32]{4,3,2,1,0:T(8,128)(2,1)S(1)}, bf16[3,3,3,32,32]{4,3,2,1,0:T(8,128)(2,1)}, u32[]{:S(2)}) copy-start(bf16[3,3,3,32,32]{4,3,2,1,0:T(8,128)(2,1)} %k1_ref.1) | copy-start | bytes 165892
  2.3 0.9 %copy-start.4 = (f32[32]{0:T(128)S(1)}, f32[32]{0:T(128)}, u32[]{:S(2)}) copy-start(f32[32]{0:T(128)} %param.9) | copy-start | bytes 388
  3.2 0.9 %copy-start.3 = (bf16[3,3,3,32,32]{4,3,2,1,0:T(8,128)(2,1)S(1)}, bf16[3,3,3,32,32]{4,3,2,1,0:T(8,128)(2,1)}, u32[]{:S(2)}) copy-start(bf16[3,3,3,32,32]{4,3,2,1,0:T(8,128)(2,1)} %k2_ref.1) | copy-start | bytes 165892
  4.5 8.0 %copy-start.1 = (bf16[4,8,32,128]{3,2,1,0:T(8,128)(2,1)S(1)}, bf16[4,8,32,128]{3,2,1,0:T(8,128)(2,1)}, u32[]{:S(2)}) copy-start(bf16[4,8,32,128]{3,2,1,0:T(8,128)(2,1)} %own_ref.1) | copy-start | bytes 786436
  4.6 8.0 %collective-permute-start.4 = (bf16[2,16,32,128]{3,2,1,0:T(8,128)(2,1)S(1)}, bf16[2,16,32,128]{3,2,1,0:T(8,128)(2,1)S(1)}, u32[]{:S(2)}, u32[]{:S(2)}) collective-permute-start(bf16[2,16,32,128]{3,2,1,0:T(8,128)(2,1)S(1)} %maximum_select_fusion), channel_id=1, source_target_pairs={{0,2},{1,4},{2,0},{3,6},{4,1},{5,8},{6,3},{7,10},{8,5},{9,12},{10,... | collective-permute-start | bytes 786440 | tf_op jit(solution)/shard_map/ppermute | solution.py:25
  7.6 5.0 %copy-start.5 = (f32[4,8,128]{2,1,0:T(8,128)S(1)}, f32[4,8,128]{2,1,0:T(8,128)}, u32[]{:S(2)}) copy-start(f32[4,8,128]{2,1,0:T(8,128)} %op_ref.1) | copy-start | bytes 49156
  7.6 6.9 %collective-permute-start.2 = (bf16[4,2,32,128]{3,2,1,0:T(8,128)(2,1)S(1)}, bf16[4,2,32,128]{3,2,1,0:T(8,128)(2,1)S(1)}, u32[]{:S(2)}, u32[]{:S(2)}) collective-permute-start(bf16[4,2,32,128]{3,2,1,0:T(8,128)(2,1)S(1)} %select_select_fusion), channel_id=1, source_target_pairs={{0,2},{1,3},{2,0},{3,1},{4,6},{5,7},{6,4},{7,5},{8,10},{9,11},{10,... | collective-permute-start | bytes 196616 | tf_op jit(solution)/shard_map/ppermute | solution.py:25
  7.7 6.8 %collective-permute-start.3 = (bf16[2,2,32,128]{3,2,1,0:T(8,128)(2,1)S(1)}, bf16[2,2,32,128]{3,2,1,0:T(8,128)(2,1)S(1)}, u32[]{:S(2)}, u32[]{:S(2)}) collective-permute-start(bf16[2,2,32,128]{3,2,1,0:T(8,128)(2,1)S(1)} %slice_select_fusion.1), channel_id=1, source_target_pairs={{0,2},{1,6},{2,0},{3,4},{4,3},{5,10},{6,1},{7,8},{8,7},{9,14},{10,... | collective-permute-start | bytes 98312 | tf_op jit(solution)/shard_map/ppermute | solution.py:25
  15.3 1.3 %collective-permute-start.5 = (bf16[304,128]{1,0:T(8,128)(2,1)S(1)}, bf16[304,128]{1,0:T(8,128)(2,1)S(1)}, u32[]{:S(2)}, u32[]{:S(2)}) collective-permute-start(bf16[304,128]{1,0:T(8,128)(2,1)S(1)} %get-tuple-element.33), channel_id=1, source_target_pairs={{0,1},{1,0},{2,3},{3,2},{4,5},{5,4},{6,7},{7,6},{8,9},{9,8},{10,11... | collective-permute-start | bytes 233480 | tf_op jit(solution)/shard_map/ppermute | solution.py:25
  16.7 6.2 %collective-permute-start.6 = (bf16[304,128]{1,0:T(8,128)(2,1)S(1)}, bf16[304,128]{1,0:T(8,128)(2,1)S(1)}, u32[]{:S(2)}, u32[]{:S(2)}) collective-permute-start(bf16[304,128]{1,0:T(8,128)(2,1)S(1)} %shard_map.72.own_ref), channel_id=1, source_target_pairs={{0,8},{1,5},{2,10},{3,7},{4,12},{5,1},{6,14},{7,3},{8,0},{9,13},{1... | collective-permute-start | bytes 233480 | tf_op jit(solution)/shard_map/ppermute | solution.py:25
  22.9 4.5 %collective-permute-start.7 = (bf16[304,128]{1,0:T(8,128)(2,1)S(1)}, bf16[304,128]{1,0:T(8,128)(2,1)S(1)}, u32[]{:S(2)}, u32[]{:S(2)}) collective-permute-start(bf16[304,128]{1,0:T(8,128)(2,1)S(1)} %shard_map.73.own_ref), channel_id=1, source_target_pairs={{0,4},{1,9},{2,6},{3,11},{4,0},{5,13},{6,2},{7,15},{8,12},{9,1},{1... | collective-permute-start | bytes 233480 | tf_op jit(solution)/shard_map/ppermute | solution.py:25

commit v6 on v5

--- a/solution.py
+++ b/solution.py
@@ -11,6 +11,7 @@
 F32 = jnp.float32
 BF16 = jnp.bfloat16
 AXES = ("depth", "rows")
+STATS = 6
 VMEM = pl.BlockSpec(memory_space=pltpu.VMEM)
 
 
@@ -94,22 +95,20 @@
 
 
 def load_stats(ref, rows):
-    flat = ref[ref.shape[0] - 6 * rows :].astype(F32)
-    flat = [flat[k * rows : (k + 1) * rows] for k in range(6)]
+    flat = ref[ref.shape[0] - STATS * rows :].astype(F32)
+    flat = [flat[k * rows : (k + 1) * rows] for k in range(STATS)]
     return ((flat[0] + flat[1]) + flat[2]) * 2.0, flat[3] + flat[4], flat[5]
 
 
-def first_layer(w, x, half, chans, first_plane, g, all_planes, store):
+def first_layer(w, x, half, chans, outside, store):
     lo, hi = shifted_sum(jnp.dot(w, x, preferred_element_type=F32), half * chans)
     for p in range(half):
         part = slice(p * chans, (p + 1) * chans)
         a, b = jnp.maximum(lo[part], 0.0), jnp.maximum(hi[part], 0.0)
-        if g + p == 0 or g + p == half + 1:
-            plane = first_plane + g + p
-            outside = jnp.logical_or(plane < 0, plane >= all_planes)
-            a = jnp.where(outside, 0.0, a)
-            b = jnp.where(outside, 0.0, b)
-        store(g + p, a.astype(BF16), b.astype(BF16))
+        if outside is not None:
+            a = jnp.where(outside[p], 0.0, a)
+            b = jnp.where(outside[p], 0.0, b)
+        store(p, a.astype(BF16), b.astype(BF16))
 
 
 def second_layer(w, x, pb, ps_ref, fracs, two_rows, over, feat_ref, stat_ref):
@@ -137,97 +136,120 @@
 
 def place_of(depth, planes):
     half = planes // 2
-    core = (lax.axis_index("rows") & 1)
+    d = lax.axis_index("depth")
+    core = lax.axis_index("rows") & 1
     over = (lax.axis_index("rows") >> 1) == 1
-    first_plane = lax.axis_index("depth") * planes + core * half - 1
-    all_planes = depth * planes
-    fracs = [((first_plane + 1 + p).astype(F32) + 0.5) / all_planes for p in range(half)]
-    return core, over, first_plane, all_planes, fracs
-
-
-def inner_kernel(
-    depth, own_ref, sib_ref, zh_ref, op_ref, sp_ref, w1_ref, w2_ref, pb_ref,
-    xs_ref, fs_ref, ps_ref, feat_ref, stat_ref,
-):
-    planes, rows, chans, width = own_ref.shape
-    half = planes // 2
-    halo = 2
-    both = 2 * rows
-    lead = rows - 1
-    core, over, first_plane, all_planes, fracs = place_of(depth, planes)
-    left = slice(0, width)
-    right = slice(width, 2 * width)
-
-    def fill(c, flip):
-        blocks = (own_ref, sib_ref) if c == 0 else (sib_ref, own_ref)
-        base = halo * (1 - c)
-        mine = slice(base, base + planes)
-        zs = slice(0, halo) if c == 0 else slice(planes, planes + halo)
-        outside = lax.axis_index("depth") == (0 if c == 0 else depth - 1)
-        zero_planes = jnp.zeros((halo, chans, width), BF16)
-        for cols, start in ((left, -1), (right, lead - 1)):
-            for slot in range(rows + 2):
-                row = start + slot
-                if row < 0:
-                    xs_ref[:, slot, :, cols] = jnp.zeros((planes + halo, chans, width), BF16)
-                    continue
-                row = both - 1 - row if flip else row
-                xs_ref[mine, slot, :, cols] = blocks[row // rows][:, row % rows]
-                xs_ref[zs, slot, :, cols] = jnp.where(outside, zero_planes, zh_ref[:, row])
-        mine_p = slice(half * c, half * c + half)
-        priors = (op_ref, sp_ref) if c == 0 else (sp_ref, op_ref)
-        for k in range(2):
-            ps_ref[k] = priors[1 - k if flip else k][mine_p]
-
+    fracs = [
+        ((d * planes + core * half + p).astype(F32) + 0.5) / (depth * planes) for p in range(half)
+    ]
+    first, last = d == 0, d == depth - 1
+    outside = [jnp.logical_and(core == 0, first)] + [False] * (half - 2)
+    outside = outside + [jnp.logical_and(core == 1, last)]
+    return core, over, fracs, outside
+
+
+def by_place(core, over, fill):
     for c in range(2):
         for flip in (False, True):
             pl.when(jnp.logical_and(core == c, over == flip))(functools.partial(fill, c, flip))
 
-    deep = (half + 2) * 3 * chans
-    w1 = w1_ref[...]
-    fs_ref[:, 0, :, left] = jnp.zeros((half + 2, chans, width), BF16)
-    for g in range(0, half + 2, half):
-        for i in range(rows):
-            def store(j, a, b, i=i):
-                fs_ref[j, i + 1, :, left] = a
-                fs_ref[j, i + 1, :, right] = b
-                if i == lead - 1:
-                    fs_ref[j, 0, :, right] = a
-
-            x = xs_ref[g : g + half + 2, i : i + 3].reshape(deep, 2 * width)
-            first_layer(w1, x, half, chans, first_plane, g, all_planes, store)
-
+
+def fill_rows(ref, to, source, planes, rows, flip):
+    chans, width = ref.shape[2], ref.shape[3] // 2
+    for cols, start in ((slice(0, width), -1), (slice(width, 2 * width), rows - 2)):
+        for slot in range(rows + 2):
+            row = start + slot
+            if row < 0:
+                ref[to, slot, :, cols] = jnp.zeros((planes, chans, width), BF16)
+            else:
+                ref[to, slot, :, cols] = source(2 * rows - 1 - row if flip else row)
+
+
+def first_rows(w, x_ref, half, rows, outside, fs_ref, base):
+    chans, wide = x_ref.shape[2:]
+    left, right = slice(0, wide // 2), slice(wide // 2, wide)
+    for p in range(half):
+        fs_ref[base + p, 0, :, left] = jnp.zeros((chans, wide // 2), BF16)
+    for i in range(rows):
+        def store(p, a, b, i=i):
+            fs_ref[base + p, i + 1, :, left] = a
+            fs_ref[base + p, i + 1, :, right] = b
+            if i == rows - 2:
+                fs_ref[base + p, 0, :, right] = a
+
+        x = x_ref[:, i : i + 3].reshape(-1, wide)
+        first_layer(w, x, half, chans, outside, store)
+
+
+def own_kernel(depth, own_ref, sib_ref, op_ref, sp_ref, w1_ref, xo_ref, fo_ref, ps_ref):
+    planes, rows, _, _ = own_ref.shape
+    half = planes // 2
+    core, over, _, _ = place_of(depth, planes)
+
+    def fill(c, flip):
+        blocks = (own_ref, sib_ref) if c == 0 else (sib_ref, own_ref)
+        fill_rows(
+            xo_ref, slice(0, planes), lambda row: blocks[row // rows][:, row % rows],
+            planes, rows, flip,
+        )
+        priors = (op_ref, sp_ref) if c == 0 else (sp_ref, op_ref)
+        for k in range(2):
+            ps_ref[k] = priors[1 - k if flip else k][half * c : half * c + half]
+
+    by_place(core, over, fill)
+    first_rows(w1_ref[...], xo_ref, half, rows, None, fo_ref, 0)
+
+
+def inner_kernel(
+    depth, zh_ref, xo_ref, fo_ref, ps_ref, w1_ref, w2_ref, pb_ref,
+    xz_ref, fs_ref, feat_ref, stat_ref,
+):
+    half = zh_ref.shape[0]
+    planes = xo_ref.shape[0]
+    rows = xo_ref.shape[1] - 2
+    wide = xo_ref.shape[3]
+    lead = rows - 1
+    core, over, fracs, outside = place_of(depth, planes)
+    ends = jnp.logical_or(outside[0], outside[-1])
+
+    def fill(c, flip):
+        theirs, mine = slice(half * c, half * c + half), slice(half * (1 - c), half * (2 - c))
+        xz_ref[mine] = xo_ref[theirs]
+        fs_ref[mine] = fo_ref[...]
+        fill_rows(
+            xz_ref, theirs,
+            lambda row: jnp.where(ends, jnp.zeros_like(zh_ref[:, row]), zh_ref[:, row]),
+            half, rows, flip,
+        )
+
+    by_place(core, over, fill)
+    first_rows(w1_ref[...], xz_ref, half, rows, outside, fs_ref, core * half)
     w2 = w2_ref[...]
     pb = pb_ref[...]
     for i in range(lead):
-        x = fs_ref[:, i : i + 3].reshape(deep, 2 * width)
+        x = fs_ref[:, i : i + 3].reshape(-1, wide)
         second_layer(w2, x, pb, ps_ref, fracs, (i, i + lead), over, feat_ref, stat_ref)
 
 
 def outer_kernel(
-    depth, side_ref, corner_ref, xs_ref, fs_ref, ps_ref, fi_ref, ti_ref, w1_ref, w2_ref, pb_ref,
-    keep_ref, stat_ref, send_ref, halo_ref, late_ref, feat_ref, all_ref,
+    depth, side_ref, corner_ref, xo_ref, ps_ref, xz_ref, fs_ref, fi_ref, ti_ref, w1_ref, w2_ref,
+    pb_ref, keep_ref, stat_ref, send_ref, own_halo_ref, halo_ref, late_ref, feat_ref, all_ref,
 ):
     planes, halo, chans, width = side_ref.shape
     half = planes // 2
     rows = keep_ref.shape[0]
-    core, over, first_plane, all_planes, fracs = place_of(depth, planes)
+    core, over, fracs, outside = place_of(depth, planes)
+    ends = jnp.logical_or(outside[0], outside[-1])
     right = slice(width, 2 * width)
 
-    def fill(c):
-        base = halo * (1 - c)
-        zs = 0 if c == 0 else planes
-        outside = lax.axis_index("depth") == (0 if c == 0 else depth - 1)
-        for k in range(halo):
-            at = jnp.where(over, halo - 1 - k, k)
-            for p in range(planes):
-                halo_ref[base + p, k] = side_ref[p, at]
-            for p in range(halo):
-                got = corner_ref[p, at]
-                halo_ref[zs + p, k] = jnp.where(outside, jnp.zeros_like(got), got)
-
-    for c in range(2):
-        pl.when(core == c)(functools.partial(fill, c))
+    for k in range(halo):
+        at = jnp.where(over, halo - 1 - k, k)
+        for p in range(planes):
+            own_halo_ref[p, k] = side_ref[p, at]
+        for p in range(half):
+            got = corner_ref[p, at]
+            halo_ref[core * half + p, k] = jnp.where(ends, jnp.zeros_like(got), got)
+            halo_ref[(1 - core) * half + p, k] = side_ref[core * half + p, at]
 
     def pair(parts):
         return jnp.concatenate(
@@ -235,20 +257,22 @@
         )
 
     w1 = w1_ref[...]
-    for g in range(0, half + 2, half):
-        span = slice(g, g + half + 2)
+    for x_ref, h_ref, mask, base in (
+        (xo_ref, own_halo_ref, None, (1 - core) * half),
+        (xz_ref, halo_ref, outside, core * half),
+    ):
         x = pair(
             [
-                [xs_ref[span, rows:, :, right], halo_ref[span, :1]],
-                [xs_ref[span, rows + 1 :, :, right], halo_ref[span]],
+                [x_ref[:, rows:, :, right], h_ref[:, :1]],
+                [x_ref[:, rows + 1 :, :, right], h_ref[...]],
             ]
         )
 
-        def store(j, a, b):
-            late_ref[j, 0] = a
-            late_ref[j, 1] = b
-
-        first_layer(w1, x, half, chans, first_plane, g, all_planes, store)
+        def store(p, a, b):
+            late_ref[base + p, 0] = a
+            late_ref[base + p, 1] = b
+
+        first_layer(w1, x, half, chans, mask, store)
 
     feat_ref[...] = fi_ref[...]
     all_ref[...] = ti_ref[...]
@@ -282,7 +306,7 @@
 
 
 def parcel(ref, rows):
-    chans = ref.shape[0] // rows - 6
+    chans = ref.shape[0] // rows - STATS
     return (lambda i: ref[i * chans : (i + 1) * chans].astype(F32)), load_stats(ref, rows)
 
 
@@ -292,34 +316,45 @@
     store_parcel(out_ref, *merge(mine, parcel(got_ref, rows), rows))
 
 
-def is_low(steps):
-    step = jnp.where((lax.axis_index("rows") & 1) == 0, steps[0], steps[1])
-    return (lax.axis_index("depth") & step) == 0
-
-
-def merge_kernel(steps, rows, own_ref, got_ref, out_ref):
-    low = is_low(steps)
-
-    def go(a_ref, b_ref):
-        store_parcel(out_ref, *merge(parcel(a_ref, rows), parcel(b_ref, rows), rows))
-
-    pl.when(low)(lambda: go(own_ref, got_ref))
-    pl.when(jnp.logical_not(low))(lambda: go(got_ref, own_ref))
-
-
-def last_merge_kernel(steps, own_ref, got_ref, joined_ref, depth_ref):
+def merge_group(step, refs, rows, finish):
+    def go(me):
+        parts = [parcel(refs[me ^ j], rows) for j in range(len(refs))]
+        while True:
+            merged = [merge(a, b, rows) for a, b in zip(parts[::2], parts[1::2])]
+            if len(merged) == 1:
+                return finish(*merged[0])
+            parts = [(m[0].__getitem__, m[1:]) for m in merged]
+
+    place = (lax.axis_index("depth") // step) & (len(refs) - 1)
+    for me in range(len(refs)):
+        pl.when(place == me)(functools.partial(go, me))
+
+
+def merge_kernel(step, rows, *refs):
+    merge_group(step, refs[:-1], rows, functools.partial(store_parcel, refs[-1]))
+
+
+def last_merge_kernel(step, *refs):
+    joined_ref, depth_ref = refs[-2:]
     rows = joined_ref.shape[0]
-    low = is_low(steps)
-
-    def go(a_ref, b_ref):
-        feats, _, total, depth = merge(parcel(a_ref, rows), parcel(b_ref, rows), rows)
+
+    def finish(feats, peak, total, depth):
         inverse = 1.0 / total
         for i in range(rows):
             joined_ref[i] = feats[i] * inverse[i : i + 1]
         depth_ref[...] = depth * inverse
 
-    pl.when(low)(lambda: go(own_ref, got_ref))
-    pl.when(jnp.logical_not(low))(lambda: go(got_ref, own_ref))
+    merge_group(step, refs[:-2], rows, finish)
+
+
+def merge_rounds(depth):
+    rounds = []
+    step = 1
+    while step < depth:
+        count = 4 if step * 4 <= depth else 2
+        rounds.append((step, count))
+        step *= count
+    return rounds
 
 
 def call(kernel, outs, *args, scratch=(), flops=0, nbytes=0, room=4):
@@ -395,29 +430,40 @@
     zh = move(edge, up)
     pay = jnp.where(col == 0, bottom_low, top_high)
     corner = jnp.where(lower, pay[:half], pay[half:])
-    side = move(pay, lambda d, r: (d, r ^ 2))
+    side = move(pay, lambda d, r: (d, r ^ 3))
     corner = move(corner, up_across)
 
-    parcel_shape = (rows * (chans + 6), width)
+    parcel_shape = (rows * (chans + STATS), width)
     stats_shape = (3, rows, width)
+    block_shape = (planes, rows + 2, chans, 2 * width)
+    xo, fo, ps = call(
+        functools.partial(own_kernel, depth),
+        [
+            (block_shape, BF16),
+            ((half, rows + 1, chans, 2 * width), BF16),
+            ((2, half, rows, width), F32),
+        ],
+        volume, beside, prior, prior_beside, w1,
+        flops=2 * 10**8, nbytes=10**6, room=6,
+    )
     inside = call(
         functools.partial(inner_kernel, depth),
         [
-            ((planes + halo, rows + 2, chans, 2 * width), BF16),
+            (block_shape, BF16),
             ((half + 2, rows + 1, chans, 2 * width), BF16),
-            ((2, half, rows, width), F32),
             ((2, rows, chans, width), F32),
             ((2,) + stats_shape, F32),
         ],
-        volume, beside, zh, prior, prior_beside, w1, w2, pb,
+        zh, xo, fo, ps, w1, w2, pb,
         flops=5 * 10**8, nbytes=10**6, room=6,
     )
     keep, stat, send = call(
         functools.partial(outer_kernel, depth),
         [((rows, chans, width), F32), (stats_shape, F32), (parcel_shape, BF16)],
-        side, corner, *inside, w1, w2, pb,
+        side, corner, xo, ps, *inside, w1, w2, pb,
         scratch=[
-            pltpu.VMEM((planes + halo, halo, chans, width), BF16),
+            pltpu.VMEM((planes, halo, chans, width), BF16),
+            pltpu.VMEM((planes, halo, chans, width), BF16),
             pltpu.VMEM((half + 2, halo, chans, width), BF16),
             pltpu.VMEM((2, rows, chans, width), F32),
             pltpu.VMEM((2,) + stats_shape, F32),
@@ -426,19 +472,18 @@
     )
     got = move(send, lambda d, r: (d, r ^ 1))
     (sums,) = call(first_merge_kernel, [(parcel_shape, BF16)], keep, stat, got)
-    order = [1 << k for k in range(depth.bit_length() - 1)]
-    for k, steps in enumerate(zip(order[::-1], order)):
-        got = move(sums, lambda d, r: (d ^ steps[r & 1], r))
-        if k + 1 < len(order):
+    rounds = merge_rounds(depth)
+    for step, count in rounds:
+        others = [move(sums, lambda d, r: (d ^ (k * step), r)) for k in range(1, count)]
+        if (step, count) != rounds[-1]:
             (sums,) = call(
-                functools.partial(merge_kernel, steps, rows), [(parcel_shape, BF16)], sums, got
+                functools.partial(merge_kernel, step, rows), [(parcel_shape, BF16)], sums, *others
             )
-        else:
-            joined, depth_estimate = call(
-                functools.partial(last_merge_kernel, steps),
-                [((rows, chans, width), F32), ((rows, width), F32)],
-                sums, got,
-            )
+    joined, depth_estimate = call(
+        functools.partial(last_merge_kernel, step),
+        [((rows, chans, width), F32), ((rows, width), F32)],
+        sums, *others,
+    )
     return joined, depth_estimate
 
 

time: 28.3 us -> 27 us (0.954)
  waiting for transfers between devices: 12.6 us -> 8.89 us
  starting transfers between devices: 7.97 us -> 10 us
  Pallas kernels: 3.83 us -> 4.23 us
    ppermute x8 -> x9, waiting for transfers between devices: 12.6 us -> 8.89 us  [exchange(): return lax.ppermute(value, AXES, pairs)]
    ppermute x8 -> x9, starting transfers between devices: 7.97 us -> 10 us  [exchange(): return lax.ppermute(value, AXES, pairs)]
    pallas_call x7, Pallas kernels: 3.83 us -> 4.23 us  [call(): pl.pallas_call(kernel, out_shape=[jax.ShapeDtypeStruct(s, t) for s, t in...]
  transfers between devices with their start and end apart: 8 -> 9, of which waited for: 4 -> 4; matrix products, arithmetic and copies ran while one was open for 0% -> 0% of each run, Pallas kernels for 8% -> 10%
where the time goes in v6:
time: 27 us; the launch traced here: 26.8 us
  starting transfers between devices  10 us (37%)
  waiting for transfers between devices  8.89 us (33%)
  Pallas kernels  4.23 us (16%)
  local copies, waits for them, and re-layouts  2.8 us (10%)
  between operations  0.75 us (3%)
    ppermute x9, starting transfers between devices, exchange(): return lax.ppermute(value, AXES, pairs)  10 us
    ppermute x9, waiting for transfers between devices, exchange(): return lax.ppermute(value, AXES, pairs)  8.89 us
    pallas_call x7, Pallas kernels, call(): pl.pallas_call(kernel, out_shape=[jax.ShapeDtypeStruct(s, t) for s, t in...  4.23 us
    unnamed x12, local copies, waits for them, and re-layouts  2.8 us
  transfers between devices with their start and end apart: 9, of which 4 were waited for; matrix products, arithmetic and copies ran while one was open for 0% of the time, Pallas kernels for 10%

profile of v6, /device:TPU:0, one launch (start us, length us, event | category | flops | bytes accessed | tf_op | source)
XLA Modules:
  0.0 26.8 jit_solution(10510116148194595373)
XLA Ops:
  0.6 0.6 %collective-permute-start = (bf16[4,8,32,128]{3,2,1,0:T(8,128)(2,1)}, bf16[4,8,32,128]{3,2,1,0:T(8,128)(2,1)S(1)}, u32[]{:S(2)}, u32[]{:S(2)}) collective-permute-start(bf16[4,8,32,128]{3,2,1,0:T(8,128)(2,1)} %own_ref.1), channel_id=1, source_target_pairs={{0,1},{1,0},{2,3},{3,2},{4,5},{5,4},{6,7},{7,6},{8,9},{9,8},{10,11... | collective-permute-start | bytes 786440 | tf_op jit(solution)/shard_map/ppermute | solution.py:26
  1.2 0.1 collective-permute-start.1
  1.3 0.0 copy-start
  1.3 0.9 %copy-done = bf16[4,8,32,128]{3,2,1,0:T(8,128)(2,1)S(1)} copy-done((bf16[4,8,32,128]{3,2,1,0:T(8,128)(2,1)S(1)}, bf16[4,8,32,128]{3,2,1,0:T(8,128)(2,1)}, u32[]{:S(2)}) %copy-start) | copy-done | bytes 262168
  2.2 0.0 copy-start.2
  2.3 0.0 copy-start.4
  2.3 0.9 %copy-done.2 = bf16[3,3,3,32,32]{4,3,2,1,0:T(8,128)(2,1)S(1)} copy-done((bf16[3,3,3,32,32]{4,3,2,1,0:T(8,128)(2,1)S(1)}, bf16[3,3,3,32,32]{4,3,2,1,0:T(8,128)(2,1)}, u32[]{:S(2)}) %copy-start.2) | copy-done | bytes 55320
  3.2 0.0 copy-done.4
  3.2 0.0 copy-start.3
  3.2 0.9 %copy-done.3 = bf16[3,3,3,32,32]{4,3,2,1,0:T(8,128)(2,1)S(1)} copy-done((bf16[3,3,3,32,32]{4,3,2,1,0:T(8,128)(2,1)S(1)}, bf16[3,3,3,32,32]{4,3,2,1,0:T(8,128)(2,1)}, u32[]{:S(2)}) %copy-start.3) | copy-done | bytes 55320
  4.1 0.4 %shard_map.69 = (bf16[192,384]{1,0:T(8,128)(2,1)S(1)}, bf16[192,384]{1,0:T(8,128)(2,1)S(1)}, f32[32,128]{1,0:T(8,128)S(1)}) custom-call(bf16[3,3,3,32,32]{4,3,2,1,0:T(8,128)(2,1)S(1)} %copy-done.2, bf16[3,3,3,32,32]{4,3,2,1,0:T(8,128)(2,1)S(1)} %copy-done.3, f32[1,32]{1,0:T(1,128)S(1)} %bitcast.1), custom_call_target="tpu_custom_call" | custom-call | flops 100000000 | bytes 1000000 | tf_op jit(solution)/shard_map/pallas_call | solution.py:361
  4.5 0.0 collective-permute-done.1.sp_ref
  4.5 0.0 collective-permute-done.sib_ref
  4.5 0.0 copy-start.1
  4.6 3.0 %collective-permute-start.4 = (bf16[2,16,32,128]{3,2,1,0:T(8,128)(2,1)S(1)}, bf16[2,16,32,128]{3,2,1,0:T(8,128)(2,1)S(1)}, u32[]{:S(2)}, u32[]{:S(2)}) collective-permute-start(bf16[2,16,32,128]{3,2,1,0:T(8,128)(2,1)S(1)} %maximum_select_fusion), channel_id=1, source_target_pairs={{0,2},{1,4},{2,0},{3,6},{4,1},{5,8},{6,3},{7,10},{8,5},{9,12},{10,... | collective-permute-start | bytes 786440 | tf_op jit(solution)/shard_map/ppermute | solution.py:26
  7.6 0.0 copy-start.5
  7.6 1.4 %collective-permute-start.2 = (bf16[4,2,32,128]{3,2,1,0:T(8,128)(2,1)S(1)}, bf16[4,2,32,128]{3,2,1,0:T(8,128)(2,1)S(1)}, u32[]{:S(2)}, u32[]{:S(2)}) collective-permute-start(bf16[4,2,32,128]{3,2,1,0:T(8,128)(2,1)S(1)} %select_select_fusion), channel_id=1, source_target_pairs={{0,3},{1,2},{2,1},{3,0},{4,7},{5,6},{6,5},{7,4},{8,11},{9,10},{10,... | collective-permute-start | bytes 196616 | tf_op jit(solution)/shard_map/ppermute | solution.py:26
  8.9 0.5 %collective-permute-start.3 = (bf16[2,2,32,128]{3,2,1,0:T(8,128)(2,1)S(1)}, bf16[2,2,32,128]{3,2,1,0:T(8,128)(2,1)S(1)}, u32[]{:S(2)}, u32[]{:S(2)}) collective-permute-start(bf16[2,2,32,128]{3,2,1,0:T(8,128)(2,1)S(1)} %slice_select_fusion.1), channel_id=1, source_target_pairs={{0,2},{1,6},{2,0},{3,4},{4,3},{5,10},{6,1},{7,8},{8,7},{9,14},{10,... | collective-permute-start | bytes 98312 | tf_op jit(solution)/shard_map/ppermute | solution.py:26
  9.5 0.0 copy-done.1
  9.5 0.0 copy-done.5
  9.5 0.8 %shard_map.70 = (bf16[4,10,32,256]{3,2,1,0:T(8,128)(2,1)S(1)}, bf16[2,9,32,256]{3,2,1,0:T(8,128)(2,1)S(1)}, f32[2,2,8,128]{3,2,1,0:T(8,128)S(1)}) custom-call(bf16[4,8,32,128]{3,2,1,0:T(8,128)(2,1)S(1)} %copy-done.1, bf16[4,8,32,128]{3,2,1,0:T(8,128)(2,1)S(1)} %collective-permute-done.sib_ref, f32[4,8,128]{2,1,0:T(8,128)S(1)} %copy-done.5, ...), custom_call_target="tpu_custom_call" | custom-call | flops 200000000 | bytes 1000000 | tf_op jit(solution)/shard_map/pallas_call | solution.py:361
  10.3 2.3 %collective-permute-done.4.zh_ref = bf16[2,16,32,128]{3,2,1,0:T(8,128)(2,1)S(1)} collective-permute-done((bf16[2,16,32,128]{3,2,1,0:T(8,128)(2,1)S(1)}, bf16[2,16,32,128]{3,2,1,0:T(8,128)(2,1)S(1)}, u32[]{:S(2)}, u32[]{:S(2)}) %collective-permute-start.4) | collective-permute-done | bytes 262176 | tf_op jit(solution)/shard_map/ppermute | solution.py:26
  12.6 1.5 %shard_map.71 = (bf16[4,10,32,256]{3,2,1,0:T(8,128)(2,1)S(1)}, bf16[4,9,32,256]{3,2,1,0:T(8,128)(2,1)S(1)}, f32[2,8,32,128]{3,2,1,0:T(8,128)S(1)}, f32[2,3,8,128]{3,2,1,0:T(8,128)S(1)}) custom-call(bf16[2,16,32,128]{3,2,1,0:T(8,128)(2,1)S(1)} %collective-permute-done.4.zh_ref, bf16[4,10,32,256]{3,2,1,0:T(8,128)(2,1)S(1)} %get-tuple-element.25.xo_ref, ...), custom_call_target="tpu_custom_call" | custom-call | flops 500000000 | bytes 1000000 | tf_op jit(solution)/shard_map/pallas_call | solution.py:361
  14.1 0.0 collective-permute-done.3.corner_ref
  14.1 0.0 collective-permute-done.2.side_ref
  14.1 0.8 %shard_map.72 = (f32[8,32,128]{2,1,0:T(8,128)S(1)}, f32[3,8,128]{2,1,0:T(8,128)S(1)}, bf16[304,128]{1,0:T(8,128)(2,1)S(1)}) custom-call(bf16[4,2,32,128]{3,2,1,0:T(8,128)(2,1)S(1)} %collective-permute-done.2.side_ref, bf16[2,2,32,128]{3,2,1,0:T(8,128)(2,1)S(1)} %collective-permute-done.3.corner_ref, bf16[4,10,32,256]{3,2,1,0:T(8,128)(2,1)S(1)} %get-tuple-element.25.xo_ref, ...), custom_call_target="tpu_custom_call" | custom-call | flops 100000000 | bytes 1000000 | tf_op jit(solution)/shard_map/pallas_call | solution.py:361
  14.9 0.1 collective-permute-start.5
  15.0 1.3 %collective-permute-done.5.got_ref = bf16[304,128]{1,0:T(8,128)(2,1)S(1)} collective-permute-done((bf16[304,128]{1,0:T(8,128)(2,1)S(1)}, bf16[304,128]{1,0:T(8,128)(2,1)S(1)}, u32[]{:S(2)}, u32[]{:S(2)}) %collective-permute-start.5) | collective-permute-done | bytes 77856 | tf_op jit(solution)/shard_map/ppermute | solution.py:26
  16.3 2.9 %collective-permute-start.8 = (bf16[304,128]{1,0:T(8,128)(2,1)S(1)}, bf16[304,128]{1,0:T(8,128)(2,1)S(1)}, u32[]{:S(2)}, u32[]{:S(2)}) collective-permute-start(bf16[304,128]{1,0:T(8,128)(2,1)S(1)} %shard_map.73.refs_0_), channel_id=1, source_target_pairs={{0,12},{1,13},{2,14},{3,15},{4,8},{5,9},{6,10},{7,11},{8,4},{9,5},... | collective-permute-start | bytes 233480 | tf_op jit(solution)/shard_map/ppermute | solution.py:26
  19.2 0.0 collective-permute-start.7
  19.2 1.5 %collective-permute-start.6 = (bf16[304,128]{1,0:T(8,128)(2,1)S(1)}, bf16[304,128]{1,0:T(8,128)(2,1)S(1)}, u32[]{:S(2)}, u32[]{:S(2)}) collective-permute-start(bf16[304,128]{1,0:T(8,128)(2,1)S(1)} %shard_map.73.refs_0_), channel_id=1, source_target_pairs={{0,4},{1,5},{2,6},{3,7},{4,0},{5,1},{6,2},{7,3},{8,12},{9,13},{10,... | collective-permute-start | bytes 233480 | tf_op jit(solution)/shard_map/ppermute | solution.py:26
  20.7 2.7 %collective-permute-done.8.refs_3_ = bf16[304,128]{1,0:T(8,128)(2,1)S(1)} collective-permute-done((bf16[304,128]{1,0:T(8,128)(2,1)S(1)}, bf16[304,128]{1,0:T(8,128)(2,1)S(1)}, u32[]{:S(2)}, u32[]{:S(2)}) %collective-permute-start.8) | collective-permute-done | bytes 77856 | tf_op jit(solution)/shard_map/ppermute | solution.py:26
  23.5 2.6 %collective-permute-done.7.refs_2_ = bf16[304,128]{1,0:T(8,128)(2,1)S(1)} collective-permute-done((bf16[304,128]{1,0:T(8,128)(2,1)S(1)}, bf16[304,128]{1,0:T(8,128)(2,1)S(1)}, u32[]{:S(2)}, u32[]{:S(2)}) %collective-permute-start.7) | collective-permute-done | bytes 77856 | tf_op jit(solution)/shard_map/ppermute | solution.py:26
  26.0 0.0 collective-permute-done.6.refs_1_
  26.0 0.8 %shard_map.74 = (f32[8,32,128]{2,1,0:T(8,128)}, f32[8,128]{1,0:T(8,128)}) custom-call(bf16[304,128]{1,0:T(8,128)(2,1)S(1)} %shard_map.73.refs_0_, bf16[304,128]{1,0:T(8,128)(2,1)S(1)} %collective-permute-done.6.refs_1_, bf16[304,128]{1,0:T(8,128)(2,1)S(1)} %collective-permute-done.7.refs_2_, bf16[304,128]{1,0:T(8,128)(2,1)S(1)} %collective-permute-done.8.refs_3_), custom_call_target="tpu_custom_call" | custom-call | tf_op jit(solution)/shard_map/pallas_call | solution.py:361
  (6 shorter events, 0.1 us)
Async XLA Ops:
  0.6 3.9 %collective-permute-start = (bf16[4,8,32,128]{3,2,1,0:T(8,128)(2,1)}, bf16[4,8,32,128]{3,2,1,0:T(8,128)(2,1)S(1)}, u32[]{:S(2)}, u32[]{:S(2)}) collective-permute-start(bf16[4,8,32,128]{3,2,1,0:T(8,128)(2,1)} %own_ref.1), channel_id=1, source_target_pairs={{0,1},{1,0},{2,3},{3,2},{4,5},{5,4},{6,7},{7,6},{8,9},{9,8},{10,11... | collective-permute-start | bytes 786440 | tf_op jit(solution)/shard_map/ppermute | solution.py:26
  1.2 3.3 %collective-permute-start.1 = (f32[4,8,128]{2,1,0:T(8,128)}, f32[4,8,128]{2,1,0:T(8,128)S(1)}, u32[]{:S(2)}, u32[]{:S(2)}) collective-permute-start(f32[4,8,128]{2,1,0:T(8,128)} %op_ref.1), channel_id=1, source_target_pairs={{0,1},{1,0},{2,3},{3,2},{4,5},{5,4},{6,7},{7,6},{8,9},{9,8},{10,11... | collective-permute-start | bytes 49160 | tf_op jit(solution)/shard_map/ppermute | solution.py:26
  1.3 0.9 %copy-start = (bf16[4,8,32,128]{3,2,1,0:T(8,128)(2,1)S(1)}, bf16[4,8,32,128]{3,2,1,0:T(8,128)(2,1)}, u32[]{:S(2)}) copy-start(bf16[4,8,32,128]{3,2,1,0:T(8,128)(2,1)} %own_ref.1) | copy-start | bytes 786436
  2.2 0.9 %copy-start.2 = (bf16[3,3,3,32,32]{4,3,2,1,0:T(8,128)(2,1)S(1)}, bf16[3,3,3,32,32]{4,3,2,1,0:T(8,128)(2,1)}, u32[]{:S(2)}) copy-start(bf16[3,3,3,32,32]{4,3,2,1,0:T(8,128)(2,1)} %k1_ref.1) | copy-start | bytes 165892
  2.3 0.9 %copy-start.4 = (f32[32]{0:T(128)S(1)}, f32[32]{0:T(128)}, u32[]{:S(2)}) copy-start(f32[32]{0:T(128)} %param.9) | copy-start | bytes 388
  3.2 0.9 %copy-start.3 = (bf16[3,3,3,32,32]{4,3,2,1,0:T(8,128)(2,1)S(1)}, bf16[3,3,3,32,32]{4,3,2,1,0:T(8,128)(2,1)}, u32[]{:S(2)}) copy-start(bf16[3,3,3,32,32]{4,3,2,1,0:T(8,128)(2,1)} %k2_ref.1) | copy-start | bytes 165892
  4.5 4.9 %copy-start.1 = (bf16[4,8,32,128]{3,2,1,0:T(8,128)(2,1)S(1)}, bf16[4,8,32,128]{3,2,1,0:T(8,128)(2,1)}, u32[]{:S(2)}) copy-start(bf16[4,8,32,128]{3,2,1,0:T(8,128)(2,1)} %own_ref.1) | copy-start | bytes 786436
  4.6 8.0 %collective-permute-start.4 = (bf16[2,16,32,128]{3,2,1,0:T(8,128)(2,1)S(1)}, bf16[2,16,32,128]{3,2,1,0:T(8,128)(2,1)S(1)}, u32[]{:S(2)}, u32[]{:S(2)}) collective-permute-start(bf16[2,16,32,128]{3,2,1,0:T(8,128)(2,1)S(1)} %maximum_select_fusion), channel_id=1, source_target_pairs={{0,2},{1,4},{2,0},{3,6},{4,1},{5,8},{6,3},{7,10},{8,5},{9,12},{10,... | collective-permute-start | bytes 786440 | tf_op jit(solution)/shard_map/ppermute | solution.py:26
  7.6 1.9 %copy-start.5 = (f32[4,8,128]{2,1,0:T(8,128)S(1)}, f32[4,8,128]{2,1,0:T(8,128)}, u32[]{:S(2)}) copy-start(f32[4,8,128]{2,1,0:T(8,128)} %op_ref.1) | copy-start | bytes 49156
  7.6 6.5 %collective-permute-start.2 = (bf16[4,2,32,128]{3,2,1,0:T(8,128)(2,1)S(1)}, bf16[4,2,32,128]{3,2,1,0:T(8,128)(2,1)S(1)}, u32[]{:S(2)}, u32[]{:S(2)}) collective-permute-start(bf16[4,2,32,128]{3,2,1,0:T(8,128)(2,1)S(1)} %select_select_fusion), channel_id=1, source_target_pairs={{0,3},{1,2},{2,1},{3,0},{4,7},{5,6},{6,5},{7,4},{8,11},{9,10},{10,... | collective-permute-start | bytes 196616 | tf_op jit(solution)/shard_map/ppermute | solution.py:26
  8.9 5.2 %collective-permute-start.3 = (bf16[2,2,32,128]{3,2,1,0:T(8,128)(2,1)S(1)}, bf16[2,2,32,128]{3,2,1,0:T(8,128)(2,1)S(1)}, u32[]{:S(2)}, u32[]{:S(2)}) collective-permute-start(bf16[2,2,32,128]{3,2,1,0:T(8,128)(2,1)S(1)} %slice_select_fusion.1), channel_id=1, source_target_pairs={{0,2},{1,6},{2,0},{3,4},{4,3},{5,10},{6,1},{7,8},{8,7},{9,14},{10,... | collective-permute-start | bytes 98312 | tf_op jit(solution)/shard_map/ppermute | solution.py:26
  14.9 1.3 %collective-permute-start.5 = (bf16[304,128]{1,0:T(8,128)(2,1)S(1)}, bf16[304,128]{1,0:T(8,128)(2,1)S(1)}, u32[]{:S(2)}, u32[]{:S(2)}) collective-permute-start(bf16[304,128]{1,0:T(8,128)(2,1)S(1)} %get-tuple-element.37), channel_id=1, source_target_pairs={{0,1},{1,0},{2,3},{3,2},{4,5},{5,4},{6,7},{7,6},{8,9},{9,8},{10,11... | collective-permute-start | bytes 233480 | tf_op jit(solution)/shard_map/ppermute | solution.py:26
  16.3 7.2 %collective-permute-start.8 = (bf16[304,128]{1,0:T(8,128)(2,1)S(1)}, bf16[304,128]{1,0:T(8,128)(2,1)S(1)}, u32[]{:S(2)}, u32[]{:S(2)}) collective-permute-start(bf16[304,128]{1,0:T(8,128)(2,1)S(1)} %shard_map.73.refs_0_), channel_id=1, source_target_pairs={{0,12},{1,13},{2,14},{3,15},{4,8},{5,9},{6,10},{7,11},{8,4},{9,5},... | collective-permute-start | bytes 233480 | tf_op jit(solution)/shard_map/ppermute | solution.py:26
  19.2 6.8 %collective-permute-start.7 = (bf16[304,128]{1,0:T(8,128)(2,1)S(1)}, bf16[304,128]{1,0:T(8,128)(2,1)S(1)}, u32[]{:S(2)}, u32[]{:S(2)}) collective-permute-start(bf16[304,128]{1,0:T(8,128)(2,1)S(1)} %shard_map.73.refs_0_), channel_id=1, source_target_pairs={{0,8},{1,9},{2,10},{3,11},{4,12},{5,13},{6,14},{7,15},{8,0},{9,1},... | collective-permute-start | bytes 233480 | tf_op jit(solution)/shard_map/ppermute | solution.py:26
  19.2 6.8 %collective-permute-start.6 = (bf16[304,128]{1,0:T(8,128)(2,1)S(1)}, bf16[304,128]{1,0:T(8,128)(2,1)S(1)}, u32[]{:S(2)}, u32[]{:S(2)}) collective-permute-start(bf16[304,128]{1,0:T(8,128)(2,1)S(1)} %shard_map.73.refs_0_), channel_id=1, source_target_pairs={{0,4},{1,5},{2,6},{3,7},{4,0},{5,1},{6,2},{7,3},{8,12},{9,13},{10,... | collective-permute-start | bytes 233480 | tf_op jit(solution)/shard_map/ppermute | solution.py:26

commit v7 on v6

--- a/solution.py
+++ b/solution.py
@@ -32,11 +32,13 @@
     span = taps * chans
     turned_over = (lax.axis_index("rows") >> 1) == 1
     row_tap = [jnp.where(turned_over, taps - 1 - b, b) for b in range(taps)]
+    upper = (lax.axis_index("rows") & 1) == 1
+    plane_tap = [jnp.where(upper, taps - 1 - a, a) for a in range(taps)]
     for k_ref, w_ref in ((k1_ref, w1_ref), (k2_ref, w2_ref)):
         made = w_ref.shape[0] // (taps * chans)
         for e in range(taps):
             flat = jnp.concatenate(
-                [k_ref[a, row_tap[b], e].astype(F32) for a in range(taps) for b in range(taps)]
+                [k_ref[plane_tap[a], row_tap[b], e].astype(F32) for a in range(taps) for b in range(taps)]
                 + [jnp.zeros(((made - 1) * span, chans), F32)],
                 axis=0,
             )
@@ -100,20 +102,20 @@
     return ((flat[0] + flat[1]) + flat[2]) * 2.0, flat[3] + flat[4], flat[5]
 
 
-def first_layer(w, x, half, chans, outside, store):
+def first_layer(w, x, half, chans, ends, store):
     lo, hi = shifted_sum(jnp.dot(w, x, preferred_element_type=F32), half * chans)
     for p in range(half):
         part = slice(p * chans, (p + 1) * chans)
         a, b = jnp.maximum(lo[part], 0.0), jnp.maximum(hi[part], 0.0)
-        if outside is not None:
-            a = jnp.where(outside[p], 0.0, a)
-            b = jnp.where(outside[p], 0.0, b)
+        if ends is not None and p == 0:
+            a = jnp.where(ends, 0.0, a)
+            b = jnp.where(ends, 0.0, b)
         store(p, a.astype(BF16), b.astype(BF16))
 
 
-def second_layer(w, x, pb, ps_ref, fracs, two_rows, over, feat_ref, stat_ref):
-    chans = feat_ref.shape[2]
-    rows = feat_ref.shape[1]
+def second_layer(w, x, pb, ps_ref, fracs, two_rows, over, put, stat_ref):
+    chans = pb.shape[0]
+    rows = ps_ref.shape[2]
     half = len(fracs)
     y = jnp.dot(w, x, preferred_element_type=F32)
     for row, side in zip(two_rows, shifted_sum(y, half * chans)):
@@ -129,7 +131,7 @@
         weights = [jnp.exp(s_ - peak) for s_ in scores]
         total = functools.reduce(jnp.add, weights)
         depth_sum = functools.reduce(jnp.add, [w_ * f for w_, f in zip(weights, fracs)])
-        feat_ref[far, at] = functools.reduce(jnp.add, [w_ * f for w_, f in zip(weights, feats)])
+        put(far, at, functools.reduce(jnp.add, [w_ * f for w_, f in zip(weights, feats)]))
         for k, value in enumerate((peak, total, depth_sum)):
             stat_ref[far, k, pl.ds(at, 1), :] = value
 
@@ -139,46 +141,40 @@
     d = lax.axis_index("depth")
     core = lax.axis_index("rows") & 1
     over = (lax.axis_index("rows") >> 1) == 1
-    fracs = [
-        ((d * planes + core * half + p).astype(F32) + 0.5) / (depth * planes) for p in range(half)
-    ]
-    first, last = d == 0, d == depth - 1
-    outside = [jnp.logical_and(core == 0, first)] + [False] * (half - 2)
-    outside = outside + [jnp.logical_and(core == 1, last)]
-    return core, over, fracs, outside
-
-
-def by_place(core, over, fill):
-    for c in range(2):
-        for flip in (False, True):
-            pl.when(jnp.logical_and(core == c, over == flip))(functools.partial(fill, c, flip))
-
-
-def fill_rows(ref, to, source, planes, rows, flip):
+    plane = [d * planes + jnp.where(core == 1, planes - 1 - p, p) for p in range(half)]
+    fracs = [(p.astype(F32) + 0.5) / (depth * planes) for p in plane]
+    ends = d == jnp.where(core == 1, depth - 1, 0)
+    return core, over, fracs, ends
+
+
+def turned(p, planes, flag):
+    return jnp.where(flag, planes - 1 - p, p)
+
+
+def fill_rows(ref, p, source, rows, row_of):
     chans, width = ref.shape[2], ref.shape[3] // 2
     for cols, start in ((slice(0, width), -1), (slice(width, 2 * width), rows - 2)):
         for slot in range(rows + 2):
             row = start + slot
             if row < 0:
-                ref[to, slot, :, cols] = jnp.zeros((planes, chans, width), BF16)
+                ref[p, slot, :, cols] = jnp.zeros((chans, width), BF16)
             else:
-                ref[to, slot, :, cols] = source(2 * rows - 1 - row if flip else row)
-
-
-def first_rows(w, x_ref, half, rows, outside, fs_ref, base):
-    chans, wide = x_ref.shape[2:]
+                ref[p, slot, :, cols] = source(row_of(row))
+
+
+def first_rows(w, x_of, half, rows, ends, fs_ref):
+    chans, wide = fs_ref.shape[2:]
     left, right = slice(0, wide // 2), slice(wide // 2, wide)
     for p in range(half):
-        fs_ref[base + p, 0, :, left] = jnp.zeros((chans, wide // 2), BF16)
+        fs_ref[p, 0, :, left] = jnp.zeros((chans, wide // 2), BF16)
     for i in range(rows):
         def store(p, a, b, i=i):
-            fs_ref[base + p, i + 1, :, left] = a
-            fs_ref[base + p, i + 1, :, right] = b
+            fs_ref[p, i + 1, :, left] = a
+            fs_ref[p, i + 1, :, right] = b
             if i == rows - 2:
-                fs_ref[base + p, 0, :, right] = a
-
-        x = x_ref[:, i : i + 3].reshape(-1, wide)
-        first_layer(w, x, half, chans, outside, store)
+                fs_ref[p, 0, :, right] = a
+
+        first_layer(w, x_of(slice(i, i + 3)).reshape(-1, wide), half, chans, ends, store)
 
 
 def own_kernel(depth, own_ref, sib_ref, op_ref, sp_ref, w1_ref, xo_ref, fo_ref, ps_ref):
@@ -188,108 +184,127 @@
 
     def fill(c, flip):
         blocks = (own_ref, sib_ref) if c == 0 else (sib_ref, own_ref)
-        fill_rows(
-            xo_ref, slice(0, planes), lambda row: blocks[row // rows][:, row % rows],
-            planes, rows, flip,
-        )
         priors = (op_ref, sp_ref) if c == 0 else (sp_ref, op_ref)
-        for k in range(2):
-            ps_ref[k] = priors[1 - k if flip else k][half * c : half * c + half]
-
-    by_place(core, over, fill)
-    first_rows(w1_ref[...], xo_ref, half, rows, None, fo_ref, 0)
+        for p in range(planes):
+            plane = planes - 1 - p if c else p
+            fill_rows(
+                xo_ref, p, lambda row: blocks[row // rows][plane, row % rows], rows,
+                lambda row: 2 * rows - 1 - row if flip else row,
+            )
+            if p < half:
+                for k in range(2):
+                    ps_ref[k, p] = priors[1 - k if flip else k][plane]
+
+    for c in range(2):
+        for flip in (False, True):
+            pl.when(jnp.logical_and(core == c, over == flip))(functools.partial(fill, c, flip))
+    first_rows(w1_ref[...], lambda at: xo_ref[:, at], half, rows, None, fo_ref)
 
 
 def inner_kernel(
     depth, zh_ref, xo_ref, fo_ref, ps_ref, w1_ref, w2_ref, pb_ref,
-    xz_ref, fs_ref, feat_ref, stat_ref,
+    xz_ref, fz_ref, feat_ref, stat_ref,
 ):
     half = zh_ref.shape[0]
     planes = xo_ref.shape[0]
     rows = xo_ref.shape[1] - 2
     wide = xo_ref.shape[3]
     lead = rows - 1
-    core, over, fracs, outside = place_of(depth, planes)
-    ends = jnp.logical_or(outside[0], outside[-1])
-
-    def fill(c, flip):
-        theirs, mine = slice(half * c, half * c + half), slice(half * (1 - c), half * (2 - c))
-        xz_ref[mine] = xo_ref[theirs]
-        fs_ref[mine] = fo_ref[...]
-        fill_rows(
-            xz_ref, theirs,
-            lambda row: jnp.where(ends, jnp.zeros_like(zh_ref[:, row]), zh_ref[:, row]),
-            half, rows, flip,
-        )
-
-    by_place(core, over, fill)
-    first_rows(w1_ref[...], xz_ref, half, rows, outside, fs_ref, core * half)
+    core, over, fracs, ends = place_of(depth, planes)
+    for p in range(half):
+        plane = turned(p, half, core == 1)
+
+        def source(row):
+            got = zh_ref[plane, row]
+            return jnp.where(ends, jnp.zeros_like(got), got)
+
+        fill_rows(xz_ref, p, source, rows, lambda row: turned(row, 2 * rows, over))
+
+    first_rows(
+        w1_ref[...], lambda at: jnp.concatenate([xz_ref[:, at], xo_ref[:half, at]], axis=0),
+        half, rows, ends, fz_ref,
+    )
+
+    def put(far, at, feat):
+        feat_ref[far, at] = feat
+
     w2 = w2_ref[...]
     pb = pb_ref[...]
     for i in range(lead):
-        x = fs_ref[:, i : i + 3].reshape(-1, wide)
-        second_layer(w2, x, pb, ps_ref, fracs, (i, i + lead), over, feat_ref, stat_ref)
+        at = slice(i, i + 3)
+        x = jnp.concatenate([fz_ref[:, at], fo_ref[:, at]], axis=0).reshape(-1, wide)
+        second_layer(w2, x, pb, ps_ref, fracs, (i, i + lead), over, put, stat_ref)
 
 
 def outer_kernel(
-    depth, side_ref, corner_ref, xo_ref, ps_ref, xz_ref, fs_ref, fi_ref, ti_ref, w1_ref, w2_ref,
-    pb_ref, keep_ref, stat_ref, send_ref, own_halo_ref, halo_ref, late_ref, feat_ref, all_ref,
+    depth, side_ref, corner_ref, xo_ref, fo_ref, ps_ref, xz_ref, fz_ref, fi_ref, ti_ref, w1_ref,
+    w2_ref, pb_ref, keep_ref, stat_ref, send_ref, all_ref,
 ):
     planes, halo, chans, width = side_ref.shape
     half = planes // 2
     rows = keep_ref.shape[0]
-    core, over, fracs, outside = place_of(depth, planes)
-    ends = jnp.logical_or(outside[0], outside[-1])
+    core, over, fracs, ends = place_of(depth, planes)
     right = slice(width, 2 * width)
-
-    for k in range(halo):
-        at = jnp.where(over, halo - 1 - k, k)
-        for p in range(planes):
-            own_halo_ref[p, k] = side_ref[p, at]
-        for p in range(half):
-            got = corner_ref[p, at]
-            halo_ref[core * half + p, k] = jnp.where(ends, jnp.zeros_like(got), got)
-            halo_ref[(1 - core) * half + p, k] = side_ref[core * half + p, at]
-
-    def pair(parts):
-        return jnp.concatenate(
-            [jnp.concatenate(p, axis=1).reshape(-1, width) for p in parts], axis=1
-        )
+    kept = jnp.where(over, 1 - core, core)
+    given = 1 - kept
+    keep_ref[...] = fi_ref[kept]
+    for i in range(rows):
+        send_ref[i * chans : (i + 1) * chans] = fi_ref[given, i].astype(BF16)
+    all_ref[...] = ti_ref[...]
+
+    row_at = [turned(k, halo, over) for k in range(halo)]
+    own_halo = [[side_ref[turned(p, planes, core == 1), at] for at in row_at] for p in range(planes)]
+    corner = [[corner_ref[turned(p, half, core == 1), at] for at in row_at] for p in range(half)]
+    corner = [[jnp.where(ends, jnp.zeros_like(v), v) for v in pair_] for pair_ in corner]
+
+    def pair(blocks):
+        sides = []
+        for start in range(2):
+            flat = []
+            for near, late in blocks:
+                flat += near[start:] + late[: start + 1]
+            sides.append(jnp.concatenate(flat, axis=0))
+        return jnp.concatenate(sides, axis=1)
+
+    def near(ref, p):
+        return [ref[p, slot, :, right] for slot in (rows, rows + 1)]
+
+    own_rows = [(near(xo_ref, p), own_halo[p]) for p in range(planes)]
+    far_rows = [(near(xz_ref, p), corner[p]) for p in range(half)]
+    late = [None] * (half + 2)
+
+    def store(base):
+        def put(p, a, b):
+            late[base + p] = [a, b]
+
+        return put
 
     w1 = w1_ref[...]
-    for x_ref, h_ref, mask, base in (
-        (xo_ref, own_halo_ref, None, (1 - core) * half),
-        (xz_ref, halo_ref, outside, core * half),
-    ):
-        x = pair(
-            [
-                [x_ref[:, rows:, :, right], h_ref[:, :1]],
-                [x_ref[:, rows + 1 :, :, right], h_ref[...]],
-            ]
-        )
-
-        def store(p, a, b):
-            late_ref[base + p, 0] = a
-            late_ref[base + p, 1] = b
-
-        first_layer(w1, x, half, chans, mask, store)
-
-    feat_ref[...] = fi_ref[...]
-    all_ref[...] = ti_ref[...]
+    first_layer(w1, pair(own_rows), half, chans, None, store(half))
+    first_layer(w1, pair(far_rows + own_rows[:half]), half, chans, ends, store(0))
     x = pair(
         [
-            [fs_ref[:, rows - 1 :, :, right], late_ref[:, :1]],
-            [fs_ref[:, rows:, :, right], late_ref[...]],
+            ([ref[p, slot, :, right] for slot in (rows - 1, rows)], late[base + p])
+            for base, ref in ((0, fz_ref), (half, fo_ref))
+            for p in range(half)
         ]
     )
     two_rows = (2 * rows - 2, 2 * rows - 1)
-    second_layer(w2_ref[...], x, pb_ref[...], ps_ref, fracs, two_rows, over, feat_ref, all_ref)
-    kept = jnp.where(over, 1 - core, core)
-    keep_ref[...] = feat_ref[kept]
+
+    def put(far, at, feat):
+        def mine():
+            keep_ref[at] = feat
+
+        def theirs():
+            send_ref[pl.ds(pl.multiple_of(at * chans, chans), chans)] = feat.astype(BF16)
+
+        pl.when(kept == far)(mine)
+        pl.when(kept != far)(theirs)
+
+    second_layer(w2_ref[...], x, pb_ref[...], ps_ref, fracs, two_rows, over, put, all_ref)
     stat_ref[...] = all_ref[kept]
-    given = 1 - kept
-    feats = [feat_ref[given, i] for i in range(rows)]
-    store_parcel(send_ref, feats, *[all_ref[given, k] for k in range(3)])
+    flat = stat_pieces(*[all_ref[given, k] for k in range(3)])
+    send_ref[rows * chans :] = jnp.concatenate(flat, axis=0).astype(BF16)
 
 
 def merge(one, two, rows):
@@ -449,8 +464,8 @@
     inside = call(
         functools.partial(inner_kernel, depth),
         [
-            (block_shape, BF16),
-            ((half + 2, rows + 1, chans, 2 * width), BF16),
+            ((half, rows + 2, chans, 2 * width), BF16),
+            ((half, rows + 1, chans, 2 * width), BF16),
             ((2, rows, chans, width), F32),
             ((2,) + stats_shape, F32),
         ],
@@ -460,14 +475,8 @@
     keep, stat, send = call(
         functools.partial(outer_kernel, depth),
         [((rows, chans, width), F32), (stats_shape, F32), (parcel_shape, BF16)],
-        side, corner, xo, ps, *inside, w1, w2, pb,
-        scratch=[
-            pltpu.VMEM((planes, halo, chans, width), BF16),
-            pltpu.VMEM((planes, halo, chans, width), BF16),
-            pltpu.VMEM((half + 2, halo, chans, width), BF16),
-            pltpu.VMEM((2, rows, chans, width), F32),
-            pltpu.VMEM((2,) + stats_shape, F32),
-        ],
+        side, corner, xo, fo, ps, *inside, w1, w2, pb,
+        scratch=[pltpu.VMEM((2,) + stats_shape, F32)],
         flops=10**8, nbytes=10**6, room=6,
     )
     got = move(send, lambda d, r: (d, r ^ 1))

time: 27 us -> 26.9 us (level)
  transfers between devices with their start and end apart: 9 -> 9, of which waited for: 4 -> 5; matrix products, arithmetic and copies ran while one was open for 0% -> 0% of each run, Pallas kernels for 10% -> 9%
where the time goes in v7:
time: 26.9 us; the launch traced here: 26.7 us
  starting transfers between devices  10 us (37%)
  waiting for transfers between devices  9.08 us (34%)
  Pallas kernels  4.02 us (15%)
  local copies, waits for them, and re-layouts  2.8 us (10%)
  between operations  0.73 us (3%)
    ppermute x9, starting transfers between devices, exchange(): return lax.ppermute(value, AXES, pairs)  10 us
    ppermute x9, waiting for transfers between devices, exchange(): return lax.ppermute(value, AXES, pairs)  9.08 us
    pallas_call x7, Pallas kernels, call(): pl.pallas_call(kernel, out_shape=[jax.ShapeDtypeStruct(s, t) for s, t in...  4.02 us
    unnamed x12, local copies, waits for them, and re-layouts  2.8 us
  transfers between devices with their start and end apart: 9, of which 5 were waited for; matrix products, arithmetic and copies ran while one was open for 0% of the time, Pallas kernels for 9%

profile of v7, /device:TPU:0, one launch (start us, length us, event | category | flops | bytes accessed | tf_op | source)
XLA Modules:
  0.0 26.7 jit_solution(5965656118854092610)
XLA Ops:
  0.6 0.6 %collective-permute-start = (bf16[4,8,32,128]{3,2,1,0:T(8,128)(2,1)}, bf16[4,8,32,128]{3,2,1,0:T(8,128)(2,1)S(1)}, u32[]{:S(2)}, u32[]{:S(2)}) collective-permute-start(bf16[4,8,32,128]{3,2,1,0:T(8,128)(2,1)} %own_ref.1), channel_id=1, source_target_pairs={{0,1},{1,0},{2,3},{3,2},{4,5},{5,4},{6,7},{7,6},{8,9},{9,8},{10,11... | collective-permute-start | bytes 786440 | tf_op jit(solution)/shard_map/ppermute | solution.py:26
  1.2 0.1 collective-permute-start.1
  1.3 0.0 copy-start
  1.3 0.9 %copy-done = bf16[4,8,32,128]{3,2,1,0:T(8,128)(2,1)S(1)} copy-done((bf16[4,8,32,128]{3,2,1,0:T(8,128)(2,1)S(1)}, bf16[4,8,32,128]{3,2,1,0:T(8,128)(2,1)}, u32[]{:S(2)}) %copy-start) | copy-done | bytes 262168
  2.2 0.0 copy-start.2
  2.3 0.0 copy-start.4
  2.3 0.9 %copy-done.2 = bf16[3,3,3,32,32]{4,3,2,1,0:T(8,128)(2,1)S(1)} copy-done((bf16[3,3,3,32,32]{4,3,2,1,0:T(8,128)(2,1)S(1)}, bf16[3,3,3,32,32]{4,3,2,1,0:T(8,128)(2,1)}, u32[]{:S(2)}) %copy-start.2) | copy-done | bytes 55320
  3.2 0.0 copy-done.4
  3.2 0.0 copy-start.3
  3.2 0.9 %copy-done.3 = bf16[3,3,3,32,32]{4,3,2,1,0:T(8,128)(2,1)S(1)} copy-done((bf16[3,3,3,32,32]{4,3,2,1,0:T(8,128)(2,1)S(1)}, bf16[3,3,3,32,32]{4,3,2,1,0:T(8,128)(2,1)}, u32[]{:S(2)}) %copy-start.3) | copy-done | bytes 55320
  4.1 0.4 %shard_map.69 = (bf16[192,384]{1,0:T(8,128)(2,1)S(1)}, bf16[192,384]{1,0:T(8,128)(2,1)S(1)}, f32[32,128]{1,0:T(8,128)S(1)}) custom-call(bf16[3,3,3,32,32]{4,3,2,1,0:T(8,128)(2,1)S(1)} %copy-done.2, bf16[3,3,3,32,32]{4,3,2,1,0:T(8,128)(2,1)S(1)} %copy-done.3, f32[1,32]{1,0:T(1,128)S(1)} %bitcast.1), custom_call_target="tpu_custom_call" | custom-call | flops 100000000 | bytes 1000000 | tf_op jit(solution)/shard_map/pallas_call | solution.py:376
  4.5 0.0 collective-permute-done.1.sp_ref
  4.5 0.0 collective-permute-done.sib_ref
  4.5 0.0 copy-start.1
  4.6 3.0 %collective-permute-start.4 = (bf16[2,16,32,128]{3,2,1,0:T(8,128)(2,1)S(1)}, bf16[2,16,32,128]{3,2,1,0:T(8,128)(2,1)S(1)}, u32[]{:S(2)}, u32[]{:S(2)}) collective-permute-start(bf16[2,16,32,128]{3,2,1,0:T(8,128)(2,1)S(1)} %maximum_select_fusion), channel_id=1, source_target_pairs={{0,2},{1,4},{2,0},{3,6},{4,1},{5,8},{6,3},{7,10},{8,5},{9,12},{10,... | collective-permute-start | bytes 786440 | tf_op jit(solution)/shard_map/ppermute | solution.py:26
  7.6 0.0 copy-start.5
  7.6 1.4 %collective-permute-start.2 = (bf16[4,2,32,128]{3,2,1,0:T(8,128)(2,1)S(1)}, bf16[4,2,32,128]{3,2,1,0:T(8,128)(2,1)S(1)}, u32[]{:S(2)}, u32[]{:S(2)}) collective-permute-start(bf16[4,2,32,128]{3,2,1,0:T(8,128)(2,1)S(1)} %select_select_fusion), channel_id=1, source_target_pairs={{0,3},{1,2},{2,1},{3,0},{4,7},{5,6},{6,5},{7,4},{8,11},{9,10},{10,... | collective-permute-start | bytes 196616 | tf_op jit(solution)/shard_map/ppermute | solution.py:26
  8.9 0.5 %collective-permute-start.3 = (bf16[2,2,32,128]{3,2,1,0:T(8,128)(2,1)S(1)}, bf16[2,2,32,128]{3,2,1,0:T(8,128)(2,1)S(1)}, u32[]{:S(2)}, u32[]{:S(2)}) collective-permute-start(bf16[2,2,32,128]{3,2,1,0:T(8,128)(2,1)S(1)} %slice_select_fusion.1), channel_id=1, source_target_pairs={{0,2},{1,6},{2,0},{3,4},{4,3},{5,10},{6,1},{7,8},{8,7},{9,14},{10,... | collective-permute-start | bytes 98312 | tf_op jit(solution)/shard_map/ppermute | solution.py:26
  9.5 0.0 copy-done.1
  9.5 0.0 copy-done.5
  9.5 0.8 %shard_map.70 = (bf16[4,10,32,256]{3,2,1,0:T(8,128)(2,1)S(1)}, bf16[2,9,32,256]{3,2,1,0:T(8,128)(2,1)S(1)}, f32[2,2,8,128]{3,2,1,0:T(8,128)S(1)}) custom-call(bf16[4,8,32,128]{3,2,1,0:T(8,128)(2,1)S(1)} %copy-done.1, bf16[4,8,32,128]{3,2,1,0:T(8,128)(2,1)S(1)} %collective-permute-done.sib_ref, f32[4,8,128]{2,1,0:T(8,128)S(1)} %copy-done.5, ...), custom_call_target="tpu_custom_call" | custom-call | flops 200000000 | bytes 1000000 | tf_op jit(solution)/shard_map/pallas_call | solution.py:376
  10.3 2.3 %collective-permute-done.4.zh_ref = bf16[2,16,32,128]{3,2,1,0:T(8,128)(2,1)S(1)} collective-permute-done((bf16[2,16,32,128]{3,2,1,0:T(8,128)(2,1)S(1)}, bf16[2,16,32,128]{3,2,1,0:T(8,128)(2,1)S(1)}, u32[]{:S(2)}, u32[]{:S(2)}) %collective-permute-start.4) | collective-permute-done | bytes 262176 | tf_op jit(solution)/shard_map/ppermute | solution.py:26
  12.6 1.3 %shard_map.71 = (bf16[2,10,32,256]{3,2,1,0:T(8,128)(2,1)S(1)}, bf16[2,9,32,256]{3,2,1,0:T(8,128)(2,1)S(1)}, f32[2,8,32,128]{3,2,1,0:T(8,128)S(1)}, f32[2,3,8,128]{3,2,1,0:T(8,128)S(1)}) custom-call(bf16[2,16,32,128]{3,2,1,0:T(8,128)(2,1)S(1)} %collective-permute-done.4.zh_ref, bf16[4,10,32,256]{3,2,1,0:T(8,128)(2,1)S(1)} %get-tuple-element.25.xo_ref, ...), custom_call_target="tpu_custom_call" | custom-call | flops 500000000 | bytes 1000000 | tf_op jit(solution)/shard_map/pallas_call | solution.py:376
  13.9 0.1 collective-permute-done.3.corner_ref
  14.0 0.0 collective-permute-done.2.side_ref
  14.0 0.8 %shard_map.72 = (f32[8,32,128]{2,1,0:T(8,128)S(1)}, f32[3,8,128]{2,1,0:T(8,128)S(1)}, bf16[304,128]{1,0:T(8,128)(2,1)S(1)}) custom-call(bf16[4,2,32,128]{3,2,1,0:T(8,128)(2,1)S(1)} %collective-permute-done.2.side_ref, bf16[2,2,32,128]{3,2,1,0:T(8,128)(2,1)S(1)} %collective-permute-done.3.corner_ref, bf16[4,10,32,256]{3,2,1,0:T(8,128)(2,1)S(1)} %get-tuple-element.25.xo_ref, ...), custom_call_target="tpu_custom_call" | custom-call | flops 100000000 | bytes 1000000 | tf_op jit(solution)/shard_map/pallas_call | solution.py:376
  14.8 0.1 collective-permute-start.5
  14.8 1.3 %collective-permute-done.5.got_ref = bf16[304,128]{1,0:T(8,128)(2,1)S(1)} collective-permute-done((bf16[304,128]{1,0:T(8,128)(2,1)S(1)}, bf16[304,128]{1,0:T(8,128)(2,1)S(1)}, u32[]{:S(2)}, u32[]{:S(2)}) %collective-permute-start.5) | collective-permute-done | bytes 77856 | tf_op jit(solution)/shard_map/ppermute | solution.py:26
  16.1 3.0 %collective-permute-start.8 = (bf16[304,128]{1,0:T(8,128)(2,1)S(1)}, bf16[304,128]{1,0:T(8,128)(2,1)S(1)}, u32[]{:S(2)}, u32[]{:S(2)}) collective-permute-start(bf16[304,128]{1,0:T(8,128)(2,1)S(1)} %shard_map.73.refs_0_), channel_id=1, source_target_pairs={{0,12},{1,13},{2,14},{3,15},{4,8},{5,9},{6,10},{7,11},{8,4},{9,5},... | collective-permute-start | bytes 233480 | tf_op jit(solution)/shard_map/ppermute | solution.py:26
  19.1 0.0 collective-permute-start.7
  19.1 1.5 %collective-permute-start.6 = (bf16[304,128]{1,0:T(8,128)(2,1)S(1)}, bf16[304,128]{1,0:T(8,128)(2,1)S(1)}, u32[]{:S(2)}, u32[]{:S(2)}) collective-permute-start(bf16[304,128]{1,0:T(8,128)(2,1)S(1)} %shard_map.73.refs_0_), channel_id=1, source_target_pairs={{0,4},{1,5},{2,6},{3,7},{4,0},{5,1},{6,2},{7,3},{8,12},{9,13},{10,... | collective-permute-start | bytes 233480 | tf_op jit(solution)/shard_map/ppermute | solution.py:26
  20.6 2.7 %collective-permute-done.8.refs_3_ = bf16[304,128]{1,0:T(8,128)(2,1)S(1)} collective-permute-done((bf16[304,128]{1,0:T(8,128)(2,1)S(1)}, bf16[304,128]{1,0:T(8,128)(2,1)S(1)}, u32[]{:S(2)}, u32[]{:S(2)}) %collective-permute-start.8) | collective-permute-done | bytes 77856 | tf_op jit(solution)/shard_map/ppermute | solution.py:26
  23.3 2.6 %collective-permute-done.7.refs_2_ = bf16[304,128]{1,0:T(8,128)(2,1)S(1)} collective-permute-done((bf16[304,128]{1,0:T(8,128)(2,1)S(1)}, bf16[304,128]{1,0:T(8,128)(2,1)S(1)}, u32[]{:S(2)}, u32[]{:S(2)}) %collective-permute-start.7) | collective-permute-done | bytes 77856 | tf_op jit(solution)/shard_map/ppermute | solution.py:26
  26.0 0.0 collective-permute-done.6.refs_1_
  26.0 0.8 %shard_map.74 = (f32[8,32,128]{2,1,0:T(8,128)}, f32[8,128]{1,0:T(8,128)}) custom-call(bf16[304,128]{1,0:T(8,128)(2,1)S(1)} %shard_map.73.refs_0_, bf16[304,128]{1,0:T(8,128)(2,1)S(1)} %collective-permute-done.6.refs_1_, bf16[304,128]{1,0:T(8,128)(2,1)S(1)} %collective-permute-done.7.refs_2_, bf16[304,128]{1,0:T(8,128)(2,1)S(1)} %collective-permute-done.8.refs_3_), custom_call_target="tpu_custom_call" | custom-call | tf_op jit(solution)/shard_map/pallas_call | solution.py:376
  (6 shorter events, 0.1 us)
Async XLA Ops:
  0.6 3.9 %collective-permute-start = (bf16[4,8,32,128]{3,2,1,0:T(8,128)(2,1)}, bf16[4,8,32,128]{3,2,1,0:T(8,128)(2,1)S(1)}, u32[]{:S(2)}, u32[]{:S(2)}) collective-permute-start(bf16[4,8,32,128]{3,2,1,0:T(8,128)(2,1)} %own_ref.1), channel_id=1, source_target_pairs={{0,1},{1,0},{2,3},{3,2},{4,5},{5,4},{6,7},{7,6},{8,9},{9,8},{10,11... | collective-permute-start | bytes 786440 | tf_op jit(solution)/shard_map/ppermute | solution.py:26
  1.2 3.3 %collective-permute-start.1 = (f32[4,8,128]{2,1,0:T(8,128)}, f32[4,8,128]{2,1,0:T(8,128)S(1)}, u32[]{:S(2)}, u32[]{:S(2)}) collective-permute-start(f32[4,8,128]{2,1,0:T(8,128)} %op_ref.1), channel_id=1, source_target_pairs={{0,1},{1,0},{2,3},{3,2},{4,5},{5,4},{6,7},{7,6},{8,9},{9,8},{10,11... | collective-permute-start | bytes 49160 | tf_op jit(solution)/shard_map/ppermute | solution.py:26
  1.3 0.9 %copy-start = (bf16[4,8,32,128]{3,2,1,0:T(8,128)(2,1)S(1)}, bf16[4,8,32,128]{3,2,1,0:T(8,128)(2,1)}, u32[]{:S(2)}) copy-start(bf16[4,8,32,128]{3,2,1,0:T(8,128)(2,1)} %own_ref.1) | copy-start | bytes 786436
  2.2 0.9 %copy-start.2 = (bf16[3,3,3,32,32]{4,3,2,1,0:T(8,128)(2,1)S(1)}, bf16[3,3,3,32,32]{4,3,2,1,0:T(8,128)(2,1)}, u32[]{:S(2)}) copy-start(bf16[3,3,3,32,32]{4,3,2,1,0:T(8,128)(2,1)} %k1_ref.1) | copy-start | bytes 165892
  2.3 0.9 %copy-start.4 = (f32[32]{0:T(128)S(1)}, f32[32]{0:T(128)}, u32[]{:S(2)}) copy-start(f32[32]{0:T(128)} %param.9) | copy-start | bytes 388
  3.2 0.9 %copy-start.3 = (bf16[3,3,3,32,32]{4,3,2,1,0:T(8,128)(2,1)S(1)}, bf16[3,3,3,32,32]{4,3,2,1,0:T(8,128)(2,1)}, u32[]{:S(2)}) copy-start(bf16[3,3,3,32,32]{4,3,2,1,0:T(8,128)(2,1)} %k2_ref.1) | copy-start | bytes 165892
  4.5 4.9 %copy-start.1 = (bf16[4,8,32,128]{3,2,1,0:T(8,128)(2,1)S(1)}, bf16[4,8,32,128]{3,2,1,0:T(8,128)(2,1)}, u32[]{:S(2)}) copy-start(bf16[4,8,32,128]{3,2,1,0:T(8,128)(2,1)} %own_ref.1) | copy-start | bytes 786436
  4.6 8.0 %collective-permute-start.4 = (bf16[2,16,32,128]{3,2,1,0:T(8,128)(2,1)S(1)}, bf16[2,16,32,128]{3,2,1,0:T(8,128)(2,1)S(1)}, u32[]{:S(2)}, u32[]{:S(2)}) collective-permute-start(bf16[2,16,32,128]{3,2,1,0:T(8,128)(2,1)S(1)} %maximum_select_fusion), channel_id=1, source_target_pairs={{0,2},{1,4},{2,0},{3,6},{4,1},{5,8},{6,3},{7,10},{8,5},{9,12},{10,... | collective-permute-start | bytes 786440 | tf_op jit(solution)/shard_map/ppermute | solution.py:26
  7.6 1.9 %copy-start.5 = (f32[4,8,128]{2,1,0:T(8,128)S(1)}, f32[4,8,128]{2,1,0:T(8,128)}, u32[]{:S(2)}) copy-start(f32[4,8,128]{2,1,0:T(8,128)} %op_ref.1) | copy-start | bytes 49156
  7.6 6.4 %collective-permute-start.2 = (bf16[4,2,32,128]{3,2,1,0:T(8,128)(2,1)S(1)}, bf16[4,2,32,128]{3,2,1,0:T(8,128)(2,1)S(1)}, u32[]{:S(2)}, u32[]{:S(2)}) collective-permute-start(bf16[4,2,32,128]{3,2,1,0:T(8,128)(2,1)S(1)} %select_select_fusion), channel_id=1, source_target_pairs={{0,3},{1,2},{2,1},{3,0},{4,7},{5,6},{6,5},{7,4},{8,11},{9,10},{10,... | collective-permute-start | bytes 196616 | tf_op jit(solution)/shard_map/ppermute | solution.py:26
  8.9 5.1 %collective-permute-start.3 = (bf16[2,2,32,128]{3,2,1,0:T(8,128)(2,1)S(1)}, bf16[2,2,32,128]{3,2,1,0:T(8,128)(2,1)S(1)}, u32[]{:S(2)}, u32[]{:S(2)}) collective-permute-start(bf16[2,2,32,128]{3,2,1,0:T(8,128)(2,1)S(1)} %slice_select_fusion.1), channel_id=1, source_target_pairs={{0,2},{1,6},{2,0},{3,4},{4,3},{5,10},{6,1},{7,8},{8,7},{9,14},{10,... | collective-permute-start | bytes 98312 | tf_op jit(solution)/shard_map/ppermute | solution.py:26
  14.8 1.3 %collective-permute-start.5 = (bf16[304,128]{1,0:T(8,128)(2,1)S(1)}, bf16[304,128]{1,0:T(8,128)(2,1)S(1)}, u32[]{:S(2)}, u32[]{:S(2)}) collective-permute-start(bf16[304,128]{1,0:T(8,128)(2,1)S(1)} %get-tuple-element.37), channel_id=1, source_target_pairs={{0,1},{1,0},{2,3},{3,2},{4,5},{5,4},{6,7},{7,6},{8,9},{9,8},{10,11... | collective-permute-start | bytes 233480 | tf_op jit(solution)/shard_map/ppermute | solution.py:26
  16.1 7.2 %collective-permute-start.8 = (bf16[304,128]{1,0:T(8,128)(2,1)S(1)}, bf16[304,128]{1,0:T(8,128)(2,1)S(1)}, u32[]{:S(2)}, u32[]{:S(2)}) collective-permute-start(bf16[304,128]{1,0:T(8,128)(2,1)S(1)} %shard_map.73.refs_0_), channel_id=1, source_target_pairs={{0,12},{1,13},{2,14},{3,15},{4,8},{5,9},{6,10},{7,11},{8,4},{9,5},... | collective-permute-start | bytes 233480 | tf_op jit(solution)/shard_map/ppermute | solution.py:26
  19.1 6.9 %collective-permute-start.7 = (bf16[304,128]{1,0:T(8,128)(2,1)S(1)}, bf16[304,128]{1,0:T(8,128)(2,1)S(1)}, u32[]{:S(2)}, u32[]{:S(2)}) collective-permute-start(bf16[304,128]{1,0:T(8,128)(2,1)S(1)} %shard_map.73.refs_0_), channel_id=1, source_target_pairs={{0,8},{1,9},{2,10},{3,11},{4,12},{5,13},{6,14},{7,15},{8,0},{9,1},... | collective-permute-start | bytes 233480 | tf_op jit(solution)/shard_map/ppermute | solution.py:26
  19.1 6.9 %collective-permute-start.6 = (bf16[304,128]{1,0:T(8,128)(2,1)S(1)}, bf16[304,128]{1,0:T(8,128)(2,1)S(1)}, u32[]{:S(2)}, u32[]{:S(2)}) collective-permute-start(bf16[304,128]{1,0:T(8,128)(2,1)S(1)} %shard_map.73.refs_0_), channel_id=1, source_target_pairs={{0,4},{1,5},{2,6},{3,7},{4,0},{5,1},{6,2},{7,3},{8,12},{9,13},{10,... | collective-permute-start | bytes 233480 | tf_op jit(solution)/shard_map/ppermute | solution.py:26

commit v8 on v7

--- a/solution.py
+++ b/solution.py
@@ -11,7 +11,7 @@
 F32 = jnp.float32
 BF16 = jnp.bfloat16
 AXES = ("depth", "rows")
-STATS = 6
+STATS = 5
 VMEM = pl.BlockSpec(memory_space=pltpu.VMEM)
 
 
@@ -85,7 +85,7 @@
 
 
 def stat_pieces(peak, total, depth):
-    return pieces(peak * 0.5, 3) + pieces(total, 2) + [depth]
+    return pieces(peak * 0.5, 3) + [total, depth]
 
 
 def store_parcel(ref, feats, peak, total, depth):
@@ -99,7 +99,7 @@
 def load_stats(ref, rows):
     flat = ref[ref.shape[0] - STATS * rows :].astype(F32)
     flat = [flat[k * rows : (k + 1) * rows] for k in range(STATS)]
-    return ((flat[0] + flat[1]) + flat[2]) * 2.0, flat[3] + flat[4], flat[5]
+    return ((flat[0] + flat[1]) + flat[2]) * 2.0, flat[3], flat[4]
 
 
 def first_layer(w, x, half, chans, ends, store):
@@ -331,9 +331,16 @@
     store_parcel(out_ref, *merge(mine, parcel(got_ref, rows), rows))
 
 
+def partner(core, k, count):
+    return (((2, 3, 1), (2, 1, 3))[core][k - 1]) if count == 4 else k
+
+
 def merge_group(step, refs, rows, finish):
-    def go(me):
-        parts = [parcel(refs[me ^ j], rows) for j in range(len(refs))]
+    def go(me, core):
+        at = [0] * len(refs)
+        for k in range(1, len(refs)):
+            at[partner(core, k, len(refs))] = k
+        parts = [parcel(refs[at[me ^ j]], rows) for j in range(len(refs))]
         while True:
             merged = [merge(a, b, rows) for a, b in zip(parts[::2], parts[1::2])]
             if len(merged) == 1:
@@ -341,8 +348,10 @@
             parts = [(m[0].__getitem__, m[1:]) for m in merged]
 
     place = (lax.axis_index("depth") // step) & (len(refs) - 1)
+    core = lax.axis_index("rows") & 1
     for me in range(len(refs)):
-        pl.when(place == me)(functools.partial(go, me))
+        for c in range(2):
+            pl.when(jnp.logical_and(place == me, core == c))(functools.partial(go, me, c))
 
 
 def merge_kernel(step, rows, *refs):
@@ -483,7 +492,10 @@
     (sums,) = call(first_merge_kernel, [(parcel_shape, BF16)], keep, stat, got)
     rounds = merge_rounds(depth)
     for step, count in rounds:
-        others = [move(sums, lambda d, r: (d ^ (k * step), r)) for k in range(1, count)]
+        others = [
+            move(sums, lambda d, r: (d ^ (partner(r & 1, k, count) * step), r))
+            for k in range(1, count)
+        ]
         if (step, count) != rounds[-1]:
             (sums,) = call(
                 functools.partial(merge_kernel, step, rows), [(parcel_shape, BF16)], sums, *others

time: 26.9 us -> 27.6 us (1.026)
  waiting for transfers between devices: 9.08 us -> 10.6 us
  starting transfers between devices: 10 us -> 9.13 us
    ppermute x9, waiting for transfers between devices: 9.08 us -> 10.6 us  [exchange(): return lax.ppermute(value, AXES, pairs)]
    ppermute x9, starting transfers between devices: 10 us -> 9.13 us  [exchange(): return lax.ppermute(value, AXES, pairs)]
  transfers between devices with their start and end apart: 9 -> 9, of which waited for: 5 -> 6; matrix products, arithmetic and copies ran while one was open for 0% -> 0% of each run, Pallas kernels for 9% -> 9%
where the time goes in v8:
time: 27.6 us; the launch traced here: 27.4 us
  waiting for transfers between devices  10.6 us (38%)
  starting transfers between devices  9.13 us (33%)
  Pallas kernels  4.05 us (15%)
  local copies, waits for them, and re-layouts  2.8 us (10%)
  between operations  0.73 us (3%)
    ppermute x9, waiting for transfers between devices, exchange(): return lax.ppermute(value, AXES, pairs)  10.6 us
    ppermute x9, starting transfers between devices, exchange(): return lax.ppermute(value, AXES, pairs)  9.13 us
    pallas_call x7, Pallas kernels, call(): pl.pallas_call(kernel, out_shape=[jax.ShapeDtypeStruct(s, t) for s, t in...  4.05 us
    unnamed x12, local copies, waits for them, and re-layouts  2.8 us
  transfers between devices with their start and end apart: 9, of which 6 were waited for; matrix products, arithmetic and copies ran while one was open for 0% of the time, Pallas kernels for 9%

profile of v8, /device:TPU:0, one launch (start us, length us, event | category | flops | bytes accessed | tf_op | source)
XLA Modules:
  0.0 27.4 jit_solution(11947156656729283547)
XLA Ops:
  0.6 0.6 %collective-permute-start = (bf16[4,8,32,128]{3,2,1,0:T(8,128)(2,1)}, bf16[4,8,32,128]{3,2,1,0:T(8,128)(2,1)S(1)}, u32[]{:S(2)}, u32[]{:S(2)}) collective-permute-start(bf16[4,8,32,128]{3,2,1,0:T(8,128)(2,1)} %own_ref.1), channel_id=1, source_target_pairs={{0,1},{1,0},{2,3},{3,2},{4,5},{5,4},{6,7},{7,6},{8,9},{9,8},{10,11... | collective-permute-start | bytes 786440 | tf_op jit(solution)/shard_map/ppermute | solution.py:26
  1.2 0.1 collective-permute-start.1
  1.3 0.0 copy-start
  1.3 0.9 %copy-done = bf16[4,8,32,128]{3,2,1,0:T(8,128)(2,1)S(1)} copy-done((bf16[4,8,32,128]{3,2,1,0:T(8,128)(2,1)S(1)}, bf16[4,8,32,128]{3,2,1,0:T(8,128)(2,1)}, u32[]{:S(2)}) %copy-start) | copy-done | bytes 262168
  2.2 0.0 copy-start.2
  2.3 0.0 copy-start.4
  2.3 0.9 %copy-done.2 = bf16[3,3,3,32,32]{4,3,2,1,0:T(8,128)(2,1)S(1)} copy-done((bf16[3,3,3,32,32]{4,3,2,1,0:T(8,128)(2,1)S(1)}, bf16[3,3,3,32,32]{4,3,2,1,0:T(8,128)(2,1)}, u32[]{:S(2)}) %copy-start.2) | copy-done | bytes 55320
  3.2 0.0 copy-done.4
  3.2 0.0 copy-start.3
  3.2 0.9 %copy-done.3 = bf16[3,3,3,32,32]{4,3,2,1,0:T(8,128)(2,1)S(1)} copy-done((bf16[3,3,3,32,32]{4,3,2,1,0:T(8,128)(2,1)S(1)}, bf16[3,3,3,32,32]{4,3,2,1,0:T(8,128)(2,1)}, u32[]{:S(2)}) %copy-start.3) | copy-done | bytes 55320
  4.1 0.4 %shard_map.69 = (bf16[192,384]{1,0:T(8,128)(2,1)S(1)}, bf16[192,384]{1,0:T(8,128)(2,1)S(1)}, f32[32,128]{1,0:T(8,128)S(1)}) custom-call(bf16[3,3,3,32,32]{4,3,2,1,0:T(8,128)(2,1)S(1)} %copy-done.2, bf16[3,3,3,32,32]{4,3,2,1,0:T(8,128)(2,1)S(1)} %copy-done.3, f32[1,32]{1,0:T(1,128)S(1)} %bitcast.1), custom_call_target="tpu_custom_call" | custom-call | flops 100000000 | bytes 1000000 | tf_op jit(solution)/shard_map/pallas_call | solution.py:385
  4.5 0.0 collective-permute-done.1.sp_ref
  4.5 0.0 collective-permute-done.sib_ref
  4.5 0.0 copy-start.1
  4.6 3.0 %collective-permute-start.4 = (bf16[2,16,32,128]{3,2,1,0:T(8,128)(2,1)S(1)}, bf16[2,16,32,128]{3,2,1,0:T(8,128)(2,1)S(1)}, u32[]{:S(2)}, u32[]{:S(2)}) collective-permute-start(bf16[2,16,32,128]{3,2,1,0:T(8,128)(2,1)S(1)} %maximum_select_fusion), channel_id=1, source_target_pairs={{0,2},{1,4},{2,0},{3,6},{4,1},{5,8},{6,3},{7,10},{8,5},{9,12},{10,... | collective-permute-start | bytes 786440 | tf_op jit(solution)/shard_map/ppermute | solution.py:26
  7.6 0.0 copy-start.5
  7.6 1.4 %collective-permute-start.2 = (bf16[4,2,32,128]{3,2,1,0:T(8,128)(2,1)S(1)}, bf16[4,2,32,128]{3,2,1,0:T(8,128)(2,1)S(1)}, u32[]{:S(2)}, u32[]{:S(2)}) collective-permute-start(bf16[4,2,32,128]{3,2,1,0:T(8,128)(2,1)S(1)} %select_select_fusion), channel_id=1, source_target_pairs={{0,3},{1,2},{2,1},{3,0},{4,7},{5,6},{6,5},{7,4},{8,11},{9,10},{10,... | collective-permute-start | bytes 196616 | tf_op jit(solution)/shard_map/ppermute | solution.py:26
  8.9 0.5 %collective-permute-start.3 = (bf16[2,2,32,128]{3,2,1,0:T(8,128)(2,1)S(1)}, bf16[2,2,32,128]{3,2,1,0:T(8,128)(2,1)S(1)}, u32[]{:S(2)}, u32[]{:S(2)}) collective-permute-start(bf16[2,2,32,128]{3,2,1,0:T(8,128)(2,1)S(1)} %slice_select_fusion.1), channel_id=1, source_target_pairs={{0,2},{1,6},{2,0},{3,4},{4,3},{5,10},{6,1},{7,8},{8,7},{9,14},{10,... | collective-permute-start | bytes 98312 | tf_op jit(solution)/shard_map/ppermute | solution.py:26
  9.5 0.0 copy-done.1
  9.5 0.0 copy-done.5
  9.5 0.8 %shard_map.70 = (bf16[4,10,32,256]{3,2,1,0:T(8,128)(2,1)S(1)}, bf16[2,9,32,256]{3,2,1,0:T(8,128)(2,1)S(1)}, f32[2,2,8,128]{3,2,1,0:T(8,128)S(1)}) custom-call(bf16[4,8,32,128]{3,2,1,0:T(8,128)(2,1)S(1)} %copy-done.1, bf16[4,8,32,128]{3,2,1,0:T(8,128)(2,1)S(1)} %collective-permute-done.sib_ref, f32[4,8,128]{2,1,0:T(8,128)S(1)} %copy-done.5, ...), custom_call_target="tpu_custom_call" | custom-call | flops 200000000 | bytes 1000000 | tf_op jit(solution)/shard_map/pallas_call | solution.py:385
  10.3 2.3 %collective-permute-done.4.zh_ref = bf16[2,16,32,128]{3,2,1,0:T(8,128)(2,1)S(1)} collective-permute-done((bf16[2,16,32,128]{3,2,1,0:T(8,128)(2,1)S(1)}, bf16[2,16,32,128]{3,2,1,0:T(8,128)(2,1)S(1)}, u32[]{:S(2)}, u32[]{:S(2)}) %collective-permute-start.4) | collective-permute-done | bytes 262176 | tf_op jit(solution)/shard_map/ppermute | solution.py:26
  12.6 1.3 %shard_map.71 = (bf16[2,10,32,256]{3,2,1,0:T(8,128)(2,1)S(1)}, bf16[2,9,32,256]{3,2,1,0:T(8,128)(2,1)S(1)}, f32[2,8,32,128]{3,2,1,0:T(8,128)S(1)}, f32[2,3,8,128]{3,2,1,0:T(8,128)S(1)}) custom-call(bf16[2,16,32,128]{3,2,1,0:T(8,128)(2,1)S(1)} %collective-permute-done.4.zh_ref, bf16[4,10,32,256]{3,2,1,0:T(8,128)(2,1)S(1)} %get-tuple-element.25.xo_ref, ...), custom_call_target="tpu_custom_call" | custom-call | flops 500000000 | bytes 1000000 | tf_op jit(solution)/shard_map/pallas_call | solution.py:385
  13.9 0.1 collective-permute-done.3.corner_ref
  14.0 0.0 collective-permute-done.2.side_ref
  14.0 0.8 %shard_map.72 = (f32[8,32,128]{2,1,0:T(8,128)S(1)}, f32[3,8,128]{2,1,0:T(8,128)S(1)}, bf16[296,128]{1,0:T(8,128)(2,1)S(1)}) custom-call(bf16[4,2,32,128]{3,2,1,0:T(8,128)(2,1)S(1)} %collective-permute-done.2.side_ref, bf16[2,2,32,128]{3,2,1,0:T(8,128)(2,1)S(1)} %collective-permute-done.3.corner_ref, bf16[4,10,32,256]{3,2,1,0:T(8,128)(2,1)S(1)} %get-tuple-element.25.xo_ref, ...), custom_call_target="tpu_custom_call" | custom-call | flops 100000000 | bytes 1000000 | tf_op jit(solution)/shard_map/pallas_call | solution.py:385
  14.8 0.1 collective-permute-start.5
  14.8 1.3 %collective-permute-done.5.got_ref = bf16[296,128]{1,0:T(8,128)(2,1)S(1)} collective-permute-done((bf16[296,128]{1,0:T(8,128)(2,1)S(1)}, bf16[296,128]{1,0:T(8,128)(2,1)S(1)}, u32[]{:S(2)}, u32[]{:S(2)}) %collective-permute-start.5) | collective-permute-done | bytes 75808 | tf_op jit(solution)/shard_map/ppermute | solution.py:26
  16.1 1.0 %collective-permute-start.8 = (bf16[296,128]{1,0:T(8,128)(2,1)S(1)}, bf16[296,128]{1,0:T(8,128)(2,1)S(1)}, u32[]{:S(2)}, u32[]{:S(2)}) collective-permute-start(bf16[296,128]{1,0:T(8,128)(2,1)S(1)} %shard_map.73.refs_0_), channel_id=1, source_target_pairs={{0,4},{1,13},{2,6},{3,15},{4,0},{5,9},{6,2},{7,11},{8,12},{9,5},{1... | collective-permute-start | bytes 227336 | tf_op jit(solution)/shard_map/ppermute | solution.py:26
  17.1 2.5 %collective-permute-start.7 = (bf16[296,128]{1,0:T(8,128)(2,1)S(1)}, bf16[296,128]{1,0:T(8,128)(2,1)S(1)}, u32[]{:S(2)}, u32[]{:S(2)}) collective-permute-start(bf16[296,128]{1,0:T(8,128)(2,1)S(1)} %shard_map.73.refs_0_), channel_id=1, source_target_pairs={{0,12},{1,5},{2,14},{3,7},{4,8},{5,1},{6,10},{7,3},{8,4},{9,13},{1... | collective-permute-start | bytes 227336 | tf_op jit(solution)/shard_map/ppermute | solution.py:26
  19.6 0.1 collective-permute-start.6
  19.7 0.9 %collective-permute-done.8.refs_3_ = bf16[296,128]{1,0:T(8,128)(2,1)S(1)} collective-permute-done((bf16[296,128]{1,0:T(8,128)(2,1)S(1)}, bf16[296,128]{1,0:T(8,128)(2,1)S(1)}, u32[]{:S(2)}, u32[]{:S(2)}) %collective-permute-start.8) | collective-permute-done | bytes 75808 | tf_op jit(solution)/shard_map/ppermute | solution.py:26
  20.6 3.8 %collective-permute-done.7.refs_2_ = bf16[296,128]{1,0:T(8,128)(2,1)S(1)} collective-permute-done((bf16[296,128]{1,0:T(8,128)(2,1)S(1)}, bf16[296,128]{1,0:T(8,128)(2,1)S(1)}, u32[]{:S(2)}, u32[]{:S(2)}) %collective-permute-start.7) | collective-permute-done | bytes 75808 | tf_op jit(solution)/shard_map/ppermute | solution.py:26
  24.4 2.2 %collective-permute-done.6.refs_1_ = bf16[296,128]{1,0:T(8,128)(2,1)S(1)} collective-permute-done((bf16[296,128]{1,0:T(8,128)(2,1)S(1)}, bf16[296,128]{1,0:T(8,128)(2,1)S(1)}, u32[]{:S(2)}, u32[]{:S(2)}) %collective-permute-start.6) | collective-permute-done | bytes 75808 | tf_op jit(solution)/shard_map/ppermute | solution.py:26
  26.6 0.8 %shard_map.74 = (f32[8,32,128]{2,1,0:T(8,128)}, f32[8,128]{1,0:T(8,128)}) custom-call(bf16[296,128]{1,0:T(8,128)(2,1)S(1)} %shard_map.73.refs_0_, bf16[296,128]{1,0:T(8,128)(2,1)S(1)} %collective-permute-done.6.refs_1_, bf16[296,128]{1,0:T(8,128)(2,1)S(1)} %collective-permute-done.7.refs_2_, bf16[296,128]{1,0:T(8,128)(2,1)S(1)} %collective-permute-done.8.refs_3_), custom_call_target="tpu_custom_call" | custom-call | tf_op jit(solution)/shard_map/pallas_call | solution.py:385
  (6 shorter events, 0.1 us)
Async XLA Ops:
  0.6 3.9 %collective-permute-start = (bf16[4,8,32,128]{3,2,1,0:T(8,128)(2,1)}, bf16[4,8,32,128]{3,2,1,0:T(8,128)(2,1)S(1)}, u32[]{:S(2)}, u32[]{:S(2)}) collective-permute-start(bf16[4,8,32,128]{3,2,1,0:T(8,128)(2,1)} %own_ref.1), channel_id=1, source_target_pairs={{0,1},{1,0},{2,3},{3,2},{4,5},{5,4},{6,7},{7,6},{8,9},{9,8},{10,11... | collective-permute-start | bytes 786440 | tf_op jit(solution)/shard_map/ppermute | solution.py:26
  1.2 3.3 %collective-permute-start.1 = (f32[4,8,128]{2,1,0:T(8,128)}, f32[4,8,128]{2,1,0:T(8,128)S(1)}, u32[]{:S(2)}, u32[]{:S(2)}) collective-permute-start(f32[4,8,128]{2,1,0:T(8,128)} %op_ref.1), channel_id=1, source_target_pairs={{0,1},{1,0},{2,3},{3,2},{4,5},{5,4},{6,7},{7,6},{8,9},{9,8},{10,11... | collective-permute-start | bytes 49160 | tf_op jit(solution)/shard_map/ppermute | solution.py:26
  1.3 0.9 %copy-start = (bf16[4,8,32,128]{3,2,1,0:T(8,128)(2,1)S(1)}, bf16[4,8,32,128]{3,2,1,0:T(8,128)(2,1)}, u32[]{:S(2)}) copy-start(bf16[4,8,32,128]{3,2,1,0:T(8,128)(2,1)} %own_ref.1) | copy-start | bytes 786436
  2.2 0.9 %copy-start.2 = (bf16[3,3,3,32,32]{4,3,2,1,0:T(8,128)(2,1)S(1)}, bf16[3,3,3,32,32]{4,3,2,1,0:T(8,128)(2,1)}, u32[]{:S(2)}) copy-start(bf16[3,3,3,32,32]{4,3,2,1,0:T(8,128)(2,1)} %k1_ref.1) | copy-start | bytes 165892
  2.3 0.9 %copy-start.4 = (f32[32]{0:T(128)S(1)}, f32[32]{0:T(128)}, u32[]{:S(2)}) copy-start(f32[32]{0:T(128)} %param.9) | copy-start | bytes 388
  3.2 0.9 %copy-start.3 = (bf16[3,3,3,32,32]{4,3,2,1,0:T(8,128)(2,1)S(1)}, bf16[3,3,3,32,32]{4,3,2,1,0:T(8,128)(2,1)}, u32[]{:S(2)}) copy-start(bf16[3,3,3,32,32]{4,3,2,1,0:T(8,128)(2,1)} %k2_ref.1) | copy-start | bytes 165892
  4.5 4.9 %copy-start.1 = (bf16[4,8,32,128]{3,2,1,0:T(8,128)(2,1)S(1)}, bf16[4,8,32,128]{3,2,1,0:T(8,128)(2,1)}, u32[]{:S(2)}) copy-start(bf16[4,8,32,128]{3,2,1,0:T(8,128)(2,1)} %own_ref.1) | copy-start | bytes 786436
  4.6 8.0 %collective-permute-start.4 = (bf16[2,16,32,128]{3,2,1,0:T(8,128)(2,1)S(1)}, bf16[2,16,32,128]{3,2,1,0:T(8,128)(2,1)S(1)}, u32[]{:S(2)}, u32[]{:S(2)}) collective-permute-start(bf16[2,16,32,128]{3,2,1,0:T(8,128)(2,1)S(1)} %maximum_select_fusion), channel_id=1, source_target_pairs={{0,2},{1,4},{2,0},{3,6},{4,1},{5,8},{6,3},{7,10},{8,5},{9,12},{10,... | collective-permute-start | bytes 786440 | tf_op jit(solution)/shard_map/ppermute | solution.py:26
  7.6 1.9 %copy-start.5 = (f32[4,8,128]{2,1,0:T(8,128)S(1)}, f32[4,8,128]{2,1,0:T(8,128)}, u32[]{:S(2)}) copy-start(f32[4,8,128]{2,1,0:T(8,128)} %op_ref.1) | copy-start | bytes 49156
  7.6 6.4 %collective-permute-start.2 = (bf16[4,2,32,128]{3,2,1,0:T(8,128)(2,1)S(1)}, bf16[4,2,32,128]{3,2,1,0:T(8,128)(2,1)S(1)}, u32[]{:S(2)}, u32[]{:S(2)}) collective-permute-start(bf16[4,2,32,128]{3,2,1,0:T(8,128)(2,1)S(1)} %select_select_fusion), channel_id=1, source_target_pairs={{0,3},{1,2},{2,1},{3,0},{4,7},{5,6},{6,5},{7,4},{8,11},{9,10},{10,... | collective-permute-start | bytes 196616 | tf_op jit(solution)/shard_map/ppermute | solution.py:26
  8.9 5.1 %collective-permute-start.3 = (bf16[2,2,32,128]{3,2,1,0:T(8,128)(2,1)S(1)}, bf16[2,2,32,128]{3,2,1,0:T(8,128)(2,1)S(1)}, u32[]{:S(2)}, u32[]{:S(2)}) collective-permute-start(bf16[2,2,32,128]{3,2,1,0:T(8,128)(2,1)S(1)} %slice_select_fusion.1), channel_id=1, source_target_pairs={{0,2},{1,6},{2,0},{3,4},{4,3},{5,10},{6,1},{7,8},{8,7},{9,14},{10,... | collective-permute-start | bytes 98312 | tf_op jit(solution)/shard_map/ppermute | solution.py:26
  14.8 1.3 %collective-permute-start.5 = (bf16[296,128]{1,0:T(8,128)(2,1)S(1)}, bf16[296,128]{1,0:T(8,128)(2,1)S(1)}, u32[]{:S(2)}, u32[]{:S(2)}) collective-permute-start(bf16[296,128]{1,0:T(8,128)(2,1)S(1)} %get-tuple-element.37), channel_id=1, source_target_pairs={{0,1},{1,0},{2,3},{3,2},{4,5},{5,4},{6,7},{7,6},{8,9},{9,8},{10,11... | collective-permute-start | bytes 227336 | tf_op jit(solution)/shard_map/ppermute | solution.py:26
  16.1 4.4 %collective-permute-start.8 = (bf16[296,128]{1,0:T(8,128)(2,1)S(1)}, bf16[296,128]{1,0:T(8,128)(2,1)S(1)}, u32[]{:S(2)}, u32[]{:S(2)}) collective-permute-start(bf16[296,128]{1,0:T(8,128)(2,1)S(1)} %shard_map.73.refs_0_), channel_id=1, source_target_pairs={{0,4},{1,13},{2,6},{3,15},{4,0},{5,9},{6,2},{7,11},{8,12},{9,5},{1... | collective-permute-start | bytes 227336 | tf_op jit(solution)/shard_map/ppermute | solution.py:26
  17.1 7.3 %collective-permute-start.7 = (bf16[296,128]{1,0:T(8,128)(2,1)S(1)}, bf16[296,128]{1,0:T(8,128)(2,1)S(1)}, u32[]{:S(2)}, u32[]{:S(2)}) collective-permute-start(bf16[296,128]{1,0:T(8,128)(2,1)S(1)} %shard_map.73.refs_0_), channel_id=1, source_target_pairs={{0,12},{1,5},{2,14},{3,7},{4,8},{5,1},{6,10},{7,3},{8,4},{9,13},{1... | collective-permute-start | bytes 227336 | tf_op jit(solution)/shard_map/ppermute | solution.py:26
  19.6 7.0 %collective-permute-start.6 = (bf16[296,128]{1,0:T(8,128)(2,1)S(1)}, bf16[296,128]{1,0:T(8,128)(2,1)S(1)}, u32[]{:S(2)}, u32[]{:S(2)}) collective-permute-start(bf16[296,128]{1,0:T(8,128)(2,1)S(1)} %shard_map.73.refs_0_), channel_id=1, source_target_pairs={{0,8},{1,9},{2,10},{3,11},{4,12},{5,13},{6,14},{7,15},{8,0},{9,1},... | collective-permute-start | bytes 227336 | tf_op jit(solution)/shard_map/ppermute | solution.py:26
